TPU v7x, 32 devices: a whole 2x2x4 slice. The times are simulated.
32 devices in a mesh: row: 8 (over y, x, core), col: 4 (over z).
Axes of the slice: x: 2, y: 2, z: 4, core: 2. Of those that a mesh axis runs over, the one named last changes fastest.
Arguments:
- ingest: bfloat16 [2048, 8192], P(('row', 'col')), may hold values from -128 to 127, as said below
- row_order: int32 [8, 256], P('row'), may hold values from 0 to 255, each once within a row
- matrix_seeds: int32 [2], replicated, may hold values from 0 to 46336
Outputs:
- second_hint: float32 [4, 2, 1024, 1024], P(None, None, 'col')
Inputs may be any that keep to these rules, and one draw needn't show every extreme that they name: `ingest`: integers. `row_order`: each row is a permutation of 0 to 255.
All inputs are finite; a program needn't handle non-finite values.
Results may differ from a plain program's by a relative error of at most 0.0003.
Values may be sent and summed in bfloat16 or wider, within the bound.
No kernel may reach another device: no remote copies, remote signals or barrier semaphores. Data moves between devices by JAX's collectives and lax.ppermute only.
A program may use at most 64 MiB of HBM per device.

v0:
```python
import functools

import jax
import jax.numpy as jnp
import numpy as np
from jax import lax
from jax.experimental import pallas as pl
from jax.experimental.pallas import tpu as pltpu
from jax.sharding import PartitionSpec as P

N = 1024

PRIME = 46337
HALF_PRIME = PRIME // 2
WHOLE = (1 << 32) // PRIME
PART = (1 << 32) / PRIME - WHOLE
SCALE = np.float32(PRIME / 2.0**32)
FINE = np.float32(1.5 * 2.0**23)
OFFSET = 32896 - HALF_PRIME
COARSE = np.float32(1.5 * 2.0**31 - 1.5 * 2.0**23 - OFFSET)
FINE_OFFSET = np.float32(1.5 * 2.0**23 + OFFSET)
SUBLANES = 16
LANES = 128
NT = (((1,), (1,)), ((), ()))


def centred(value):
    return value - jnp.where(value > HALF_PRIME, PRIME, 0)


def fixed(value):
    value = centred(value)
    return value * WHOLE + jnp.round(value.astype(jnp.float32) * np.float32(PART)).astype(jnp.int32)


def first_vectors(index, seed, step):
    factor = 2 * (29989 * step % PRIME) % PRIME
    vectors = []
    for extra in (0, 7919):
        inner = (index % PRIME * 40503 % PRIME + (seed + extra)) % PRIME
        a = inner * inner % PRIME
        vectors += [
            centred(a),
            fixed((a * a % PRIME + (12345 - HALF_PRIME + PRIME)) % PRIME),
            fixed(a * factor % PRIME),
        ]
    return vectors


def second_vectors(index, step):
    shift = 29989 * step % PRIME
    b = index % PRIME * 29989 % PRIME
    slope = b * (2 * shift % PRIME) % PRIME + shift * shift % PRIME
    return [fixed(2 * b % PRIME), fixed(b * b % PRIME), fixed(slope % PRIME)]


def bend(step):
    value = 2 * (29989 * step % PRIME) ** 2 % PRIME
    value = value - PRIME if value > HALF_PRIME else value
    return np.int32(round(value * 2**32 / PRIME))


def limb_pair(value):
    rounded = value.astype(jnp.float32) * SCALE + FINE
    kept = (rounded + COARSE) - COARSE
    return (rounded - kept).astype(jnp.bfloat16), (kept - FINE_OFFSET).astype(jnp.bfloat16)


def join(products):
    low_p, high_p, low_q, high_q = products
    small = np.float32(1 / 256)
    p = low_p.astype(jnp.int32) + ((high_p * small).astype(jnp.int32) << 8)
    q = low_q.astype(jnp.int32) + ((high_q * small).astype(jnp.int32) << 8)
    return p + (q << 16)


def first_kernel(width, lane, own_ref, peer_ref, first_ref, second_ref, out_ref, even, odd):
    parts, half, _ = out_ref.shape
    total = own_ref.shape[1] // width * parts

    def make(step, limbs):
        chunk, part = step // parts, step % parts
        by_n = [jnp.concatenate([second_ref[i, part]] * (lane // LANES), axis=1) for i in range(3)]
        for t in range(width // lane):
            at = pl.ds(pl.multiple_of(chunk * width + t * lane, lane), lane)
            for mix in range(2):
                a, square, slope = (first_ref[3 * mix + i : 3 * mix + i + 1, at] for i in range(3))
                value = a * by_n[0] + square + by_n[1]
                slope = slope + by_n[2]
                for k in range(half // SUBLANES):
                    low, high = limb_pair(value)
                    top = 2 * mix * half + k * SUBLANES
                    limbs[top : top + SUBLANES, t * lane : (t + 1) * lane] = low
                    limbs[top + half : top + half + SUBLANES, t * lane : (t + 1) * lane] = high
                    value = value + slope
                    slope = slope + bend(SUBLANES)

    def use(step, limbs):
        chunk, part = step // parts, step % parts
        at = pl.ds(pl.multiple_of(chunk * width, width), width)
        records = jnp.concatenate([own_ref[:, at], peer_ref[:, at]], axis=0)
        product = lax.dot_general(limbs[...], records, NT, preferred_element_type=jnp.float32)
        out_ref[part] += join([product[i * half : (i + 1) * half] for i in range(4)])

    out_ref[...] = jnp.zeros_like(out_ref)
    make(0, even)

    @pl.loop(0, total // 2 - 1)
    def _(i):
        use(2 * i, even)
        make(2 * i + 1, odd)
        use(2 * i + 1, odd)
        make(2 * i + 2, even)

    use(total - 2, even)
    make(total - 1, odd)
    use(total - 1, odd)


def first_hint(own, peer, by_first, by_second, parts, half):
    rows, depth = own.shape
    width = min(1024, depth)
    lane = min(512, width)
    return pl.pallas_call(
        functools.partial(first_kernel, width, lane),
        out_shape=jax.ShapeDtypeStruct((parts, half, 2 * rows), jnp.int32),
        in_specs=[pl.BlockSpec(memory_space=pltpu.VMEM)] * 4,
        out_specs=pl.BlockSpec(memory_space=pltpu.VMEM),
        scratch_shapes=[pltpu.VMEM((4 * half, width), jnp.bfloat16)] * 2,
        name="first_hint",
    )(own, peer, by_first, by_second)


def matrix_kernel(columns, group, first_ref, second_ref, *refs):
    out_ref = refs[-1]

    @pl.loop(0, out_ref.shape[1] // group)
    def _(i):
        at = pl.ds(pl.multiple_of(i * group, group), group)
        by_row = first_ref[at, :]
        for mix in range(2):
            a, square, slope = (by_row[:, 3 * mix + i : 3 * mix + i + 1] for i in range(3))
            value = a * second_ref[0:1] + square + second_ref[1:2]
            slope = slope + second_ref[2:3]
            for k in range(columns // LANES):
                low, high = limb_pair(value)
                out_ref[2 * mix, at, k * LANES : (k + 1) * LANES] = low
                out_ref[2 * mix + 1, at, k * LANES : (k + 1) * LANES] = high
                value = value + slope
                slope = slope + bend(LANES)


def second_matrix(by_first, by_second, columns, after=None):
    rows = by_first.shape[0]
    block = min(256, rows)
    return pl.pallas_call(
        functools.partial(matrix_kernel, columns, min(32, block)),
        grid=(rows // block,),
        out_shape=jax.ShapeDtypeStruct((4, rows, columns), jnp.bfloat16),
        in_specs=[
            pl.BlockSpec((block, by_first.shape[1]), lambda i: (i, 0)),
            pl.BlockSpec(by_second.shape, lambda i: (0, 0)),
        ]
        + ([] if after is None else [pl.BlockSpec(memory_space=pl.ANY)]),
        out_specs=pl.BlockSpec((4, block, columns), lambda i: (0, i, 0)),
        name="second_matrix",
    )(by_first, by_second, *([] if after is None else [after]))


def second_kernel(hint_ref, matrix_ref, *refs):
    out_ref, digits = refs[-2:]
    pieces, half, rows = hint_ref.shape

    @pl.when(pl.program_id(0) == 0)
    def _():
        for s in range(pieces):
            hint = hint_ref[s]
            for place in range(4):
                byte = (lax.shift_right_logical(hint, jnp.int32(8 * place)) & 255) - 128
                digits[place * half : (place + 1) * half, s * rows : (s + 1) * rows] = byte.astype(
                    jnp.float32
                ).astype(jnp.bfloat16)

    total = join(
        [
            jnp.dot(digits[...], matrix_ref[i], preferred_element_type=jnp.float32)
            for i in range(4)
        ]
    )
    for place in range(4):
        term = total[place * half : (place + 1) * half]
        out_ref[place] = term if len(refs) == 2 else refs[0][place] + term


def second_hint(hint, matrix, total=None):
    pieces, half, rows = hint.shape
    _, depth, columns = matrix.shape
    block = min(256, columns)
    out_spec = pl.BlockSpec((4, half, block), lambda i: (0, 0, i))
    return pl.pallas_call(
        second_kernel,
        grid=(columns // block,),
        out_shape=jax.ShapeDtypeStruct((4, half, columns), jnp.int32),
        in_specs=[
            pl.BlockSpec(hint.shape, lambda i: (0, 0, 0)),
            pl.BlockSpec((4, depth, block), lambda i: (0, 0, i)),
        ]
        + ([] if total is None else [out_spec]),
        out_specs=out_spec,
        scratch_shapes=[pltpu.VMEM((4 * half, depth), jnp.bfloat16)],
        input_output_aliases={} if total is None else {2: 0},
        cost_estimate=pl.CostEstimate(
            flops=32 * half * depth * columns,
            bytes_accessed=8 * depth * columns + 32 * half * columns,
            transcendentals=0,
        ),
        name="second_hint",
    )(hint, matrix, *([] if total is None else [total]))


def halves_kernel(_, value_ref, *refs):
    out_ref = refs[-1]
    value = value_ref[...]
    scale = np.float32(1 / 65536)
    out_ref[:, 0] = (value & 65535).astype(jnp.float32) * scale
    out_ref[:, 1] = lax.shift_right_logical(value, jnp.int32(16)).astype(jnp.float32) * scale


def write_halves(value, place, out=None):
    digits, half, columns = value.shape
    return pl.pallas_call(
        halves_kernel,
        grid_spec=pltpu.PrefetchScalarGridSpec(
            num_scalar_prefetch=1,
            grid=(digits,),
            in_specs=[pl.BlockSpec((1, half, columns), lambda i, place: (i, 0, 0))]
            + ([] if out is None else [pl.BlockSpec(memory_space=pl.ANY)]),
            out_specs=pl.BlockSpec((1, 2, half, columns), lambda i, place: (i, 0, place[0], 0)),
        ),
        out_shape=jax.ShapeDtypeStruct((digits, 2, 2 * half, columns), jnp.float32),
        input_output_aliases={} if out is None else {2: 0},
        name="write_halves",
    )(place, value, *([] if out is None else [out]))


def shift_by(value, axis, offset):
    return lax.ppermute(value, axis, [(i, i ^ offset) for i in range(lax.axis_size(axis))])


def on_device(ingest, row_order, matrix_seeds):
    row_size, col_size = lax.axis_size("row"), lax.axis_size("col")
    row, col = lax.axis_index("row"), lax.axis_index("col")
    core = row % 2
    rows, depth = ingest.shape
    half = N // col_size // 2

    peer = shift_by(ingest, "row", 1)

    by_first = first_vectors(jnp.arange(depth, dtype=jnp.int32), matrix_seeds[0], SUBLANES)
    by_first = jnp.stack(by_first + by_first[:2])
    first_n = (2 * jnp.arange(col_size, dtype=jnp.int32)[:, None] + core) * half
    n_index = first_n + jnp.arange(SUBLANES, dtype=jnp.int32)[None, :]
    by_second = jnp.stack(second_vectors(n_index, SUBLANES))
    by_second = jnp.broadcast_to(by_second[..., None], by_second.shape + (LANES,))

    hint = first_hint(ingest, peer, by_first, by_second, col_size, half)

    order = row_order[0]
    block_rows = order.shape[0]
    k_index = lax.broadcasted_iota(jnp.int32, (block_rows, block_rows), 1)
    r_index = lax.broadcasted_iota(jnp.int32, (block_rows, block_rows), 0)
    place = jnp.sum(jnp.where(order[None, :] == r_index, k_index, 0), axis=1) + row * block_rows
    place = jnp.concatenate(
        [lax.dynamic_slice_in_dim(place, (col ^ s) * rows, rows) for s in range(col_size)]
    )[None]
    step = 1
    while step < row_size:
        place = jnp.concatenate([place, shift_by(place, "row", step)])
        step *= 2
    place = place.reshape(row_size // 2, 2, col_size, rows).transpose(0, 2, 1, 3)
    by_row = first_vectors(place.reshape(row_size // 2, -1), matrix_seeds[1], LANES)
    by_row = jnp.stack(by_row + by_row[:2], axis=2)
    by_column = second_vectors(jnp.arange(LANES, dtype=jnp.int32), LANES)
    by_column = jnp.stack(by_column + by_column[:1] * 5)

    mine = lax.dynamic_index_in_dim(hint, col, 0, keepdims=False)
    pieces = [mine]
    for s in range(1, col_size):
        piece = lax.dynamic_index_in_dim(hint, col ^ s, 0, keepdims=False)
        pieces.append(shift_by(piece, "col", s))
    pieces = jnp.stack(pieces)
    total = None
    for t in range(row_size // 2):
        matrix = second_matrix(by_row[t], by_column, N, total if t >= 4 else None)
        total = second_hint(shift_by(pieces, "row", 2 * t) if t else pieces, matrix, total)

    other = shift_by(total, "row", 1)
    out = write_halves(total, core[None])
    return write_halves(other, 1 - core[None], out)


def solution(mesh):
    in_specs = (P(("row", "col"), None), P("row", None), P())
    out_specs = P(None, None, "col", None)
    return jax.shard_map(
        on_device, mesh=mesh, in_specs=in_specs, out_specs=out_specs, check_vma=False
    )
```

profile of v0, /device:TPU:0, one launch (start us, length us, event | category | flops | bytes accessed | tf_op | source)
XLA Modules:
  0.0 128.2 jit_solution(4632893778734693905)
XLA Ops:
  0.0 0.8 select_reduce_fusion
  1.6 1.3 %fusion.37 = (s32[1]{0:T(128)}, s32[1]{0:T(128)}) fusion(s32[2]{0:T(128)} %param.5), kind=kLoop, calls=%fused_computation.124 | loop fusion | bytes 16 | tf_op jit(solution)/shard_map/slice | solution.py:281
  2.9 1.5 %fusion.10 = (s32[1,8192]{1,0:T(1,128)S(1)}, s32[1,8192]{1,0:T(1,128)S(1)}) fusion(s32[]{:T(128)} %bitcast.1), kind=kLoop, calls=%fused_computation.61 | loop fusion | flops 327680 | bytes 65540 | tf_op jit(solution)/shard_map/sub | solution.py:28
  5.0 2.3 %convert_add_fusion.5 = (s32[1,8192]{1,0:T(1,128)S(1)}, s32[1,8192]{1,0:T(1,128)S(1)}) fusion(s32[]{:T(128)S(6)} %add.969, s32[]{:T(128)} %bitcast.1), kind=kLoop, calls=%fused_computation.76 | loop fusion | flops 663552 | bytes 65544 | tf_op jit(solution)/shard_map/add | solution.py:33
  8.4 3.0 %collective-permute-start.6 = (s32[2,256]{1,0:T(2,128)S(1)}, s32[2,256]{1,0:T(2,128)S(1)}, u32[]{:S(2)}, u32[]{:S(2)}) collective-permute-start(s32[2,256]{1,0:T(2,128)S(1)} %pad_add_fusion.3), channel_id=1, source_target_pairs={{0,8},{4,12},{8,0},{12,4},{16,24},{20,28},{24,16},{28,20},{1,9},{5... | collective-permute-start | bytes 6152 | tf_op jit(solution)/shard_map/ppermute | solution.py:247
  11.4 1.5 %collective-permute-done.6 = s32[2,256]{1,0:T(2,128)S(1)} collective-permute-done((s32[2,256]{1,0:T(2,128)S(1)}, s32[2,256]{1,0:T(2,128)S(1)}, u32[]{:S(2)}, u32[]{:S(2)}) %collective-permute-start.6) | collective-permute-done | bytes 2080 | tf_op jit(solution)/shard_map/ppermute | solution.py:247
  12.9 2.1 %collective-permute-start.7 = (s32[4,256]{1,0:T(4,128)S(1)}, s32[4,256]{1,0:T(4,128)S(1)}, u32[]{:S(2)}, u32[]{:S(2)}) collective-permute-start(s32[4,256]{1,0:T(4,128)S(1)} %pad_add_fusion.2), channel_id=1, source_target_pairs={{0,16},{4,20},{8,24},{12,28},{16,0},{20,4},{24,8},{28,12},{1,17},{... | collective-permute-start | bytes 12296 | tf_op jit(solution)/shard_map/ppermute | solution.py:247
  16.3 1.1 stack.16.first_ref
  17.5 1.0 rem.658
  18.6 6.9 %convert_add_fusion = (s32[4,512,1]{2,1,0:T(8,128)}, s32[4,512,1]{2,1,0:T(8,128)}, s32[4,512,1]{2,1,0:T(8,128)}, s32[4,512,1]{2,1,0:T(8,128)}) fusion(s32[]{:T(128)S(6)} %add.1018, s32[4,512,1]{2,1,0:T(8,128)S(1)} %rem.658, s32[]{:T(128)} %bitcast.11), kind=kLoop, calls=%fused_computation.22 | loop fusion | flops 147456 | bytes 40968 | tf_op jit(solution)/shard_map/add | solution.py:33
  25.5 0.9 broadcast_in_dim.64.second_ref
  26.5 19.8 %first_hint.1 = s32[4,128,128]{2,1,0:T(8,128)} custom-call(bf16[64,8192]{1,0:T(8,128)(2,1)} %own_ref.1, bf16[64,8192]{1,0:T(8,128)(2,1)} %copy-done.1, s32[8,8192]{1,0:T(8,128)} %stack.16.first_ref, s32[3,4,16,128]{3,2,1,0:T(8,128)} %broadcast_in_dim.64.second_ref), custom_call_target="tpu_custom_call" | custom-call | tf_op jit(solution)/shard_map/first_hint/pallas_call | solution.py:124
  46.3 1.0 constant_dynamic-slice_fusion
  47.3 3.7 %collective-permute-start.3 = (s32[128,128]{1,0:T(8,128)S(1)}, s32[128,128]{1,0:T(8,128)S(1)}, u32[]{:S(2)}, u32[]{:S(2)}) collective-permute-start(s32[128,128]{1,0:T(8,128)S(1)} %get-tuple-element.20), channel_id=1, source_target_pairs={{0,3},{1,2},{2,1},{3,0},{4,7},{5,6},{6,5},{7,4},{8,11},{9,10},{10,... | collective-permute-start | bytes 196616 | tf_op jit(solution)/shard_map/ppermute | solution.py:247
  51.7 5.5 %convert_add_fusion.1 = (s32[4,512,1]{2,1,0:T(8,128)}, s32[4,512,1]{2,1,0:T(8,128)}, s32[4,512,1]{2,1,0:T(8,128)S(1)}, s32[4,512,1]{2,1,0:T(8,128)S(1)}) fusion(s32[4,512,1]{2,1,0:T(8,128)} %get-tuple-element.6, s32[4,512,1]{2,1,0:T(8,128)} %get-tuple-element.16), kind=kLoop, calls=%fused_computation.24 | loop fusion | flops 106496 | bytes 49152 | tf_op jit(solution)/shard_map/add | solution.py:33
  57.3 6.1 %stack.22 = s32[4,512,8]{2,1,0:T(8,128)S(1)} concatenate(s32[4,512,1]{2,1,0:T(8,128)S(1)} %get-tuple-element.40, s32[4,512,1]{2,1,0:T(8,128)S(1)} %get-tuple-element.41, s32[4,512,1]{2,1,0:T(8,128)} %get-tuple-element.15, s32[4,512,1]{2,1,0:T(8,128)} %get-tuple-element.14, s32[4,512,1]{2,1,0:T(8,128)} %get-tuple-element.13, s32[4,512,1]{2,1,0:T(8,128)} %get-tuple-element.5, ...), dimensions={2} | concatenate | bytes 131072 | tf_op jit(solution)/shard_map/stack | solution.py:282
  63.4 0.9 pad_add_fusion.hint_ref
  64.2 1.6 %collective-permute-start.9 = (s32[4,128,128]{2,1,0:T(8,128)S(1)}, s32[4,128,128]{2,1,0:T(8,128)S(1)}, u32[]{:S(2)}, u32[]{:S(2)}) collective-permute-start(s32[4,128,128]{2,1,0:T(8,128)S(1)} %pad_add_fusion.hint_ref), channel_id=1, source_target_pairs={{0,8},{4,12},{8,0},{12,4},{16,24},{20,28},{24,16},{28,20},{1,9},{5... | collective-permute-start | bytes 786440 | tf_op jit(solution)/shard_map/ppermute | solution.py:247
  65.8 1.0 slice_bitcast_fusion
  66.8 5.2 %second_matrix.7.matrix_ref = bf16[4,512,1024]{2,1,0:T(8,128)(2,1)} custom-call(s32[512,8]{1,0:T(8,128)} %get-tuple-element.9.first_ref, s32[8,128]{1,0:T(8,128)} %stack.23.second_ref), custom_call_target="tpu_custom_call" | custom-call | tf_op jit(solution)/shard_map/second_matrix/pallas_call | solution.py:156
  72.0 5.3 %second_matrix.6.matrix_ref = bf16[4,512,1024]{2,1,0:T(8,128)(2,1)} custom-call(s32[512,8]{1,0:T(8,128)} %get-tuple-element.10.first_ref, s32[8,128]{1,0:T(8,128)} %stack.23.second_ref), custom_call_target="tpu_custom_call" | custom-call | tf_op jit(solution)/shard_map/second_matrix/pallas_call | solution.py:156
  77.3 5.2 %second_matrix.5.matrix_ref = bf16[4,512,1024]{2,1,0:T(8,128)(2,1)} custom-call(s32[512,8]{1,0:T(8,128)} %get-tuple-element.11.first_ref, s32[8,128]{1,0:T(8,128)} %stack.23.second_ref), custom_call_target="tpu_custom_call" | custom-call | tf_op jit(solution)/shard_map/second_matrix/pallas_call | solution.py:156
  82.5 5.2 %second_matrix.4.matrix_ref = bf16[4,512,1024]{2,1,0:T(8,128)(2,1)} custom-call(s32[512,8]{1,0:T(8,128)} %get-tuple-element.12.first_ref, s32[8,128]{1,0:T(8,128)} %stack.23.second_ref), custom_call_target="tpu_custom_call" | custom-call | tf_op jit(solution)/shard_map/second_matrix/pallas_call | solution.py:156
  87.7 1.2 collective-permute-start.8
  88.9 0.8 collective-permute-start.4
  89.8 6.0 %second_hint.4.refs_0_ = s32[4,128,1024]{2,1,0:T(8,128)} custom-call(s32[4,128,128]{2,1,0:T(8,128)} %copy-done.5, bf16[4,512,1024]{2,1,0:T(8,128)(2,1)} %second_matrix.7.matrix_ref), custom_call_target="tpu_custom_call" | custom-call | flops 2147483648 | bytes 8388608 | tf_op jit(solution)/shard_map/second_hint/pallas_call | solution.py:200
  96.5 6.8 %second_hint.5.refs_0_ = s32[4,128,1024]{2,1,0:T(8,128)} custom-call(s32[4,128,128]{2,1,0:T(8,128)} %copy-done.2, bf16[4,512,1024]{2,1,0:T(8,128)(2,1)} %second_matrix.6.matrix_ref, s32[4,128,1024]{2,1,0:T(8,128)} %second_hint.4.refs_0_), custom_call_target="tpu_custom_call", output_to_operand_aliasing={{}: (2, {})} | custom-call | flops 2147483648 | bytes 8388608 | tf_op jit(solution)/shard_map/second_hint/pallas_call | solution.py:200
  104.0 6.8 %second_hint.6.refs_0_ = s32[4,128,1024]{2,1,0:T(8,128)} custom-call(s32[4,128,128]{2,1,0:T(8,128)} %copy-done.4, bf16[4,512,1024]{2,1,0:T(8,128)(2,1)} %second_matrix.5.matrix_ref, s32[4,128,1024]{2,1,0:T(8,128)} %second_hint.5.refs_0_), custom_call_target="tpu_custom_call", output_to_operand_aliasing={{}: (2, {})} | custom-call | flops 2147483648 | bytes 8388608 | tf_op jit(solution)/shard_map/second_hint/pallas_call | solution.py:200
  111.5 6.8 %second_hint.7.value_ref = s32[4,128,1024]{2,1,0:T(8,128)} custom-call(s32[4,128,128]{2,1,0:T(8,128)} %copy-done.3, bf16[4,512,1024]{2,1,0:T(8,128)(2,1)} %second_matrix.4.matrix_ref, s32[4,128,1024]{2,1,0:T(8,128)} %second_hint.6.refs_0_), custom_call_target="tpu_custom_call", output_to_operand_aliasing={{}: (2, {})} | custom-call | flops 2147483648 | bytes 8388608 | tf_op jit(solution)/shard_map/second_hint/pallas_call | solution.py:200
  118.3 4.3 %write_halves.2.refs_0_ = f32[4,2,256,1024]{3,2,1,0:T(8,128)} custom-call(s32[1]{0:T(128)} %bitcast._, s32[4,128,1024]{2,1,0:T(8,128)} %second_hint.7.value_ref), custom_call_target="tpu_custom_call" | custom-call | tf_op jit(solution)/shard_map/write_halves/pallas_call | solution.py:231
  122.6 1.3 %copy-done = s32[4,128,1024]{2,1,0:T(8,128)} copy-done((s32[4,128,1024]{2,1,0:T(8,128)}, s32[4,128,1024]{2,1,0:T(8,128)S(1)}, u32[]{:S(2)}) %copy-start) | copy-done | bytes 2097176
  124.0 4.3 %write_halves.3 = f32[4,2,256,1024]{3,2,1,0:T(8,128)} custom-call(s32[1]{0:T(128)S(6)} %sub.193._, s32[4,128,1024]{2,1,0:T(8,128)} %copy-done, f32[4,2,256,1024]{3,2,1,0:T(8,128)} %write_halves.2.refs_0_), custom_call_target="tpu_custom_call", output_to_operand_aliasing={{}: (2, {})} | custom-call | tf_op jit(solution)/shard_map/write_halves/pallas_call | solution.py:231
  (41 shorter events, 5.6 us)
Async XLA Ops:
  1.0 7.3 %collective-permute-start.5 = (s32[1,256]{1,0:T(1,128)S(1)}, s32[1,256]{1,0:T(1,128)S(1)}, u32[]{:S(2)}, u32[]{:S(2)}) collective-permute-start(s32[1,256]{1,0:T(1,128)S(1)} %bitcast.26), channel_id=1, source_target_pairs={{0,4},{4,0},{8,12},{12,8},{16,20},{20,16},{24,28},{28,24},{1,5},{5... | collective-permute-start | bytes 3080 | tf_op jit(solution)/shard_map/ppermute | solution.py:247
  1.5 24.0 %collective-permute-start = (bf16[64,8192]{1,0:T(8,128)(2,1)}, bf16[64,8192]{1,0:T(8,128)(2,1)S(1)}, u32[]{:S(2)}, u32[]{:S(2)}) collective-permute-start(bf16[64,8192]{1,0:T(8,128)(2,1)} %own_ref.1), channel_id=1, source_target_pairs={{0,4},{4,0},{8,12},{12,8},{16,20},{20,16},{24,28},{28,24},{1,5},{5... | collective-permute-start | bytes 3145736 | tf_op jit(solution)/shard_map/ppermute | solution.py:247
  8.4 4.5 %collective-permute-start.6 = (s32[2,256]{1,0:T(2,128)S(1)}, s32[2,256]{1,0:T(2,128)S(1)}, u32[]{:S(2)}, u32[]{:S(2)}) collective-permute-start(s32[2,256]{1,0:T(2,128)S(1)} %pad_add_fusion.3), channel_id=1, source_target_pairs={{0,8},{4,12},{8,0},{12,4},{16,24},{20,28},{24,16},{28,20},{1,9},{5... | collective-permute-start | bytes 6152 | tf_op jit(solution)/shard_map/ppermute | solution.py:247
  12.9 4.5 %collective-permute-start.7 = (s32[4,256]{1,0:T(4,128)S(1)}, s32[4,256]{1,0:T(4,128)S(1)}, u32[]{:S(2)}, u32[]{:S(2)}) collective-permute-start(s32[4,256]{1,0:T(4,128)S(1)} %pad_add_fusion.2), channel_id=1, source_target_pairs={{0,16},{4,20},{8,24},{12,28},{16,0},{20,4},{24,8},{28,12},{1,17},{... | collective-permute-start | bytes 12296 | tf_op jit(solution)/shard_map/ppermute | solution.py:247
  25.5 1.0 copy-start.1
  47.3 16.1 %collective-permute-start.3 = (s32[128,128]{1,0:T(8,128)S(1)}, s32[128,128]{1,0:T(8,128)S(1)}, u32[]{:S(2)}, u32[]{:S(2)}) collective-permute-start(s32[128,128]{1,0:T(8,128)S(1)} %get-tuple-element.20), channel_id=1, source_target_pairs={{0,3},{1,2},{2,1},{3,0},{4,7},{5,6},{6,5},{7,4},{8,11},{9,10},{10,... | collective-permute-start | bytes 196616 | tf_op jit(solution)/shard_map/ppermute | solution.py:247
  50.9 12.4 %collective-permute-start.2 = (s32[128,128]{1,0:T(8,128)S(1)}, s32[128,128]{1,0:T(8,128)S(1)}, u32[]{:S(2)}, u32[]{:S(2)}) collective-permute-start(s32[128,128]{1,0:T(8,128)S(1)} %get-tuple-element.21), channel_id=1, source_target_pairs={{0,2},{1,3},{2,0},{3,1},{4,6},{5,7},{6,4},{7,5},{8,10},{9,11},{10,... | collective-permute-start | bytes 196616 | tf_op jit(solution)/shard_map/ppermute | solution.py:247
  50.9 12.4 %collective-permute-start.1 = (s32[128,128]{1,0:T(8,128)S(1)}, s32[128,128]{1,0:T(8,128)}, u32[]{:S(2)}, u32[]{:S(2)}) collective-permute-start(s32[128,128]{1,0:T(8,128)S(1)} %get-tuple-element.22), channel_id=1, source_target_pairs={{0,1},{1,0},{2,3},{3,2},{4,5},{5,4},{6,7},{7,6},{8,9},{9,8},{10,11... | collective-permute-start | bytes 196616 | tf_op jit(solution)/shard_map/ppermute | solution.py:247
  64.2 24.7 %copy-start.5 = (s32[4,128,128]{2,1,0:T(8,128)}, s32[4,128,128]{2,1,0:T(8,128)S(1)}, u32[]{:S(2)}) copy-start(s32[4,128,128]{2,1,0:T(8,128)S(1)} %pad_add_fusion.hint_ref) | copy-start | bytes 786436
  64.2 31.6 %collective-permute-start.9 = (s32[4,128,128]{2,1,0:T(8,128)S(1)}, s32[4,128,128]{2,1,0:T(8,128)S(1)}, u32[]{:S(2)}, u32[]{:S(2)}) collective-permute-start(s32[4,128,128]{2,1,0:T(8,128)S(1)} %pad_add_fusion.hint_ref), channel_id=1, source_target_pairs={{0,8},{4,12},{8,0},{12,4},{16,24},{20,28},{24,16},{28,20},{1,9},{5... | collective-permute-start | bytes 786440 | tf_op jit(solution)/shard_map/ppermute | solution.py:247
  87.7 15.6 %collective-permute-start.8 = (s32[4,128,128]{2,1,0:T(8,128)S(1)}, s32[4,128,128]{2,1,0:T(8,128)S(1)}, u32[]{:S(2)}, u32[]{:S(2)}) collective-permute-start(s32[4,128,128]{2,1,0:T(8,128)S(1)} %pad_add_fusion.hint_ref), channel_id=1, source_target_pairs={{0,16},{4,20},{8,24},{12,28},{16,0},{20,4},{24,8},{28,12},{1,17},{... | collective-permute-start | bytes 786440 | tf_op jit(solution)/shard_map/ppermute | solution.py:247
  88.9 21.9 %collective-permute-start.4 = (s32[4,128,128]{2,1,0:T(8,128)S(1)}, s32[4,128,128]{2,1,0:T(8,128)S(1)}, u32[]{:S(2)}, u32[]{:S(2)}) collective-permute-start(s32[4,128,128]{2,1,0:T(8,128)S(1)} %pad_add_fusion.hint_ref), channel_id=1, source_target_pairs={{0,24},{4,28},{8,16},{12,20},{16,8},{20,12},{24,0},{28,4},{1,25},{... | collective-permute-start | bytes 786440 | tf_op jit(solution)/shard_map/ppermute | solution.py:247
  95.8 0.7 copy-start.2
  103.3 0.7 copy-start.4
  110.8 0.7 copy-start.3
  118.3 4.4 %collective-permute-start.10 = (s32[4,128,1024]{2,1,0:T(8,128)}, s32[4,128,1024]{2,1,0:T(8,128)S(1)}, u32[]{:S(2)}, u32[]{:S(2)}) collective-permute-start(s32[4,128,1024]{2,1,0:T(8,128)} %second_hint.7.value_ref), channel_id=1, source_target_pairs={{0,4},{4,0},{8,12},{12,8},{16,20},{20,16},{24,28},{28,24},{1,5},{5... | collective-permute-start | bytes 6291464 | tf_op jit(solution)/shard_map/ppermute | solution.py:247
  122.6 1.3 %copy-start = (s32[4,128,1024]{2,1,0:T(8,128)}, s32[4,128,1024]{2,1,0:T(8,128)S(1)}, u32[]{:S(2)}) copy-start(s32[4,128,1024]{2,1,0:T(8,128)S(1)} %collective-permute-done.10.value_ref) | copy-start | bytes 6291460
where the time goes:
time: 129 us; the launch traced here: 128 us
  Pallas kernels  75.6 us (59%)
  other arithmetic  19 us (15%)
  local copies, waits for them, and re-layouts  16.7 us (13%)
  starting transfers between devices  13.7 us (11%)
  waiting for transfers between devices  1.63 us (1%)
  between operations  1.53 us (1%)
    pallas_call x4, Pallas kernels, second_hint(): pl.pallas_call(second_kernel, grid=(columns // block,), out_shape=jax.Sha...  26.3 us
    pallas_call x4, Pallas kernels, second_matrix(): pl.pallas_call(functools.partial(matrix_kernel, columns, min(32, block)),...  20.9 us
    pallas_call x1, Pallas kernels, first_hint(): pl.pallas_call(functools.partial(first_kernel, width, lane), out_shape=ja...  19.8 us
    add x6, other arithmetic, fixed(): value * WHOLE  15 us
    ppermute x11, starting transfers between devices, shift_by(): lax.ppermute(value, axis, [(i, i ^ offset) for i in range(lax.axis_size(a...  13.7 us
    pallas_call x2, Pallas kernels, write_halves(): pl.pallas_call(halves_kernel, grid_spec=pltpu.PrefetchScalarGridSpec(num_...  8.54 us
    another operation x1, local copies, waits for them, and re-layouts, on_device(): by_row = jnp.stack(by_row + by_row[:2], axis=2)  6.07 us
    unnamed x12, local copies, waits for them, and re-layouts  3.58 us
  transfers between devices with their start and end apart: 11, of which 2 were waited for; matrix products, arithmetic and copies ran while one was open for 22% of the time, Pallas kernels for 35%

commit v1 on v0

v1 whole, which is shorter than its diff:
```python
import functools

import jax
import jax.numpy as jnp
import numpy as np
from jax import lax
from jax.experimental import pallas as pl
from jax.experimental.pallas import tpu as pltpu
from jax.sharding import PartitionSpec as P

N = 1024

PRIME = 46337
HALF_PRIME = PRIME // 2
WHOLE = (1 << 32) // PRIME
PART = (1 << 32) / PRIME - WHOLE
SCALE = np.float32(PRIME / 2.0**32)
FINE = np.float32(1.5 * 2.0**23)
INVERSE = np.float32(1 / PRIME)
OFFSET = 32896 - HALF_PRIME
COARSE = np.float32(1.5 * 2.0**31 - 1.5 * 2.0**23 - OFFSET)
FINE_OFFSET = np.float32(1.5 * 2.0**23 + OFFSET)
SUBLANES = 16
LANES = 128
NT = (((1,), (1,)), ((), ()))


def residue(value):
    value = value - (value.astype(jnp.float32) * INVERSE).astype(jnp.int32) * PRIME
    value = value + jnp.where(value < 0, PRIME, 0)
    return value - jnp.where(value >= PRIME, PRIME, 0)


def centred(value):
    return value - jnp.where(value > HALF_PRIME, PRIME, 0)


def fixed(value):
    value = centred(value)
    return value * WHOLE + jnp.round(value.astype(jnp.float32) * np.float32(PART)).astype(jnp.int32)


def bend(step):
    value = 2 * (29989 * step % PRIME) ** 2 % PRIME
    value = value - PRIME if value > HALF_PRIME else value
    return np.int32(round(value * 2**32 / PRIME))


def by_first(index, seed, step):
    rows = 8
    shape = (rows, index.shape[1])
    row = lax.broadcasted_iota(jnp.int32, shape, 0)
    kind, second = row % 4, row >= 4
    start = jnp.where(second, 7919, 0) + seed
    a = residue(residue(residue(jnp.broadcast_to(index, shape)) * 40503) + start)
    a = residue(a * a)
    factor = 2 * (29989 * step % PRIME) % PRIME
    product = residue(a * jnp.where(kind == 1, a, factor))
    product = residue(product + jnp.where(kind == 1, 12345 - HALF_PRIME + PRIME, 0))
    return jnp.where(kind == 0, centred(a), fixed(product))


def by_second(index, step):
    shift = 29989 * step % PRIME
    b = residue(residue(index) * 29989)
    slope = residue(b * (2 * shift % PRIME))
    return [
        fixed(residue(2 * b)),
        fixed(residue(b * b)),
        fixed(residue(slope + shift * shift % PRIME)),
    ]


def tables_kernel(parts, half, where_ref, seeds_ref, first_ref, second_ref):
    core, col = where_ref[0], where_ref[1]
    index = lax.broadcasted_iota(jnp.int32, (1, first_ref.shape[1]), 1)
    first_ref[...] = by_first(index, seeds_ref[0], SUBLANES)
    sub = lax.broadcasted_iota(jnp.int32, (SUBLANES, LANES), 0)
    for s in range(parts):
        index = ((col ^ s) * 2 + core) * half + sub
        for i, value in enumerate(by_second(index, SUBLANES)):
            second_ref[s, i] = value


def tables(where, seeds, depth, parts, half):
    return pl.pallas_call(
        functools.partial(tables_kernel, parts, half),
        out_shape=[
            jax.ShapeDtypeStruct((8, depth), jnp.int32),
            jax.ShapeDtypeStruct((parts, 3, SUBLANES, LANES), jnp.int32),
        ],
        in_specs=[pl.BlockSpec(memory_space=pltpu.SMEM)] * 2,
        out_specs=[pl.BlockSpec(memory_space=pltpu.VMEM)] * 2,
        name="tables",
    )(where, seeds)


def limb_pair(value):
    rounded = value.astype(jnp.float32) * SCALE + FINE
    kept = (rounded + COARSE) - COARSE
    return (rounded - kept).astype(jnp.bfloat16), (kept - FINE_OFFSET).astype(jnp.bfloat16)


def join(products):
    low_p, high_p, low_q, high_q = products
    small = np.float32(1 / 256)
    p = low_p.astype(jnp.int32) + ((high_p * small).astype(jnp.int32) << 8)
    q = low_q.astype(jnp.int32) + ((high_q * small).astype(jnp.int32) << 8)
    return p + (q << 16)


def make_limbs(first_ref, second, start, width, lane, count, store):
    second = [jnp.concatenate([value] * (lane // LANES), axis=1) for value in second]
    for t in range(width // lane):
        at = pl.ds(pl.multiple_of(start + t * lane, lane), lane)
        for mix in range(2):
            a, square, slope = (first_ref[4 * mix + i : 4 * mix + i + 1, at] for i in range(3))
            value = a * second[0] + square + second[1]
            slope = slope + second[2]
            for k in range(count):
                low, high = limb_pair(value)
                store(2 * mix, k * SUBLANES, t * lane, low)
                store(2 * mix + 1, k * SUBLANES, t * lane, high)
                value = value + slope
                slope = slope + bend(SUBLANES)


def first_kernel(width, lane, own_ref, peer_ref, first_ref, second_ref, out_ref, even, odd):
    half = out_ref.shape[0]
    total = own_ref.shape[1] // width

    def make(step, limbs):
        def store(i, row, column, value):
            top = i * half + row
            limbs[top : top + SUBLANES, column : column + lane] = value

        second = [second_ref[i] for i in range(3)]
        make_limbs(first_ref, second, step * width, width, lane, half // SUBLANES, store)

    def use(step, limbs):
        at = pl.ds(pl.multiple_of(step * width, width), width)
        records = jnp.concatenate([own_ref[:, at], peer_ref[:, at]], axis=0)
        product = lax.dot_general(limbs[...], records, NT, preferred_element_type=jnp.float32)
        out_ref[...] += join([product[i * half : (i + 1) * half] for i in range(4)])

    out_ref[...] = jnp.zeros_like(out_ref)
    make(0, even)

    @pl.loop(0, total // 2 - 1)
    def _(i):
        use(2 * i, even)
        make(2 * i + 1, odd)
        use(2 * i + 1, odd)
        make(2 * i + 2, even)

    use(total - 2, even)
    make(total - 1, odd)
    use(total - 1, odd)


def first_hint(own, peer, by_column, by_n, s, half):
    rows, depth = own.shape
    width = min(1024, depth)
    lane = min(512, width)
    whole = pl.BlockSpec(memory_space=pltpu.VMEM)
    return pl.pallas_call(
        functools.partial(first_kernel, width, lane),
        grid=(1,),
        out_shape=jax.ShapeDtypeStruct((half, 2 * rows), jnp.int32),
        in_specs=[whole] * 3 + [pl.BlockSpec((None,) + by_n.shape[1:], lambda i: (s, 0, 0, 0))],
        out_specs=whole,
        scratch_shapes=[pltpu.VMEM((4 * half, width), jnp.bfloat16)] * 2,
        cost_estimate=pl.CostEstimate(
            flops=64 * half * depth * rows, bytes_accessed=4 * depth * rows, transcendentals=0
        ),
        name="first_hint",
    )(own, peer, by_column, by_n)


def rows_kernel(seeds_ref, place_ref, out_ref):
    out_ref[...] = by_first(place_ref[...], seeds_ref[1], SUBLANES)


def row_tables(place, seeds):
    return pl.pallas_call(
        rows_kernel,
        out_shape=jax.ShapeDtypeStruct((8, place.shape[1]), jnp.int32),
        in_specs=[
            pl.BlockSpec(memory_space=pltpu.SMEM),
            pl.BlockSpec(memory_space=pltpu.VMEM),
        ],
        name="row_tables",
    )(seeds, place)


def matrix_kernel(first_ref, *refs):
    out_ref = refs[-1]
    _, block, depth = out_ref.shape

    def store(i, row, column, value):
        out_ref[i, row : row + SUBLANES, column : column + value.shape[1]] = value

    sub = lax.broadcasted_iota(jnp.int32, (SUBLANES, LANES), 0)
    second = by_second(pl.program_id(0) * block + sub, SUBLANES)
    make_limbs(first_ref, second, 0, depth, min(512, depth), block // SUBLANES, store)


def second_matrix(by_row, t, depth, columns, after=None):
    block = min(256, columns)
    return pl.pallas_call(
        matrix_kernel,
        grid=(columns // block,),
        out_shape=jax.ShapeDtypeStruct((4, columns, depth), jnp.bfloat16),
        in_specs=[pl.BlockSpec((8, depth), lambda i: (0, t))]
        + ([] if after is None else [pl.BlockSpec(memory_space=pl.ANY)]),
        out_specs=pl.BlockSpec((4, block, depth), lambda i: (0, i, 0)),
        cost_estimate=pl.CostEstimate(
            flops=400 * 20 * depth * columns,
            bytes_accessed=8 * depth * columns,
            transcendentals=0,
        ),
        name="second_matrix",
    )(by_row, *([] if after is None else [after]))


def second_kernel(count, hint_refs, matrix_ref, total_ref, out_ref, digits):
    @pl.when(pl.program_id(0) == 0)
    def _():
        half, rows = hint_refs[0].shape[-2:]
        hints = [ref[i] for ref in hint_refs for i in range(ref.shape[0])]
        for s, hint in enumerate(hints):
            for place in range(4):
                byte = (lax.shift_right_logical(hint, jnp.int32(8 * place)) & 255) - 128
                digits[place * half : (place + 1) * half, s * rows : (s + 1) * rows] = byte.astype(
                    jnp.float32
                ).astype(jnp.bfloat16)

    half = out_ref.shape[1]
    total = join(
        [
            lax.dot_general(digits[...], matrix_ref[i], NT, preferred_element_type=jnp.float32)
            for i in range(4)
        ]
    )
    for place in range(4):
        term = total[place * half : (place + 1) * half]
        out_ref[place] = term if total_ref is None else total_ref[place] + term


def second_hint(hints, matrix, total=None):
    half, rows = hints[0].shape[1:]
    _, columns, depth = matrix.shape
    block = min(256, columns)
    out_spec = pl.BlockSpec((4, half, block), lambda i: (0, 0, i))
    count = len(hints)

    def kernel(*refs):
        previous = None if total is None else refs[count + 1]
        second_kernel(count, refs[:count], refs[count], previous, refs[-2], refs[-1])

    return pl.pallas_call(
        kernel,
        grid=(columns // block,),
        out_shape=jax.ShapeDtypeStruct((4, half, columns), jnp.int32),
        in_specs=[pl.BlockSpec(hint.shape, lambda i: (0, 0, 0)) for hint in hints]
        + [pl.BlockSpec((4, block, depth), lambda i: (0, i, 0))]
        + ([] if total is None else [out_spec]),
        out_specs=out_spec,
        scratch_shapes=[pltpu.VMEM((4 * half, depth), jnp.bfloat16)],
        input_output_aliases={} if total is None else {count + 1: 0},
        cost_estimate=pl.CostEstimate(
            flops=32 * half * depth * columns,
            bytes_accessed=8 * depth * columns + 32 * half * columns,
            transcendentals=0,
        ),
        name="second_hint",
    )(*hints, matrix, *([] if total is None else [total]))


def halves_kernel(_, value_ref, *refs):
    out_ref = refs[-1]
    value = value_ref[...]
    scale = np.float32(1 / 65536)
    out_ref[:, 0] = (value & 65535).astype(jnp.float32) * scale
    out_ref[:, 1] = lax.shift_right_logical(value, jnp.int32(16)).astype(jnp.float32) * scale


def write_halves(value, place, out=None):
    digits, half, columns = value.shape
    return pl.pallas_call(
        halves_kernel,
        grid_spec=pltpu.PrefetchScalarGridSpec(
            num_scalar_prefetch=1,
            grid=(digits,),
            in_specs=[pl.BlockSpec((1, half, columns), lambda i, place: (i, 0, 0))]
            + ([] if out is None else [pl.BlockSpec(memory_space=pl.ANY)]),
            out_specs=pl.BlockSpec((1, 2, half, columns), lambda i, place: (i, 0, place[0], 0)),
        ),
        out_shape=jax.ShapeDtypeStruct((digits, 2, 2 * half, columns), jnp.float32),
        input_output_aliases={} if out is None else {2: 0},
        name="write_halves",
    )(place, value, *([] if out is None else [out]))


def shift_by(value, axis, offset):
    return lax.ppermute(value, axis, [(i, i ^ offset) for i in range(lax.axis_size(axis))])


def on_device(ingest, row_order, matrix_seeds):
    row_size, col_size = lax.axis_size("row"), lax.axis_size("col")
    row, col = lax.axis_index("row"), lax.axis_index("col")
    core = row % 2
    rows, depth = ingest.shape
    half = N // col_size // 2

    peer = shift_by(ingest, "row", 1)
    order = row_order[0]
    block_rows = order.shape[0]
    k_index = lax.broadcasted_iota(jnp.int32, (block_rows, block_rows), 1)
    r_index = lax.broadcasted_iota(jnp.int32, (block_rows, block_rows), 0)
    place = jnp.sum(jnp.where(order[None, :] == r_index, k_index, 0), axis=1) + row * block_rows
    place = jnp.concatenate(
        [lax.dynamic_slice_in_dim(place, (col ^ s) * rows, rows) for s in range(col_size)]
    )
    place = jnp.stack([place, shift_by(place, "row", 1)])
    places = [place] + [shift_by(place, "row", 2 * t) for t in range(1, row_size // 2)]

    where = jnp.stack([core, col]).astype(jnp.int32)
    by_column, by_n = tables(where, matrix_seeds, depth, col_size, half)

    hints = [None] * col_size
    for s in reversed(range(col_size)):
        part = first_hint(ingest, peer, by_column, by_n, s, half)
        hints[s] = shift_by(part, "col", s) if s else part

    place = jnp.stack(places).reshape(row_size // 2, 2, col_size, rows).transpose(0, 2, 1, 3)
    by_row = row_tables(place.reshape(1, -1), matrix_seeds)

    cut = col_size // 2
    late, early = jnp.stack(hints[:cut]), jnp.stack(hints[cut:])
    total = None
    for t in range(row_size // 2):
        matrix = second_matrix(by_row, t, 2 * col_size * rows, N, total if t >= 4 else None)
        groups = [shift_by(late, "row", 2 * t), shift_by(early, "row", 2 * t)] if t else [late, early]
        total = second_hint(groups, matrix, total)

    other = shift_by(total, "row", 1)
    out = write_halves(total, core[None])
    return write_halves(other, 1 - core[None], out)


def solution(mesh):
    in_specs = (P(("row", "col"), None), P("row", None), P())
    out_specs = P(None, None, "col", None)
    return jax.shard_map(
        on_device, mesh=mesh, in_specs=in_specs, out_specs=out_specs, check_vma=False
    )
```

time: 129 us -> 108 us (0.84)
  other arithmetic: 19 us -> 2.34 us
  local copies, waits for them, and re-layouts: 16.7 us -> 7.04 us
  Pallas kernels: 75.6 us -> 80.1 us
  starting transfers between devices: 13.7 us -> 16.5 us
  between operations: 1.53 us -> 0.12 us
    add x6 -> x0, other arithmetic: 15 us -> none  [fixed(): value * WHOLE]
    another operation x3 -> x5, local copies, waits for them, and re-layouts: 7.77 us -> 0.41 us  [the longest x3 0.24 us: on_device(): jnp.stack(places).reshape(row_size // 2, 2, col_size, rows)]
    pallas_call x9 -> x14, Pallas kernels: 67.1 us -> 71.6 us  [the longest x4 26.3 us: first_hint(): pl.pallas_call(functools.partial(first_kernel, width, lane), grid=(1,), o...]
    ppermute x11 -> x15, starting transfers between devices: 13.7 us -> 16.5 us  [shift_by(): lax.ppermute(value, axis, [(i, i ^ offset) for i in range(lax.axis_size(a...]
    unnamed x12 -> x20, local copies, waits for them, and re-layouts: 3.58 us -> 5.85 us
    sub x2 -> x0, other arithmetic: 2.23 us -> none  [centred(): return value - jnp.where(value > HALF_PRIME, PRIME, 0)]
    slice x1 -> x0, local copies, waits for them, and re-layouts: 1.32 us -> none  [on_device(): matrix_seeds[1]]
  transfers between devices with their start and end apart: 11 -> 15, of which waited for: 2 -> 3; matrix products, arithmetic and copies ran while one was open for 22% -> 2% of each run, Pallas kernels for 35% -> 58%
where the time goes in v1:
time: 108 us; the launch traced here: 107 us
  Pallas kernels  80.1 us (74%)
  starting transfers between devices  16.5 us (15%)
  local copies, waits for them, and re-layouts  7.04 us (7%)
  other arithmetic  2.34 us (2%)
  waiting for transfers between devices  1.17 us (1%)
    pallas_call x4, Pallas kernels, first_hint(): pl.pallas_call(functools.partial(first_kernel, width, lane), grid=(1,), o...  26.3 us
    pallas_call x4, Pallas kernels, second_hint(): pl.pallas_call(kernel, grid=(columns // block,), out_shape=jax.ShapeDtype...  25.6 us
    ppermute x15, starting transfers between devices, shift_by(): lax.ppermute(value, axis, [(i, i ^ offset) for i in range(lax.axis_size(a...  16.5 us
    pallas_call x4, Pallas kernels, second_matrix(): pl.pallas_call(matrix_kernel, grid=(columns // block,), out_shape=jax.Sha...  15.9 us
    pallas_call x2, Pallas kernels, write_halves(): pl.pallas_call(halves_kernel, grid_spec=pltpu.PrefetchScalarGridSpec(num_...  8.54 us
    unnamed x20, local copies, waits for them, and re-layouts  5.85 us
    pallas_call x1, Pallas kernels, tables(): pl.pallas_call(functools.partial(tables_kernel, parts, half), out_shape=[...  2.23 us
  transfers between devices with their start and end apart: 15, of which 3 were waited for; matrix products, arithmetic and copies ran while one was open for 2% of the time, Pallas kernels for 58%

profile of v1, /device:TPU:0, one launch (start us, length us, event | category | flops | bytes accessed | tf_op | source)
XLA Modules:
  0.0 107.3 jit_solution(16694344350790065025)
XLA Ops:
  0.0 0.8 select_reduce_fusion
  1.6 0.7 collective-permute-done.6
  2.3 3.8 %collective-permute-start.9 = (s32[2,256]{1,0:T(2,128)S(1)}, s32[2,256]{1,0:T(2,128)S(1)}, u32[]{:S(2)}, u32[]{:S(2)}) collective-permute-start(s32[2,256]{1,0:T(2,128)S(1)} %pad_add_fusion.2), channel_id=1, source_target_pairs={{0,24},{4,28},{8,16},{12,20},{16,8},{20,12},{24,0},{28,4},{1,25},{... | collective-permute-start | bytes 6152 | tf_op jit(solution)/shard_map/ppermute | solution.py:306
  7.4 2.2 %tables.1 = (s32[8,8192]{1,0:T(8,128)}, s32[4,3,16,128]{3,2,1,0:T(8,128)}) custom-call(s32[2]{0:T(128)} %pad_add_fusion.4.where_ref, s32[2]{0:T(128)} %seeds_ref.3), custom_call_target="tpu_custom_call" | custom-call | tf_op jit(solution)/shard_map/tables/pallas_call | solution.py:86
  10.3 0.7 reshape.16.place_ref
  11.0 1.6 %row_tables.1.first_ref = s32[8,2048]{1,0:T(8,128)} custom-call(s32[2]{0:T(128)} %seeds_ref.3, s32[1,2048]{1,0:T(1,128)} %reshape.16.place_ref), custom_call_target="tpu_custom_call" | custom-call | tf_op jit(solution)/shard_map/row_tables/pallas_call | solution.py:185
  12.5 4.0 %second_matrix.7.refs_2_ = bf16[4,1024,512]{2,1,0:T(8,128)(2,1)} custom-call(s32[8,2048]{1,0:T(8,128)} %row_tables.1.first_ref), custom_call_target="tpu_custom_call" | custom-call | flops 4194304000 | bytes 4194304 | tf_op jit(solution)/shard_map/second_matrix/pallas_call | solution.py:210
  16.5 4.0 %second_matrix.6.refs_2_ = bf16[4,1024,512]{2,1,0:T(8,128)(2,1)} custom-call(s32[8,2048]{1,0:T(8,128)} %row_tables.1.first_ref), custom_call_target="tpu_custom_call" | custom-call | flops 4194304000 | bytes 4194304 | tf_op jit(solution)/shard_map/second_matrix/pallas_call | solution.py:210
  20.5 4.0 %second_matrix.5.refs_2_ = bf16[4,1024,512]{2,1,0:T(8,128)(2,1)} custom-call(s32[8,2048]{1,0:T(8,128)} %row_tables.1.first_ref), custom_call_target="tpu_custom_call" | custom-call | flops 4194304000 | bytes 4194304 | tf_op jit(solution)/shard_map/second_matrix/pallas_call | solution.py:210
  24.5 3.9 %second_matrix.4.refs_2_ = bf16[4,1024,512]{2,1,0:T(8,128)(2,1)} custom-call(s32[8,2048]{1,0:T(8,128)} %row_tables.1.first_ref), custom_call_target="tpu_custom_call" | custom-call | flops 4194304000 | bytes 4194304 | tf_op jit(solution)/shard_map/second_matrix/pallas_call | solution.py:210
  28.4 1.0 copy-done.9
  29.5 6.6 %first_hint.5 = s32[128,128]{1,0:T(8,128)} custom-call(bf16[64,8192]{1,0:T(8,128)(2,1)} %own_ref.7, bf16[64,8192]{1,0:T(8,128)(2,1)} %copy-done.9, s32[8,8192]{1,0:T(8,128)} %get-tuple-element.7.first_ref, s32[4,3,16,128]{3,2,1,0:T(8,128)} %get-tuple-element.8.second_ref), custom_call_target="tpu_custom_call" | custom-call | flops 4294967296 | bytes 2097152 | tf_op jit(solution)/shard_map/first_hint/pallas_call | solution.py:166
  36.0 1.7 %collective-permute-start.1 = (s32[128,128]{1,0:T(8,128)}, s32[128,128]{1,0:T(8,128)S(1)}, u32[]{:S(2)}, u32[]{:S(2)}) collective-permute-start(s32[128,128]{1,0:T(8,128)} %first_hint.5), channel_id=1, source_target_pairs={{0,1},{1,0},{2,3},{3,2},{4,5},{5,4},{6,7},{7,6},{8,9},{9,8},{10,11... | collective-permute-start | bytes 196616 | tf_op jit(solution)/shard_map/ppermute | solution.py:306
  37.7 6.6 %first_hint.6 = s32[128,128]{1,0:T(8,128)} custom-call(bf16[64,8192]{1,0:T(8,128)(2,1)} %own_ref.7, bf16[64,8192]{1,0:T(8,128)(2,1)} %copy-done.9, s32[8,8192]{1,0:T(8,128)} %get-tuple-element.7.first_ref, s32[4,3,16,128]{3,2,1,0:T(8,128)} %get-tuple-element.8.second_ref), custom_call_target="tpu_custom_call" | custom-call | flops 4294967296 | bytes 2097152 | tf_op jit(solution)/shard_map/first_hint/pallas_call | solution.py:166
  44.3 2.6 %collective-permute-start.3 = (s32[128,128]{1,0:T(8,128)}, s32[128,128]{1,0:T(8,128)S(1)}, u32[]{:S(2)}, u32[]{:S(2)}) collective-permute-start(s32[128,128]{1,0:T(8,128)} %first_hint.6), channel_id=1, source_target_pairs={{0,2},{1,3},{2,0},{3,1},{4,6},{5,7},{6,4},{7,5},{8,10},{9,11},{10,... | collective-permute-start | bytes 196616 | tf_op jit(solution)/shard_map/ppermute | solution.py:306
  46.9 6.6 %first_hint.7 = s32[128,128]{1,0:T(8,128)} custom-call(bf16[64,8192]{1,0:T(8,128)(2,1)} %own_ref.7, bf16[64,8192]{1,0:T(8,128)(2,1)} %copy-done.9, s32[8,8192]{1,0:T(8,128)} %get-tuple-element.7.first_ref, s32[4,3,16,128]{3,2,1,0:T(8,128)} %get-tuple-element.8.second_ref), custom_call_target="tpu_custom_call" | custom-call | flops 4294967296 | bytes 2097152 | tf_op jit(solution)/shard_map/first_hint/pallas_call | solution.py:166
  53.5 6.6 %first_hint.4 = s32[128,128]{1,0:T(8,128)} custom-call(bf16[64,8192]{1,0:T(8,128)(2,1)} %own_ref.7, bf16[64,8192]{1,0:T(8,128)(2,1)} %copy-done.9, s32[8,8192]{1,0:T(8,128)} %get-tuple-element.7.first_ref, s32[4,3,16,128]{3,2,1,0:T(8,128)} %get-tuple-element.8.second_ref), custom_call_target="tpu_custom_call" | custom-call | flops 4294967296 | bytes 2097152 | tf_op jit(solution)/shard_map/first_hint/pallas_call | solution.py:166
  60.1 1.7 %collective-permute-start.13 = (s32[2,128,128]{2,1,0:T(8,128)S(1)}, s32[2,128,128]{2,1,0:T(8,128)S(1)}, u32[]{:S(2)}, u32[]{:S(2)}) collective-permute-start(s32[2,128,128]{2,1,0:T(8,128)S(1)} %pad_add_fusion.1.refs_1_), channel_id=1, source_target_pairs={{0,8},{4,12},{8,0},{12,4},{16,24},{20,28},{24,16},{28,20},{1,9},{5... | collective-permute-start | bytes 393224 | tf_op jit(solution)/shard_map/ppermute | solution.py:306
  61.8 1.5 %collective-permute-start.11 = (s32[2,128,128]{2,1,0:T(8,128)S(1)}, s32[2,128,128]{2,1,0:T(8,128)S(1)}, u32[]{:S(2)}, u32[]{:S(2)}) collective-permute-start(s32[2,128,128]{2,1,0:T(8,128)S(1)} %pad_add_fusion.1.refs_1_), channel_id=1, source_target_pairs={{0,16},{4,20},{8,24},{12,28},{16,0},{20,4},{24,8},{28,12},{1,17},{... | collective-permute-start | bytes 393224 | tf_op jit(solution)/shard_map/ppermute | solution.py:306
  63.7 0.8 pad_add_fusion.refs_0_
  64.6 1.7 %collective-permute-start.12 = (s32[2,128,128]{2,1,0:T(8,128)S(1)}, s32[2,128,128]{2,1,0:T(8,128)S(1)}, u32[]{:S(2)}, u32[]{:S(2)}) collective-permute-start(s32[2,128,128]{2,1,0:T(8,128)S(1)} %pad_add_fusion.refs_0_), channel_id=1, source_target_pairs={{0,8},{4,12},{8,0},{12,4},{16,24},{20,28},{24,16},{28,20},{1,9},{5... | collective-permute-start | bytes 393224 | tf_op jit(solution)/shard_map/ppermute | solution.py:306
  66.2 1.5 %collective-permute-start.10 = (s32[2,128,128]{2,1,0:T(8,128)S(1)}, s32[2,128,128]{2,1,0:T(8,128)S(1)}, u32[]{:S(2)}, u32[]{:S(2)}) collective-permute-start(s32[2,128,128]{2,1,0:T(8,128)S(1)} %pad_add_fusion.refs_0_), channel_id=1, source_target_pairs={{0,16},{4,20},{8,24},{12,28},{16,0},{20,4},{24,8},{28,12},{1,17},{... | collective-permute-start | bytes 393224 | tf_op jit(solution)/shard_map/ppermute | solution.py:306
  67.8 6.1 %second_hint.4.refs_3_ = s32[4,128,1024]{2,1,0:T(8,128)} custom-call(s32[2,128,128]{2,1,0:T(8,128)} %copy-done.8, s32[2,128,128]{2,1,0:T(8,128)} %copy-done.7, bf16[4,1024,512]{2,1,0:T(8,128)(2,1)} %second_matrix.7.refs_2_), custom_call_target="tpu_custom_call" | custom-call | flops 2147483648 | bytes 8388608 | tf_op jit(solution)/shard_map/second_hint/pallas_call | solution.py:261
  74.5 0.7 copy-done.6
  75.2 6.5 %second_hint.5.refs_3_ = s32[4,128,1024]{2,1,0:T(8,128)} custom-call(s32[2,128,128]{2,1,0:T(8,128)} %copy-done.6, s32[2,128,128]{2,1,0:T(8,128)} %copy-done.3, bf16[4,1024,512]{2,1,0:T(8,128)(2,1)} %second_matrix.6.refs_2_, s32[4,128,1024]{2,1,0:T(8,128)} %second_hint.4.refs_3_), custom_call_target="tpu_custom_call", output_to_operand_aliasing={{}: (3, {})} | custom-call | flops 2147483648 | bytes 8388608 | tf_op jit(solution)/shard_map/second_hint/pallas_call | solution.py:261
  81.7 0.7 copy-done.2
  82.4 0.7 copy-done.5
  83.0 6.5 %second_hint.6.refs_3_ = s32[4,128,1024]{2,1,0:T(8,128)} custom-call(s32[2,128,128]{2,1,0:T(8,128)} %copy-done.5, s32[2,128,128]{2,1,0:T(8,128)} %copy-done.2, bf16[4,1024,512]{2,1,0:T(8,128)(2,1)} %second_matrix.5.refs_2_, s32[4,128,1024]{2,1,0:T(8,128)} %second_hint.5.refs_3_), custom_call_target="tpu_custom_call", output_to_operand_aliasing={{}: (3, {})} | custom-call | flops 2147483648 | bytes 8388608 | tf_op jit(solution)/shard_map/second_hint/pallas_call | solution.py:261
  90.8 6.5 %second_hint.7.value_ref = s32[4,128,1024]{2,1,0:T(8,128)} custom-call(s32[2,128,128]{2,1,0:T(8,128)} %copy-done.4, s32[2,128,128]{2,1,0:T(8,128)} %copy-done.1, bf16[4,1024,512]{2,1,0:T(8,128)(2,1)} %second_matrix.4.refs_2_, s32[4,128,1024]{2,1,0:T(8,128)} %second_hint.6.refs_3_), custom_call_target="tpu_custom_call", output_to_operand_aliasing={{}: (3, {})} | custom-call | flops 2147483648 | bytes 8388608 | tf_op jit(solution)/shard_map/second_hint/pallas_call | solution.py:261
  97.3 4.3 %write_halves.2.refs_0_ = f32[4,2,256,1024]{3,2,1,0:T(8,128)} custom-call(s32[1]{0:T(128)} %bitcast._, s32[4,128,1024]{2,1,0:T(8,128)} %second_hint.7.value_ref), custom_call_target="tpu_custom_call" | custom-call | tf_op jit(solution)/shard_map/write_halves/pallas_call | solution.py:290
  101.7 1.3 %copy-done = s32[4,128,1024]{2,1,0:T(8,128)} copy-done((s32[4,128,1024]{2,1,0:T(8,128)}, s32[4,128,1024]{2,1,0:T(8,128)S(1)}, u32[]{:S(2)}) %copy-start) | copy-done | bytes 2097176
  103.0 4.3 %write_halves.3 = f32[4,2,256,1024]{3,2,1,0:T(8,128)} custom-call(s32[1]{0:T(128)S(6)} %sub.3._, s32[4,128,1024]{2,1,0:T(8,128)} %copy-done, f32[4,2,256,1024]{3,2,1,0:T(8,128)} %write_halves.2.refs_0_), custom_call_target="tpu_custom_call", output_to_operand_aliasing={{}: (2, {})} | custom-call | tf_op jit(solution)/shard_map/write_halves/pallas_call | solution.py:290
  (50 shorter events, 5.3 us)
Async XLA Ops:
  1.0 1.3 %collective-permute-start.6 = (s32[256]{0:T(256)S(1)}, s32[256]{0:T(256)S(1)}, u32[]{:S(2)}, u32[]{:S(2)}) collective-permute-start(s32[256]{0:T(256)S(1)} %pad_add_fusion.3), channel_id=1, source_target_pairs={{0,4},{4,0},{8,12},{12,8},{16,20},{20,16},{24,28},{28,24},{1,5},{5... | collective-permute-start | bytes 3080 | tf_op jit(solution)/shard_map/ppermute | solution.py:306
  1.5 26.9 %collective-permute-start = (bf16[64,8192]{1,0:T(8,128)(2,1)}, bf16[64,8192]{1,0:T(8,128)(2,1)S(1)}, u32[]{:S(2)}, u32[]{:S(2)}) collective-permute-start(bf16[64,8192]{1,0:T(8,128)(2,1)} %own_ref.7), channel_id=1, source_target_pairs={{0,4},{4,0},{8,12},{12,8},{16,20},{20,16},{24,28},{28,24},{1,5},{5... | collective-permute-start | bytes 3145736 | tf_op jit(solution)/shard_map/ppermute | solution.py:306
  2.3 7.4 %collective-permute-start.9 = (s32[2,256]{1,0:T(2,128)S(1)}, s32[2,256]{1,0:T(2,128)S(1)}, u32[]{:S(2)}, u32[]{:S(2)}) collective-permute-start(s32[2,256]{1,0:T(2,128)S(1)} %pad_add_fusion.2), channel_id=1, source_target_pairs={{0,24},{4,28},{8,16},{12,20},{16,8},{20,12},{24,0},{28,4},{1,25},{... | collective-permute-start | bytes 6152 | tf_op jit(solution)/shard_map/ppermute | solution.py:306
  6.1 3.7 %collective-permute-start.8 = (s32[2,256]{1,0:T(2,128)S(1)}, s32[2,256]{1,0:T(2,128)S(1)}, u32[]{:S(2)}, u32[]{:S(2)}) collective-permute-start(s32[2,256]{1,0:T(2,128)S(1)} %pad_add_fusion.2), channel_id=1, source_target_pairs={{0,16},{4,20},{8,24},{12,28},{16,0},{20,4},{24,8},{28,12},{1,17},{... | collective-permute-start | bytes 6152 | tf_op jit(solution)/shard_map/ppermute | solution.py:306
  6.6 3.6 %collective-permute-start.7 = (s32[2,256]{1,0:T(2,128)S(1)}, s32[2,256]{1,0:T(2,128)S(1)}, u32[]{:S(2)}, u32[]{:S(2)}) collective-permute-start(s32[2,256]{1,0:T(2,128)S(1)} %pad_add_fusion.2), channel_id=1, source_target_pairs={{0,8},{4,12},{8,0},{12,4},{16,24},{20,28},{24,16},{28,20},{1,9},{5... | collective-permute-start | bytes 6152 | tf_op jit(solution)/shard_map/ppermute | solution.py:306
  28.4 1.0 copy-start.9
  36.0 27.7 %collective-permute-start.1 = (s32[128,128]{1,0:T(8,128)}, s32[128,128]{1,0:T(8,128)S(1)}, u32[]{:S(2)}, u32[]{:S(2)}) collective-permute-start(s32[128,128]{1,0:T(8,128)} %first_hint.5), channel_id=1, source_target_pairs={{0,1},{1,0},{2,3},{3,2},{4,5},{5,4},{6,7},{7,6},{8,9},{9,8},{10,11... | collective-permute-start | bytes 196616 | tf_op jit(solution)/shard_map/ppermute | solution.py:306
  44.3 15.8 %collective-permute-start.3 = (s32[128,128]{1,0:T(8,128)}, s32[128,128]{1,0:T(8,128)S(1)}, u32[]{:S(2)}, u32[]{:S(2)}) collective-permute-start(s32[128,128]{1,0:T(8,128)} %first_hint.6), channel_id=1, source_target_pairs={{0,2},{1,3},{2,0},{3,1},{4,6},{5,7},{6,4},{7,5},{8,10},{9,11},{10,... | collective-permute-start | bytes 196616 | tf_op jit(solution)/shard_map/ppermute | solution.py:306
  53.4 6.7 %collective-permute-start.4 = (s32[128,128]{1,0:T(8,128)}, s32[128,128]{1,0:T(8,128)S(1)}, u32[]{:S(2)}, u32[]{:S(2)}) collective-permute-start(s32[128,128]{1,0:T(8,128)} %first_hint.7), channel_id=1, source_target_pairs={{0,3},{1,2},{2,1},{3,0},{4,7},{5,6},{6,5},{7,4},{8,11},{9,10},{10,... | collective-permute-start | bytes 196616 | tf_op jit(solution)/shard_map/ppermute | solution.py:306
  60.1 7.6 %copy-start.7 = (s32[2,128,128]{2,1,0:T(8,128)}, s32[2,128,128]{2,1,0:T(8,128)S(1)}, u32[]{:S(2)}) copy-start(s32[2,128,128]{2,1,0:T(8,128)S(1)} %pad_add_fusion.1.refs_1_) | copy-start | bytes 393220
  60.1 13.7 %collective-permute-start.13 = (s32[2,128,128]{2,1,0:T(8,128)S(1)}, s32[2,128,128]{2,1,0:T(8,128)S(1)}, u32[]{:S(2)}, u32[]{:S(2)}) collective-permute-start(s32[2,128,128]{2,1,0:T(8,128)S(1)} %pad_add_fusion.1.refs_1_), channel_id=1, source_target_pairs={{0,8},{4,12},{8,0},{12,4},{16,24},{20,28},{24,16},{28,20},{1,9},{5... | collective-permute-start | bytes 393224 | tf_op jit(solution)/shard_map/ppermute | solution.py:306
  61.8 19.9 %collective-permute-start.11 = (s32[2,128,128]{2,1,0:T(8,128)S(1)}, s32[2,128,128]{2,1,0:T(8,128)S(1)}, u32[]{:S(2)}, u32[]{:S(2)}) collective-permute-start(s32[2,128,128]{2,1,0:T(8,128)S(1)} %pad_add_fusion.1.refs_1_), channel_id=1, source_target_pairs={{0,16},{4,20},{8,24},{12,28},{16,0},{20,4},{24,8},{28,12},{1,17},{... | collective-permute-start | bytes 393224 | tf_op jit(solution)/shard_map/ppermute | solution.py:306
  63.3 26.2 %collective-permute-start.5 = (s32[2,128,128]{2,1,0:T(8,128)S(1)}, s32[2,128,128]{2,1,0:T(8,128)S(1)}, u32[]{:S(2)}, u32[]{:S(2)}) collective-permute-start(s32[2,128,128]{2,1,0:T(8,128)S(1)} %pad_add_fusion.1.refs_1_), channel_id=1, source_target_pairs={{0,24},{4,28},{8,16},{12,20},{16,8},{20,12},{24,0},{28,4},{1,25},{... | collective-permute-start | bytes 393224 | tf_op jit(solution)/shard_map/ppermute | solution.py:306
  64.5 3.2 %copy-start.8 = (s32[2,128,128]{2,1,0:T(8,128)}, s32[2,128,128]{2,1,0:T(8,128)S(1)}, u32[]{:S(2)}) copy-start(s32[2,128,128]{2,1,0:T(8,128)S(1)} %pad_add_fusion.refs_0_) | copy-start | bytes 393220
  64.6 9.8 %collective-permute-start.12 = (s32[2,128,128]{2,1,0:T(8,128)S(1)}, s32[2,128,128]{2,1,0:T(8,128)S(1)}, u32[]{:S(2)}, u32[]{:S(2)}) collective-permute-start(s32[2,128,128]{2,1,0:T(8,128)S(1)} %pad_add_fusion.refs_0_), channel_id=1, source_target_pairs={{0,8},{4,12},{8,0},{12,4},{16,24},{20,28},{24,16},{28,20},{1,9},{5... | collective-permute-start | bytes 393224 | tf_op jit(solution)/shard_map/ppermute | solution.py:306
  66.2 15.5 %collective-permute-start.10 = (s32[2,128,128]{2,1,0:T(8,128)S(1)}, s32[2,128,128]{2,1,0:T(8,128)S(1)}, u32[]{:S(2)}, u32[]{:S(2)}) collective-permute-start(s32[2,128,128]{2,1,0:T(8,128)S(1)} %pad_add_fusion.refs_0_), channel_id=1, source_target_pairs={{0,16},{4,20},{8,24},{12,28},{16,0},{20,4},{24,8},{28,12},{1,17},{... | collective-permute-start | bytes 393224 | tf_op jit(solution)/shard_map/ppermute | solution.py:306
  73.9 0.7 copy-start.3
  73.9 15.7 %collective-permute-start.2 = (s32[2,128,128]{2,1,0:T(8,128)}, s32[2,128,128]{2,1,0:T(8,128)S(1)}, u32[]{:S(2)}, u32[]{:S(2)}) collective-permute-start(s32[2,128,128]{2,1,0:T(8,128)} %copy-done.8), channel_id=1, source_target_pairs={{0,24},{4,28},{8,16},{12,20},{16,8},{20,12},{24,0},{28,4},{1,25},{... | collective-permute-start | bytes 393224 | tf_op jit(solution)/shard_map/ppermute | solution.py:306
  74.5 0.7 copy-start.6
  81.7 0.7 copy-start.2
  82.4 0.7 copy-start.5
  89.5 0.6 copy-start.1
  90.2 0.7 copy-start.4
  97.3 4.4 %collective-permute-start.14 = (s32[4,128,1024]{2,1,0:T(8,128)}, s32[4,128,1024]{2,1,0:T(8,128)S(1)}, u32[]{:S(2)}, u32[]{:S(2)}) collective-permute-start(s32[4,128,1024]{2,1,0:T(8,128)} %second_hint.7.value_ref), channel_id=1, source_target_pairs={{0,4},{4,0},{8,12},{12,8},{16,20},{20,16},{24,28},{28,24},{1,5},{5... | collective-permute-start | bytes 6291464 | tf_op jit(solution)/shard_map/ppermute | solution.py:306
  101.7 1.3 %copy-start = (s32[4,128,1024]{2,1,0:T(8,128)}, s32[4,128,1024]{2,1,0:T(8,128)S(1)}, u32[]{:S(2)}) copy-start(s32[4,128,1024]{2,1,0:T(8,128)S(1)} %collective-permute-done.14.value_ref) | copy-start | bytes 6291460

commit v2 on v1

--- a/solution.py
+++ b/solution.py
@@ -21,6 +21,7 @@
 COARSE = np.float32(1.5 * 2.0**31 - 1.5 * 2.0**23 - OFFSET)
 FINE_OFFSET = np.float32(1.5 * 2.0**23 + OFFSET)
 SUBLANES = 16
+VMEM_LIMIT = 16 << 20
 LANES = 128
 NT = (((1,), (1,)), ((), ()))
 
@@ -91,6 +92,7 @@
         ],
         in_specs=[pl.BlockSpec(memory_space=pltpu.SMEM)] * 2,
         out_specs=[pl.BlockSpec(memory_space=pltpu.VMEM)] * 2,
+        compiler_params=pltpu.CompilerParams(vmem_limit_bytes=VMEM_LIMIT),
         name="tables",
     )(where, seeds)
 
@@ -102,11 +104,8 @@
 
 
 def join(products):
-    low_p, high_p, low_q, high_q = products
-    small = np.float32(1 / 256)
-    p = low_p.astype(jnp.int32) + ((high_p * small).astype(jnp.int32) << 8)
-    q = low_q.astype(jnp.int32) + ((high_q * small).astype(jnp.int32) << 8)
-    return p + (q << 16)
+    low_p, high_p, low_q, high_q = (product.astype(jnp.int32) for product in products)
+    return low_p + (((low_q + (high_q << 8)) << 8) + high_p << 8)
 
 
 def make_limbs(first_ref, second, start, width, lane, count, store):
@@ -125,25 +124,36 @@
                 slope = slope + bend(SUBLANES)
 
 
-def first_kernel(width, lane, own_ref, peer_ref, first_ref, second_ref, out_ref, even, odd):
-    half = out_ref.shape[0]
+def first_kernel(width, lane, own_ref, peer_ref, first_ref, second_ref, *refs):
+    outs, even, odd = refs[:-2], refs[-2], refs[-1]
+    half = outs[0].shape[0]
     total = own_ref.shape[1] // width
+    small = jnp.bfloat16(1 / 256)
 
     def make(step, limbs):
-        def store(i, row, column, value):
-            top = i * half + row
-            limbs[top : top + SUBLANES, column : column + lane] = value
-
-        second = [second_ref[i] for i in range(3)]
-        make_limbs(first_ref, second, step * width, width, lane, half // SUBLANES, store)
+        for s in range(len(outs)):
+
+            def store(i, row, column, value):
+                top = ((i % 2 * len(outs) + s) * 2 + i // 2) * half + row
+                limbs[top : top + SUBLANES, column : column + lane] = value
+
+            second = [second_ref[s, i] for i in range(3)]
+            make_limbs(first_ref, second, step * width, width, lane, half // SUBLANES, store)
 
     def use(step, limbs):
         at = pl.ds(pl.multiple_of(step * width, width), width)
         records = jnp.concatenate([own_ref[:, at], peer_ref[:, at]], axis=0)
-        product = lax.dot_general(limbs[...], records, NT, preferred_element_type=jnp.float32)
-        out_ref[...] += join([product[i * half : (i + 1) * half] for i in range(4)])
-
-    out_ref[...] = jnp.zeros_like(out_ref)
+        middle = limbs.shape[0] // 2
+        low = lax.dot_general(limbs[:middle], records, NT, preferred_element_type=jnp.float32)
+        high = lax.dot_general(
+            limbs[middle:], records * small, NT, preferred_element_type=jnp.float32
+        )
+        for s, out_ref in enumerate(outs):
+            p, q = (slice((2 * s + i) * half, (2 * s + i + 1) * half) for i in range(2))
+            out_ref[...] += join([low[p], high[p], low[q], high[q]])
+
+    for out_ref in outs:
+        out_ref[...] = jnp.zeros_like(out_ref)
     make(0, even)
 
     @pl.loop(0, total // 2 - 1)
@@ -158,20 +168,24 @@
     use(total - 1, odd)
 
 
-def first_hint(own, peer, by_column, by_n, s, half):
+def first_hint(own, peer, by_column, by_n, s, count, half, width, lane):
     rows, depth = own.shape
-    width = min(1024, depth)
-    lane = min(512, width)
+    width = min(width, depth)
+    lane = min(lane, width)
     whole = pl.BlockSpec(memory_space=pltpu.VMEM)
     return pl.pallas_call(
         functools.partial(first_kernel, width, lane),
         grid=(1,),
-        out_shape=jax.ShapeDtypeStruct((half, 2 * rows), jnp.int32),
-        in_specs=[whole] * 3 + [pl.BlockSpec((None,) + by_n.shape[1:], lambda i: (s, 0, 0, 0))],
-        out_specs=whole,
-        scratch_shapes=[pltpu.VMEM((4 * half, width), jnp.bfloat16)] * 2,
+        out_shape=[jax.ShapeDtypeStruct((half, 2 * rows), jnp.int32)] * count,
+        in_specs=[whole] * 3
+        + [pl.BlockSpec((count,) + by_n.shape[1:], lambda i: (s // count, 0, 0, 0))],
+        out_specs=[whole] * count,
+        scratch_shapes=[pltpu.VMEM((4 * count * half, width), jnp.bfloat16)] * 2,
+        compiler_params=pltpu.CompilerParams(vmem_limit_bytes=VMEM_LIMIT),
         cost_estimate=pl.CostEstimate(
-            flops=64 * half * depth * rows, bytes_accessed=4 * depth * rows, transcendentals=0
+            flops=64 * count * half * depth * rows,
+            bytes_accessed=4 * depth * rows,
+            transcendentals=0,
         ),
         name="first_hint",
     )(own, peer, by_column, by_n)
@@ -189,92 +203,103 @@
             pl.BlockSpec(memory_space=pltpu.SMEM),
             pl.BlockSpec(memory_space=pltpu.VMEM),
         ],
+        compiler_params=pltpu.CompilerParams(vmem_limit_bytes=VMEM_LIMIT),
         name="row_tables",
     )(seeds, place)
 
 
-def matrix_kernel(first_ref, *refs):
+def matrix_kernel(block, first_ref, *refs):
     out_ref = refs[-1]
-    _, block, depth = out_ref.shape
-
-    def store(i, row, column, value):
-        out_ref[i, row : row + SUBLANES, column : column + value.shape[1]] = value
-
+    _, columns, depth = out_ref.shape
+    lane = min(512, depth)
     sub = lax.broadcasted_iota(jnp.int32, (SUBLANES, LANES), 0)
-    second = by_second(pl.program_id(0) * block + sub, SUBLANES)
-    make_limbs(first_ref, second, 0, depth, min(512, depth), block // SUBLANES, store)
-
-
-def second_matrix(by_row, t, depth, columns, after=None):
+
+    @pl.loop(0, columns // block)
+    def _(i):
+        start = pl.multiple_of(i * block, block)
+
+        def store(i, row, column, value):
+            out_ref[i, pl.ds(start + row, SUBLANES), column : column + lane] = value
+
+        second = by_second(start + sub, SUBLANES)
+        make_limbs(first_ref, second, 0, depth, lane, block // SUBLANES, store)
+
+
+def second_matrix(by_row, t, depth, columns, after=()):
     block = min(256, columns)
-    return pl.pallas_call(
-        matrix_kernel,
-        grid=(columns // block,),
+    whole = pl.BlockSpec(memory_space=pltpu.VMEM)
+    return pl.pallas_call(
+        functools.partial(matrix_kernel, block),
+        grid=(1,),
         out_shape=jax.ShapeDtypeStruct((4, columns, depth), jnp.bfloat16),
         in_specs=[pl.BlockSpec((8, depth), lambda i: (0, t))]
-        + ([] if after is None else [pl.BlockSpec(memory_space=pl.ANY)]),
-        out_specs=pl.BlockSpec((4, block, depth), lambda i: (0, i, 0)),
+        + [pl.BlockSpec(memory_space=pl.ANY)] * len(after),
+        out_specs=whole,
+        compiler_params=pltpu.CompilerParams(vmem_limit_bytes=VMEM_LIMIT),
         cost_estimate=pl.CostEstimate(
-            flops=400 * 20 * depth * columns,
+            flops=2000 * depth * columns,
             bytes_accessed=8 * depth * columns,
             transcendentals=0,
         ),
         name="second_matrix",
-    )(by_row, *([] if after is None else [after]))
-
-
-def second_kernel(count, hint_refs, matrix_ref, total_ref, out_ref, digits):
-    @pl.when(pl.program_id(0) == 0)
-    def _():
-        half, rows = hint_refs[0].shape[-2:]
-        hints = [ref[i] for ref in hint_refs for i in range(ref.shape[0])]
-        for s, hint in enumerate(hints):
-            for place in range(4):
-                byte = (lax.shift_right_logical(hint, jnp.int32(8 * place)) & 255) - 128
-                digits[place * half : (place + 1) * half, s * rows : (s + 1) * rows] = byte.astype(
-                    jnp.float32
-                ).astype(jnp.bfloat16)
-
-    half = out_ref.shape[1]
-    total = join(
-        [
-            lax.dot_general(digits[...], matrix_ref[i], NT, preferred_element_type=jnp.float32)
-            for i in range(4)
-        ]
-    )
-    for place in range(4):
-        term = total[place * half : (place + 1) * half]
-        out_ref[place] = term if total_ref is None else total_ref[place] + term
-
-
-def second_hint(hints, matrix, total=None):
-    half, rows = hints[0].shape[1:]
+    )(by_row, *after)
+
+
+def second_kernel(block, hint_ref, matrix_ref, total_ref, out_ref, digits, small_digits):
+    pieces, half, rows = hint_ref.shape
+    for s in range(pieces):
+        hint = hint_ref[s]
+        for place in range(4):
+            byte = (lax.shift_right_logical(hint, jnp.int32(8 * place)) & 255) - 128
+            byte = byte.astype(jnp.float32).astype(jnp.bfloat16)
+            at = (slice(place * half, (place + 1) * half), slice(s * rows, (s + 1) * rows))
+            digits[at] = byte
+            small_digits[at] = byte * jnp.bfloat16(1 / 256)
+
+    @pl.loop(0, matrix_ref.shape[1] // block)
+    def _(i):
+        at = pl.ds(pl.multiple_of(i * block, block), block)
+        total = join(
+            [
+                lax.dot_general(
+                    [digits, small_digits][limb % 2][...],
+                    matrix_ref[limb, at],
+                    NT,
+                    preferred_element_type=jnp.float32,
+                )
+                for limb in range(4)
+            ]
+        )
+        for place in range(4):
+            term = total[place * half : (place + 1) * half]
+            out_ref[place, :, at] = term if total_ref is None else total_ref[place, :, at] + term
+
+
+def second_hint(hint, matrix, total=None):
+    half = hint.shape[1]
     _, columns, depth = matrix.shape
     block = min(256, columns)
-    out_spec = pl.BlockSpec((4, half, block), lambda i: (0, 0, i))
-    count = len(hints)
+    whole = pl.BlockSpec(memory_space=pltpu.VMEM)
 
     def kernel(*refs):
-        previous = None if total is None else refs[count + 1]
-        second_kernel(count, refs[:count], refs[count], previous, refs[-2], refs[-1])
+        previous = None if total is None else refs[2]
+        second_kernel(block, *refs[:2], previous, *refs[-3:])
 
     return pl.pallas_call(
         kernel,
-        grid=(columns // block,),
         out_shape=jax.ShapeDtypeStruct((4, half, columns), jnp.int32),
-        in_specs=[pl.BlockSpec(hint.shape, lambda i: (0, 0, 0)) for hint in hints]
-        + [pl.BlockSpec((4, block, depth), lambda i: (0, i, 0))]
-        + ([] if total is None else [out_spec]),
-        out_specs=out_spec,
-        scratch_shapes=[pltpu.VMEM((4 * half, depth), jnp.bfloat16)],
-        input_output_aliases={} if total is None else {count + 1: 0},
+        in_specs=[whole] * (2 if total is None else 3),
+        out_specs=whole,
+        scratch_shapes=[pltpu.VMEM((4 * half, depth), jnp.bfloat16)] * 2,
+        input_output_aliases={} if total is None else {2: 0},
+        compiler_params=pltpu.CompilerParams(vmem_limit_bytes=VMEM_LIMIT),
         cost_estimate=pl.CostEstimate(
             flops=32 * half * depth * columns,
             bytes_accessed=8 * depth * columns + 32 * half * columns,
             transcendentals=0,
         ),
         name="second_hint",
-    )(*hints, matrix, *([] if total is None else [total]))
+    )(hint, matrix, *([] if total is None else [total]))
 
 
 def halves_kernel(_, value_ref, *refs):
@@ -298,6 +323,7 @@
         ),
         out_shape=jax.ShapeDtypeStruct((digits, 2, 2 * half, columns), jnp.float32),
         input_output_aliases={} if out is None else {2: 0},
+        compiler_params=pltpu.CompilerParams(vmem_limit_bytes=VMEM_LIMIT),
         name="write_halves",
     )(place, value, *([] if out is None else [out]))
 
@@ -329,20 +355,22 @@
     by_column, by_n = tables(where, matrix_seeds, depth, col_size, half)
 
     hints = [None] * col_size
-    for s in reversed(range(col_size)):
-        part = first_hint(ingest, peer, by_column, by_n, s, half)
-        hints[s] = shift_by(part, "col", s) if s else part
+    count = 2
+    for s in reversed(range(0, col_size, count)):
+        parts = first_hint(ingest, peer, by_column, by_n, s, count, half, 1024, 512)
+        for i, part in enumerate(parts):
+            hints[s + i] = shift_by(part, "col", s + i) if s + i else part
 
     place = jnp.stack(places).reshape(row_size // 2, 2, col_size, rows).transpose(0, 2, 1, 3)
     by_row = row_tables(place.reshape(1, -1), matrix_seeds)
 
-    cut = col_size // 2
-    late, early = jnp.stack(hints[:cut]), jnp.stack(hints[cut:])
+    stacked = jnp.stack(hints)
     total = None
     for t in range(row_size // 2):
-        matrix = second_matrix(by_row, t, 2 * col_size * rows, N, total if t >= 4 else None)
-        groups = [shift_by(late, "row", 2 * t), shift_by(early, "row", 2 * t)] if t else [late, early]
-        total = second_hint(groups, matrix, total)
+        after = [hints[0]] if t < 4 else [total]
+        matrix = second_matrix(by_row, t, 2 * col_size * rows, N, after)
+        hint = shift_by(stacked, "row", 2 * t) if t else stacked
+        total = second_hint(hint, matrix, total)
 
     other = shift_by(total, "row", 1)
     out = write_halves(total, core[None])

time: 108 us -> 70.3 us (0.65)
  Pallas kernels: 80.1 us -> 44 us
  waiting for transfers between devices: 1.17 us -> 8.81 us
  local copies, waits for them, and re-layouts: 7.04 us -> 3.13 us
  starting transfers between devices: 16.5 us -> 12.9 us
  other arithmetic: 2.34 us -> 0.98 us
    pallas_call x8, Pallas kernels: 41.5 us -> 21.8 us  [the longest x4 14 us: second_hint(): pl.pallas_call(kernel, out_shape=jax.ShapeDtypeStruct((4, half, columns),...]
    pallas_call x4 -> x2, Pallas kernels: 26.3 us -> 15 us  [first_hint(): pl.pallas_call(functools.partial(first_kernel, width, lane), grid=(1,), o...]
    ppermute x15 -> x12, waiting for transfers between devices: 1.17 us -> 8.81 us  [shift_by(): lax.ppermute(value, axis, [(i, i ^ offset) for i in range(lax.axis_size(a...]
    ppermute x15 -> x12, starting transfers between devices: 16.5 us -> 12.9 us  [shift_by(): lax.ppermute(value, axis, [(i, i ^ offset) for i in range(lax.axis_size(a...]
    pallas_call x2, Pallas kernels: 8.54 us -> 5.02 us  [write_halves(): pl.pallas_call(halves_kernel, grid_spec=pltpu.PrefetchScalarGridSpec(num_...]
    unnamed x20 -> x6, local copies, waits for them, and re-layouts: 5.85 us -> 2.53 us
  transfers between devices with their start and end apart: 15 -> 12, of which waited for: 3 -> 8; matrix products, arithmetic and copies ran while one was open for 2% -> 2% of each run, Pallas kernels for 58% -> 27%
where the time goes in v2:
time: 70.3 us; the launch traced here: 70 us
  Pallas kernels  44 us (63%)
  starting transfers between devices  12.9 us (18%)
  waiting for transfers between devices  8.81 us (13%)
  local copies, waits for them, and re-layouts  3.13 us (4%)
  other arithmetic  0.98 us (1%)
    pallas_call x2, Pallas kernels, first_hint(): pl.pallas_call(functools.partial(first_kernel, width, lane), grid=(1,), o...  15 us
    pallas_call x4, Pallas kernels, second_hint(): pl.pallas_call(kernel, out_shape=jax.ShapeDtypeStruct((4, half, columns),...  14 us
    ppermute x12, starting transfers between devices, shift_by(): lax.ppermute(value, axis, [(i, i ^ offset) for i in range(lax.axis_size(a...  12.9 us
    ppermute x12, waiting for transfers between devices, shift_by(): lax.ppermute(value, axis, [(i, i ^ offset) for i in range(lax.axis_size(a...  8.81 us
    pallas_call x4, Pallas kernels, second_matrix(): pl.pallas_call(functools.partial(matrix_kernel, block), grid=(1,), out_sh...  7.84 us
    pallas_call x2, Pallas kernels, write_halves(): pl.pallas_call(halves_kernel, grid_spec=pltpu.PrefetchScalarGridSpec(num_...  5.02 us
    unnamed x6, local copies, waits for them, and re-layouts  2.53 us
    pallas_call x1, Pallas kernels, tables(): pl.pallas_call(functools.partial(tables_kernel, parts, half), out_shape=[...  1.44 us
  transfers between devices with their start and end apart: 12, of which 8 were waited for; matrix products, arithmetic and copies ran while one was open for 2% of the time, Pallas kernels for 27%

profile of v2, /device:TPU:0, one launch (start us, length us, event | category | flops | bytes accessed | tf_op | source)
XLA Modules:
  0.0 70.0 jit_solution(6703398019563616894)
XLA Ops:
  0.0 0.5 collective-permute-start
  0.5 0.8 %select_reduce_fusion = s32[256]{0:T(256)S(1)} fusion(s32[256]{0:T(256)} %bitcast.17), kind=kLoop, calls=%fused_computation.1 | loop fusion | flops 196352 | bytes 2048 | tf_op jit(solution)/shard_map/reduce_sum | solution.py:347
  1.5 1.5 %collective-permute-done.5 = s32[256]{0:T(256)S(1)} collective-permute-done((s32[256]{0:T(256)S(1)}, s32[256]{0:T(256)S(1)}, u32[]{:S(2)}, u32[]{:S(2)}) %collective-permute-start.5) | collective-permute-done | bytes 1056 | tf_op jit(solution)/shard_map/ppermute | solution.py:332
  3.0 3.8 %collective-permute-start.8 = (s32[2,256]{1,0:T(2,128)S(1)}, s32[2,256]{1,0:T(2,128)S(1)}, u32[]{:S(2)}, u32[]{:S(2)}) collective-permute-start(s32[2,256]{1,0:T(2,128)S(1)} %pad_add_fusion.1), channel_id=1, source_target_pairs={{0,24},{4,28},{8,16},{12,20},{16,8},{20,12},{24,0},{28,4},{1,25},{... | collective-permute-start | bytes 6152 | tf_op jit(solution)/shard_map/ppermute | solution.py:332
  6.8 0.5 collective-permute-start.7
  7.6 0.7 copy-done
  8.3 1.4 %tables.1 = (s32[8,8192]{1,0:T(8,128)S(1)}, s32[4,3,16,128]{3,2,1,0:T(8,128)S(1)}) custom-call(s32[2]{0:T(128)S(1)} %pad_add_fusion.3.where_ref, s32[2]{0:T(128)S(1)} %copy-done), custom_call_target="tpu_custom_call" | custom-call | tf_op jit(solution)/shard_map/tables/pallas_call | solution.py:87
  9.9 0.5 collective-permute-done.7
  11.1 0.7 copy-done.1
  11.7 0.8 %row_tables.1.first_ref = s32[8,2048]{1,0:T(8,128)S(1)} custom-call(s32[2]{0:T(128)S(1)} %copy-done.1, s32[1,2048]{1,0:T(1,128)S(1)} %reshape.16.place_ref), custom_call_target="tpu_custom_call" | custom-call | tf_op jit(solution)/shard_map/row_tables/pallas_call | solution.py:199
  12.5 1.2 %copy-done.2 = bf16[64,8192]{1,0:T(8,128)(2,1)S(1)} copy-done((bf16[64,8192]{1,0:T(8,128)(2,1)S(1)}, bf16[64,8192]{1,0:T(8,128)(2,1)}, u32[]{:S(2)}) %copy-start.2) | copy-done | bytes 1048600
  13.8 7.6 %first_hint.2 = (s32[128,128]{1,0:T(8,128)S(1)}, s32[128,128]{1,0:T(8,128)S(1)}) custom-call(bf16[64,8192]{1,0:T(8,128)(2,1)S(1)} %copy-done.2, bf16[64,8192]{1,0:T(8,128)(2,1)S(1)} %collective-permute-done.peer_ref, s32[8,8192]{1,0:T(8,128)S(1)} %get-tuple-element.11.first_ref, s32[4,3,16,128]{3,2,1,0:T(8,128)S(1)} %get-tuple-element.12.second_ref), custom_call_target="tpu_custom_call" | custom-call | flops 8589934592 | bytes 2097152 | tf_op jit(solution)/shard_map/first_hint/pallas_call | solution.py:176
  21.4 2.0 %second_matrix.7.refs_1_ = bf16[4,1024,512]{2,1,0:T(8,128)(2,1)S(1)} custom-call(s32[8,2048]{1,0:T(8,128)S(1)} %row_tables.1.first_ref, s32[128,128]{1,0:T(8,128)S(1)} %get-tuple-element.13.refs_0_), custom_call_target="tpu_custom_call" | custom-call | flops 1048576000 | bytes 4194304 | tf_op jit(solution)/shard_map/second_matrix/pallas_call | solution.py:231
  23.3 2.0 %second_matrix.6.refs_1_ = bf16[4,1024,512]{2,1,0:T(8,128)(2,1)S(1)} custom-call(s32[8,2048]{1,0:T(8,128)S(1)} %row_tables.1.first_ref, s32[128,128]{1,0:T(8,128)S(1)} %get-tuple-element.13.refs_0_), custom_call_target="tpu_custom_call" | custom-call | flops 1048576000 | bytes 4194304 | tf_op jit(solution)/shard_map/second_matrix/pallas_call | solution.py:231
  25.3 7.4 %first_hint.3 = (s32[128,128]{1,0:T(8,128)S(1)}, s32[128,128]{1,0:T(8,128)S(1)}) custom-call(bf16[64,8192]{1,0:T(8,128)(2,1)S(1)} %copy-done.2, bf16[64,8192]{1,0:T(8,128)(2,1)S(1)} %collective-permute-done.peer_ref, s32[8,8192]{1,0:T(8,128)S(1)} %get-tuple-element.11.first_ref, s32[4,3,16,128]{3,2,1,0:T(8,128)S(1)} %get-tuple-element.12.second_ref), custom_call_target="tpu_custom_call" | custom-call | flops 8589934592 | bytes 2097152 | tf_op jit(solution)/shard_map/first_hint/pallas_call | solution.py:176
  32.7 2.6 %collective-permute-start.2 = (s32[128,128]{1,0:T(8,128)S(1)}, s32[128,128]{1,0:T(8,128)S(1)}, u32[]{:S(2)}, u32[]{:S(2)}) collective-permute-start(s32[128,128]{1,0:T(8,128)S(1)} %get-tuple-element.15), channel_id=1, source_target_pairs={{0,2},{1,3},{2,0},{3,1},{4,6},{5,7},{6,4},{7,5},{8,10},{9,11},{10,... | collective-permute-start | bytes 196616 | tf_op jit(solution)/shard_map/ppermute | solution.py:332
  35.3 1.4 %collective-permute-start.3 = (s32[128,128]{1,0:T(8,128)S(1)}, s32[128,128]{1,0:T(8,128)S(1)}, u32[]{:S(2)}, u32[]{:S(2)}) collective-permute-start(s32[128,128]{1,0:T(8,128)S(1)} %get-tuple-element.16), channel_id=1, source_target_pairs={{0,3},{1,2},{2,1},{3,0},{4,7},{5,6},{6,5},{7,4},{8,11},{9,10},{10,... | collective-permute-start | bytes 196616 | tf_op jit(solution)/shard_map/ppermute | solution.py:332
  36.9 2.0 %second_matrix.5.refs_1_ = bf16[4,1024,512]{2,1,0:T(8,128)(2,1)S(1)} custom-call(s32[8,2048]{1,0:T(8,128)S(1)} %row_tables.1.first_ref, s32[128,128]{1,0:T(8,128)S(1)} %get-tuple-element.13.refs_0_), custom_call_target="tpu_custom_call" | custom-call | flops 1048576000 | bytes 4194304 | tf_op jit(solution)/shard_map/second_matrix/pallas_call | solution.py:231
  38.9 0.9 %collective-permute-done.2 = s32[128,128]{1,0:T(8,128)S(1)} collective-permute-done((s32[128,128]{1,0:T(8,128)S(1)}, s32[128,128]{1,0:T(8,128)S(1)}, u32[]{:S(2)}, u32[]{:S(2)}) %collective-permute-start.2) | collective-permute-done | bytes 65568 | tf_op jit(solution)/shard_map/ppermute | solution.py:332
  39.8 1.7 %collective-permute-done.3 = s32[128,128]{1,0:T(8,128)S(1)} collective-permute-done((s32[128,128]{1,0:T(8,128)S(1)}, s32[128,128]{1,0:T(8,128)S(1)}, u32[]{:S(2)}, u32[]{:S(2)}) %collective-permute-start.3) | collective-permute-done | bytes 65568 | tf_op jit(solution)/shard_map/ppermute | solution.py:332
  41.7 1.0 %collective-permute-start.10 = (s32[4,128,128]{2,1,0:T(8,128)S(1)}, s32[4,128,128]{2,1,0:T(8,128)S(1)}, u32[]{:S(2)}, u32[]{:S(2)}) collective-permute-start(s32[4,128,128]{2,1,0:T(8,128)S(1)} %pad_add_fusion.refs_0_), channel_id=1, source_target_pairs={{0,8},{4,12},{8,0},{12,4},{16,24},{20,28},{24,16},{28,20},{1,9},{5... | collective-permute-start | bytes 786440 | tf_op jit(solution)/shard_map/ppermute | solution.py:332
  42.7 2.0 %second_matrix.4.refs_1_ = bf16[4,1024,512]{2,1,0:T(8,128)(2,1)S(1)} custom-call(s32[8,2048]{1,0:T(8,128)S(1)} %row_tables.1.first_ref, s32[128,128]{1,0:T(8,128)S(1)} %get-tuple-element.13.refs_0_), custom_call_target="tpu_custom_call" | custom-call | flops 1048576000 | bytes 4194304 | tf_op jit(solution)/shard_map/second_matrix/pallas_call | solution.py:231
  44.7 1.6 %collective-permute-start.9 = (s32[4,128,128]{2,1,0:T(8,128)S(1)}, s32[4,128,128]{2,1,0:T(8,128)S(1)}, u32[]{:S(2)}, u32[]{:S(2)}) collective-permute-start(s32[4,128,128]{2,1,0:T(8,128)S(1)} %pad_add_fusion.refs_0_), channel_id=1, source_target_pairs={{0,16},{4,20},{8,24},{12,28},{16,0},{20,4},{24,8},{28,12},{1,17},{... | collective-permute-start | bytes 786440 | tf_op jit(solution)/shard_map/ppermute | solution.py:332
  46.3 1.0 %collective-permute-start.4 = (s32[4,128,128]{2,1,0:T(8,128)S(1)}, s32[4,128,128]{2,1,0:T(8,128)S(1)}, u32[]{:S(2)}, u32[]{:S(2)}) collective-permute-start(s32[4,128,128]{2,1,0:T(8,128)S(1)} %pad_add_fusion.refs_0_), channel_id=1, source_target_pairs={{0,24},{4,28},{8,16},{12,20},{16,8},{20,12},{24,0},{28,4},{1,25},{... | collective-permute-start | bytes 786440 | tf_op jit(solution)/shard_map/ppermute | solution.py:332
  47.3 3.4 %second_hint.4.refs_2_ = s32[4,128,1024]{2,1,0:T(8,128)S(1)} custom-call(s32[4,128,128]{2,1,0:T(8,128)S(1)} %pad_add_fusion.refs_0_, bf16[4,1024,512]{2,1,0:T(8,128)(2,1)S(1)} %second_matrix.7.refs_1_), custom_call_target="tpu_custom_call" | custom-call | flops 2147483648 | bytes 8388608 | tf_op jit(solution)/shard_map/second_hint/pallas_call | solution.py:288
  50.7 3.5 %second_hint.5.refs_2_ = s32[4,128,1024]{2,1,0:T(8,128)S(1)} custom-call(s32[4,128,128]{2,1,0:T(8,128)S(1)} %collective-permute-done.10.refs_0_, bf16[4,1024,512]{2,1,0:T(8,128)(2,1)S(1)} %second_matrix.6.refs_1_, s32[4,128,1024]{2,1,0:T(8,128)S(1)} %second_hint.4.refs_2_), custom_call_target="tpu_custom_call", output_to_operand_aliasing={{}: (2, {})} | custom-call | flops 2147483648 | bytes 8388608 | tf_op jit(solution)/shard_map/second_hint/pallas_call | solution.py:288
  54.2 2.0 %collective-permute-done.9.refs_0_ = s32[4,128,128]{2,1,0:T(8,128)S(1)} collective-permute-done((s32[4,128,128]{2,1,0:T(8,128)S(1)}, s32[4,128,128]{2,1,0:T(8,128)S(1)}, u32[]{:S(2)}, u32[]{:S(2)}) %collective-permute-start.9) | collective-permute-done | bytes 262176 | tf_op jit(solution)/shard_map/ppermute | solution.py:332
  56.2 3.5 %second_hint.6.refs_2_ = s32[4,128,1024]{2,1,0:T(8,128)S(1)} custom-call(s32[4,128,128]{2,1,0:T(8,128)S(1)} %collective-permute-done.9.refs_0_, bf16[4,1024,512]{2,1,0:T(8,128)(2,1)S(1)} %second_matrix.5.refs_1_, s32[4,128,1024]{2,1,0:T(8,128)S(1)} %second_hint.5.refs_2_), custom_call_target="tpu_custom_call", output_to_operand_aliasing={{}: (2, {})} | custom-call | flops 2147483648 | bytes 8388608 | tf_op jit(solution)/shard_map/second_hint/pallas_call | solution.py:288
  59.7 3.5 %second_hint.7.value_ref = s32[4,128,1024]{2,1,0:T(8,128)S(1)} custom-call(s32[4,128,128]{2,1,0:T(8,128)S(1)} %collective-permute-done.4.refs_0_, bf16[4,1024,512]{2,1,0:T(8,128)(2,1)S(1)} %second_matrix.4.refs_1_, s32[4,128,1024]{2,1,0:T(8,128)S(1)} %second_hint.6.refs_2_), custom_call_target="tpu_custom_call", output_to_operand_aliasing={{}: (2, {})} | custom-call | flops 2147483648 | bytes 8388608 | tf_op jit(solution)/shard_map/second_hint/pallas_call | solution.py:288
  63.3 2.5 %write_halves.2.refs_0_ = f32[4,2,256,1024]{3,2,1,0:T(8,128)} custom-call(s32[1]{0:T(128)} %bitcast._, s32[4,128,1024]{2,1,0:T(8,128)S(1)} %second_hint.7.value_ref), custom_call_target="tpu_custom_call" | custom-call | tf_op jit(solution)/shard_map/write_halves/pallas_call | solution.py:315
  65.9 1.6 %collective-permute-done.11.value_ref = s32[4,128,1024]{2,1,0:T(8,128)S(1)} collective-permute-done((s32[4,128,1024]{2,1,0:T(8,128)S(1)}, s32[4,128,1024]{2,1,0:T(8,128)S(1)}, u32[]{:S(2)}, u32[]{:S(2)}) %collective-permute-start.11) | collective-permute-done | bytes 2097184 | tf_op jit(solution)/shard_map/ppermute | solution.py:332
  67.5 2.5 %write_halves.3 = f32[4,2,256,1024]{3,2,1,0:T(8,128)} custom-call(s32[1]{0:T(128)S(6)} %sub.3._, s32[4,128,1024]{2,1,0:T(8,128)S(1)} %collective-permute-done.11.value_ref, f32[4,2,256,1024]{3,2,1,0:T(8,128)} %write_halves.2.refs_0_), custom_call_target="tpu_custom_call", output_to_operand_aliasing={{}: (2, {})} | custom-call | tf_op jit(solution)/shard_map/write_halves/pallas_call | solution.py:315
  (27 shorter events, 1.8 us)
Async XLA Ops:
  0.0 12.5 %collective-permute-start = (bf16[64,8192]{1,0:T(8,128)(2,1)}, bf16[64,8192]{1,0:T(8,128)(2,1)S(1)}, u32[]{:S(2)}, u32[]{:S(2)}) collective-permute-start(bf16[64,8192]{1,0:T(8,128)(2,1)} %own_ref.3), channel_id=1, source_target_pairs={{0,4},{4,0},{8,12},{12,8},{16,20},{20,16},{24,28},{28,24},{1,5},{5... | collective-permute-start | bytes 3145736 | tf_op jit(solution)/shard_map/ppermute | solution.py:332
  1.5 1.5 %collective-permute-start.5 = (s32[256]{0:T(256)S(1)}, s32[256]{0:T(256)S(1)}, u32[]{:S(2)}, u32[]{:S(2)}) collective-permute-start(s32[256]{0:T(256)S(1)} %pad_add_fusion.2), channel_id=1, source_target_pairs={{0,4},{4,0},{8,12},{12,8},{16,20},{20,16},{24,28},{28,24},{1,5},{5... | collective-permute-start | bytes 3080 | tf_op jit(solution)/shard_map/ppermute | solution.py:332
  3.0 6.8 %collective-permute-start.8 = (s32[2,256]{1,0:T(2,128)S(1)}, s32[2,256]{1,0:T(2,128)S(1)}, u32[]{:S(2)}, u32[]{:S(2)}) collective-permute-start(s32[2,256]{1,0:T(2,128)S(1)} %pad_add_fusion.1), channel_id=1, source_target_pairs={{0,24},{4,28},{8,16},{12,20},{16,8},{20,12},{24,0},{28,4},{1,25},{... | collective-permute-start | bytes 6152 | tf_op jit(solution)/shard_map/ppermute | solution.py:332
  6.8 3.6 %collective-permute-start.7 = (s32[2,256]{1,0:T(2,128)S(1)}, s32[2,256]{1,0:T(2,128)S(1)}, u32[]{:S(2)}, u32[]{:S(2)}) collective-permute-start(s32[2,256]{1,0:T(2,128)S(1)} %pad_add_fusion.1), channel_id=1, source_target_pairs={{0,16},{4,20},{8,24},{12,28},{16,0},{20,4},{24,8},{28,12},{1,17},{... | collective-permute-start | bytes 6152 | tf_op jit(solution)/shard_map/ppermute | solution.py:332
  7.3 3.6 %collective-permute-start.6 = (s32[2,256]{1,0:T(2,128)S(1)}, s32[2,256]{1,0:T(2,128)S(1)}, u32[]{:S(2)}, u32[]{:S(2)}) collective-permute-start(s32[2,256]{1,0:T(2,128)S(1)} %pad_add_fusion.1), channel_id=1, source_target_pairs={{0,8},{4,12},{8,0},{12,4},{16,24},{20,28},{24,16},{28,20},{1,9},{5... | collective-permute-start | bytes 6152 | tf_op jit(solution)/shard_map/ppermute | solution.py:332
  7.6 0.7 copy-start
  11.1 0.7 copy-start.1
  12.5 1.2 %copy-start.2 = (bf16[64,8192]{1,0:T(8,128)(2,1)S(1)}, bf16[64,8192]{1,0:T(8,128)(2,1)}, u32[]{:S(2)}) copy-start(bf16[64,8192]{1,0:T(8,128)(2,1)} %own_ref.3) | copy-start | bytes 3145732
  32.7 7.1 %collective-permute-start.2 = (s32[128,128]{1,0:T(8,128)S(1)}, s32[128,128]{1,0:T(8,128)S(1)}, u32[]{:S(2)}, u32[]{:S(2)}) collective-permute-start(s32[128,128]{1,0:T(8,128)S(1)} %get-tuple-element.15), channel_id=1, source_target_pairs={{0,2},{1,3},{2,0},{3,1},{4,6},{5,7},{6,4},{7,5},{8,10},{9,11},{10,... | collective-permute-start | bytes 196616 | tf_op jit(solution)/shard_map/ppermute | solution.py:332
  35.3 6.2 %collective-permute-start.3 = (s32[128,128]{1,0:T(8,128)S(1)}, s32[128,128]{1,0:T(8,128)S(1)}, u32[]{:S(2)}, u32[]{:S(2)}) collective-permute-start(s32[128,128]{1,0:T(8,128)S(1)} %get-tuple-element.16), channel_id=1, source_target_pairs={{0,3},{1,2},{2,1},{3,0},{4,7},{5,6},{6,5},{7,4},{8,11},{9,10},{10,... | collective-permute-start | bytes 196616 | tf_op jit(solution)/shard_map/ppermute | solution.py:332
  36.7 5.0 %collective-permute-start.1 = (s32[128,128]{1,0:T(8,128)S(1)}, s32[128,128]{1,0:T(8,128)S(1)}, u32[]{:S(2)}, u32[]{:S(2)}) collective-permute-start(s32[128,128]{1,0:T(8,128)S(1)} %get-tuple-element.14), channel_id=1, source_target_pairs={{0,1},{1,0},{2,3},{3,2},{4,5},{5,4},{6,7},{7,6},{8,9},{9,8},{10,11... | collective-permute-start | bytes 196616 | tf_op jit(solution)/shard_map/ppermute | solution.py:332
  41.7 9.0 %collective-permute-start.10 = (s32[4,128,128]{2,1,0:T(8,128)S(1)}, s32[4,128,128]{2,1,0:T(8,128)S(1)}, u32[]{:S(2)}, u32[]{:S(2)}) collective-permute-start(s32[4,128,128]{2,1,0:T(8,128)S(1)} %pad_add_fusion.refs_0_), channel_id=1, source_target_pairs={{0,8},{4,12},{8,0},{12,4},{16,24},{20,28},{24,16},{28,20},{1,9},{5... | collective-permute-start | bytes 786440 | tf_op jit(solution)/shard_map/ppermute | solution.py:332
  44.7 11.5 %collective-permute-start.9 = (s32[4,128,128]{2,1,0:T(8,128)S(1)}, s32[4,128,128]{2,1,0:T(8,128)S(1)}, u32[]{:S(2)}, u32[]{:S(2)}) collective-permute-start(s32[4,128,128]{2,1,0:T(8,128)S(1)} %pad_add_fusion.refs_0_), channel_id=1, source_target_pairs={{0,16},{4,20},{8,24},{12,28},{16,0},{20,4},{24,8},{28,12},{1,17},{... | collective-permute-start | bytes 786440 | tf_op jit(solution)/shard_map/ppermute | solution.py:332
  46.3 13.5 %collective-permute-start.4 = (s32[4,128,128]{2,1,0:T(8,128)S(1)}, s32[4,128,128]{2,1,0:T(8,128)S(1)}, u32[]{:S(2)}, u32[]{:S(2)}) collective-permute-start(s32[4,128,128]{2,1,0:T(8,128)S(1)} %pad_add_fusion.refs_0_), channel_id=1, source_target_pairs={{0,24},{4,28},{8,16},{12,20},{16,8},{20,12},{24,0},{28,4},{1,25},{... | collective-permute-start | bytes 786440 | tf_op jit(solution)/shard_map/ppermute | solution.py:332
  63.3 4.2 %collective-permute-start.11 = (s32[4,128,1024]{2,1,0:T(8,128)S(1)}, s32[4,128,1024]{2,1,0:T(8,128)S(1)}, u32[]{:S(2)}, u32[]{:S(2)}) collective-permute-start(s32[4,128,1024]{2,1,0:T(8,128)S(1)} %second_hint.7.value_ref), channel_id=1, source_target_pairs={{0,4},{4,0},{8,12},{12,8},{16,20},{20,16},{24,28},{28,24},{1,5},{5... | collective-permute-start | bytes 6291464 | tf_op jit(solution)/shard_map/ppermute | solution.py:332

commit v3 on v2

v3 whole, which is shorter than its diff:
```python
import functools

import jax
import jax.numpy as jnp
import numpy as np
from jax import lax
from jax.experimental import pallas as pl
from jax.experimental.pallas import tpu as pltpu
from jax.sharding import PartitionSpec as P


N = 1024

PRIME = 46337
HALF_PRIME = PRIME // 2
WHOLE = (1 << 32) // PRIME
PART = (1 << 32) / PRIME - WHOLE
SCALE = np.float32(PRIME / 2.0**32)
FINE = np.float32(1.5 * 2.0**23)
INVERSE = np.float32(1 / PRIME)
OFFSET = 32896 - HALF_PRIME
COARSE = np.float32(1.5 * 2.0**31 - 1.5 * 2.0**23 - OFFSET)
FINE_OFFSET = np.float32(1.5 * 2.0**23 + OFFSET)
SUBLANES = 16
VMEM_LIMIT = 16 << 20
LANES = 128
NT = (((1,), (1,)), ((), ()))


def residue(value):
    value = value - (value.astype(jnp.float32) * INVERSE).astype(jnp.int32) * PRIME
    value = value + jnp.where(value < 0, PRIME, 0)
    return value - jnp.where(value >= PRIME, PRIME, 0)


def centred(value):
    return value - jnp.where(value > HALF_PRIME, PRIME, 0)


def fixed(value):
    value = centred(value)
    return value * WHOLE + jnp.round(value.astype(jnp.float32) * np.float32(PART)).astype(jnp.int32)


def bend(step):
    value = 2 * (29989 * step % PRIME) ** 2 % PRIME
    value = value - PRIME if value > HALF_PRIME else value
    return np.int32(round(value * 2**32 / PRIME))


def by_first(index, seed, step):
    rows = 8
    shape = (rows, index.shape[1])
    row = lax.broadcasted_iota(jnp.int32, shape, 0)
    kind, second = row % 4, row >= 4
    start = jnp.where(second, 7919, 0) + seed
    a = residue(residue(residue(jnp.broadcast_to(index, shape)) * 40503) + start)
    a = residue(a * a)
    factor = 2 * (29989 * step % PRIME) % PRIME
    product = residue(a * jnp.where(kind == 1, a, factor))
    product = residue(product + jnp.where(kind == 1, 12345 - HALF_PRIME + PRIME, 0))
    return jnp.where(kind == 0, centred(a), fixed(product))


def by_second(index, step):
    shift = 29989 * step % PRIME
    b = residue(residue(index) * 29989)
    slope = residue(b * (2 * shift % PRIME))
    return [
        fixed(residue(2 * b)),
        fixed(residue(b * b)),
        fixed(residue(slope + shift * shift % PRIME)),
    ]


def tables_kernel(half, block_rows, seeds_ref, column_ref, n_ref, row_ref):
    row, col = lax.axis_index("row"), lax.axis_index("col")
    index = lax.broadcasted_iota(jnp.int32, (1, column_ref.shape[1]), 1)
    column_ref[...] = by_first(index, seeds_ref[0], SUBLANES)
    pair_rows = 2 * block_rows
    for t in range(row_ref.shape[0]):
        index = (row // 2 ^ t) * pair_rows + lax.broadcasted_iota(jnp.int32, (1, pair_rows), 1)
        row_ref[t] = by_first(index, seeds_ref[1], SUBLANES)
    sub = lax.broadcasted_iota(jnp.int32, (SUBLANES, LANES), 0)
    for s in range(n_ref.shape[0]):
        index = ((col ^ s) * 2 + row % 2) * half + sub
        for i, value in enumerate(by_second(index, SUBLANES)):
            n_ref[s, i] = value


def tables(seeds, depth, parts, half, chips, block_rows):
    return pl.pallas_call(
        functools.partial(tables_kernel, half, block_rows),
        out_shape=[
            jax.ShapeDtypeStruct((8, depth), jnp.int32),
            jax.ShapeDtypeStruct((parts, 3, SUBLANES, LANES), jnp.int32),
            jax.ShapeDtypeStruct((chips, 8, 2 * block_rows), jnp.int32),
        ],
        in_specs=[pl.BlockSpec(memory_space=pltpu.SMEM)],
        out_specs=[pl.BlockSpec(memory_space=pltpu.VMEM)] * 3,
        compiler_params=pltpu.CompilerParams(vmem_limit_bytes=VMEM_LIMIT),
        name="tables",
    )(seeds)


def limb_pair(value):
    rounded = value.astype(jnp.float32) * SCALE + FINE
    kept = (rounded + COARSE) - COARSE
    return (rounded - kept).astype(jnp.bfloat16), (kept - FINE_OFFSET).astype(jnp.bfloat16)


def join(products):
    low_p, high_p, low_q, high_q = (whole_number(product) for product in products)
    return low_p + (((low_q + (high_q << 8)) << 8) + high_p << 8)


def make_limbs(first_ref, second, start, width, lane, count, store):
    second = [jnp.concatenate([value] * (lane // LANES), axis=1) for value in second]
    for t in range(width // lane):
        at = pl.ds(pl.multiple_of(start + t * lane, lane), lane)
        for mix in range(2):
            a, square, slope = (first_ref[4 * mix + i : 4 * mix + i + 1, at] for i in range(3))
            value = a * second[0] + square + second[1]
            slope = slope + second[2]
            for k in range(count):
                low, high = limb_pair(value)
                store(2 * mix, k * SUBLANES, t * lane, low)
                store(2 * mix + 1, k * SUBLANES, t * lane, high)
                value = value + slope
                slope = slope + bend(SUBLANES)


def first_kernel(width, lane, own_ref, peer_ref, first_ref, second_ref, *refs):
    outs, even, odd = refs[:-2], refs[-2], refs[-1]
    half = outs[0].shape[0]
    total = own_ref.shape[1] // width
    small = jnp.bfloat16(1 / 256)

    def make(step, limbs):
        for s in range(len(outs)):

            def store(i, row, column, value):
                top = ((i % 2 * len(outs) + s) * 2 + i // 2) * half + row
                limbs[top : top + SUBLANES, column : column + lane] = value

            second = [second_ref[s, i] for i in range(3)]
            make_limbs(first_ref, second, step * width, width, lane, half // SUBLANES, store)

    def use(step, limbs):
        at = pl.ds(pl.multiple_of(step * width, width), width)
        records = jnp.concatenate([own_ref[:, at], peer_ref[:, at]], axis=0)
        middle = limbs.shape[0] // 2
        low = lax.dot_general(limbs[:middle], records, NT, preferred_element_type=jnp.float32)
        high = lax.dot_general(
            limbs[middle:], records * small, NT, preferred_element_type=jnp.float32
        )
        for s, out_ref in enumerate(outs):
            p, q = (slice((2 * s + i) * half, (2 * s + i + 1) * half) for i in range(2))
            out_ref[...] += join([low[p], high[p], low[q], high[q]])

    for out_ref in outs:
        out_ref[...] = jnp.zeros_like(out_ref)
    make(0, even)

    @pl.loop(0, total // 2 - 1)
    def _(i):
        use(2 * i, even)
        make(2 * i + 1, odd)
        use(2 * i + 1, odd)
        make(2 * i + 2, even)

    use(total - 2, even)
    make(total - 1, odd)
    use(total - 1, odd)


def first_hint(own, peer, by_column, by_n, s, count, half, width, lane):
    rows, depth = own.shape
    width = min(width, depth)
    lane = min(lane, width)
    whole = pl.BlockSpec(memory_space=pltpu.VMEM)
    return pl.pallas_call(
        functools.partial(first_kernel, width, lane),
        grid=(1,),
        out_shape=[jax.ShapeDtypeStruct((half, 2 * rows), jnp.int32)] * count,
        in_specs=[whole] * 3
        + [pl.BlockSpec((count,) + by_n.shape[1:], lambda i: (s // count, 0, 0, 0))],
        out_specs=[whole] * count,
        scratch_shapes=[pltpu.VMEM((4 * count * half, width), jnp.bfloat16)] * 2,
        compiler_params=pltpu.CompilerParams(vmem_limit_bytes=VMEM_LIMIT),
        cost_estimate=pl.CostEstimate(
            flops=64 * count * half * depth * rows,
            bytes_accessed=4 * depth * rows,
            transcendentals=0,
        ),
        name="first_hint",
    )(own, peer, by_column, by_n)


def byte_digits(hint, place):
    byte = (lax.shift_right_logical(hint, jnp.int32(8 * place)) & 255) - 128
    return byte.astype(jnp.float32).astype(jnp.bfloat16)


def whole_number(value):
    return jnp.round(value).astype(jnp.int32)


def sort_kernel(pieces, *refs):
    hints, (own_ref, peer_ref, out_ref, digits, select) = refs[:pieces], refs[pieces:]
    core, col = lax.axis_index("row") % 2, lax.axis_index("col")
    half, rows = hints[0].shape
    block_rows = own_ref.shape[1]
    slice_rows = rows // 2
    for s, hint_ref in enumerate(hints):
        hint = hint_ref[...]
        for place in range(4):
            at = (slice(place * half, (place + 1) * half), slice(s * rows, (s + 1) * rows))
            digits[at] = byte_digits(hint, place)
    orders = [own_ref[...], peer_ref[...] + block_rows]
    swapped = core == 1
    target = jnp.concatenate(
        [
            jnp.where(swapped, orders[1], orders[0]),
            jnp.where(swapped, orders[0], orders[1]),
        ],
        axis=1,
    )
    for s in range(pieces):
        for e in range(2):
            start = e * block_rows + (col ^ s) * slice_rows
            row = start + lax.broadcasted_iota(jnp.int32, (slice_rows, 2 * block_rows), 0)
            top = s * rows + e * slice_rows
            select[top : top + slice_rows, :] = jnp.where(row == target, 1.0, 0.0).astype(
                jnp.bfloat16
            )
    hint = None
    for place in range(4):
        moved = jnp.dot(
            digits[place * half : (place + 1) * half],
            select[...],
            preferred_element_type=jnp.float32,
        )
        term = (whole_number(moved) + 128) << (8 * place)
        hint = term if hint is None else hint + term
    out_ref[...] = hint


def sort_rows(hints, own_order, peer_order):
    half, _ = hints[0].shape
    total = 2 * own_order.shape[1]
    whole = pl.BlockSpec(memory_space=pltpu.VMEM)
    return pl.pallas_call(
        functools.partial(sort_kernel, len(hints)),
        out_shape=jax.ShapeDtypeStruct((half, total), jnp.int32),
        in_specs=[whole] * (len(hints) + 2),
        out_specs=whole,
        scratch_shapes=[
            pltpu.VMEM((4 * half, total), jnp.bfloat16),
            pltpu.VMEM((total, total), jnp.bfloat16),
        ],
        compiler_params=pltpu.CompilerParams(vmem_limit_bytes=VMEM_LIMIT),
        name="sort_rows",
    )(*hints, own_order, peer_order)


def matrix_kernel(block, first_ref, *refs):
    out_ref = refs[-1]
    count, _, depth = first_ref.shape
    columns = out_ref.shape[1]
    lane = min(512, depth)
    sub = lax.broadcasted_iota(jnp.int32, (SUBLANES, LANES), 0)

    @pl.loop(0, columns // block)
    def _(i):
        start = pl.multiple_of(i * block, block)
        second = by_second(start + sub, SUBLANES)
        for t in range(count):

            def store(i, row, column, value):
                at = slice(t * depth + column, t * depth + column + lane)
                out_ref[i, pl.ds(start + row, SUBLANES), at] = value

            make_limbs(first_ref.at[t], second, 0, depth, lane, block // SUBLANES, store)


def second_matrix(by_row, group, count, columns, after=()):
    _, quantities, depth = by_row.shape
    block = min(128, columns)
    whole = pl.BlockSpec(memory_space=pltpu.VMEM)
    return pl.pallas_call(
        functools.partial(matrix_kernel, block),
        grid=(1,),
        out_shape=jax.ShapeDtypeStruct((4, columns, count * depth), jnp.bfloat16),
        in_specs=[pl.BlockSpec((count, quantities, depth), lambda i: (group, 0, 0))]
        + [pl.BlockSpec(memory_space=pl.ANY)] * len(after),
        out_specs=whole,
        compiler_params=pltpu.CompilerParams(vmem_limit_bytes=VMEM_LIMIT),
        cost_estimate=pl.CostEstimate(
            flops=2000 * count * depth * columns,
            bytes_accessed=8 * count * depth * columns,
            transcendentals=0,
        ),
        name="second_matrix",
    )(by_row, *after)


def second_kernel(block, places, hints, matrix_ref, totals, outs, digits, small_digits):
    half, rows = hints[0].shape
    for t, hint_ref in enumerate(hints):
        hint = hint_ref[...]
        for i, place in enumerate(places):
            byte = byte_digits(hint, place)
            at = (slice(i * half, (i + 1) * half), slice(t * rows, (t + 1) * rows))
            digits[at] = byte
            small_digits[at] = byte * jnp.bfloat16(1 / 256)

    per_out = len(places) // len(outs)
    for start in range(0, matrix_ref.shape[1], block):
        at = slice(start, start + block)
        total = join(
            [
                lax.dot_general(
                    [digits, small_digits][limb % 2][...],
                    matrix_ref[limb, at],
                    NT,
                    preferred_element_type=jnp.float32,
                )
                for limb in range(4)
            ]
        )
        for i in range(len(places)):
            term = total[i * half : (i + 1) * half]
            k, j = i // per_out, i % per_out
            outs[k][j, :, at] = totals[k][j, :, at] + term if totals else term


def second_hint(hints, matrix, places, count, totals=()):
    half = hints[0].shape[0]
    _, columns, depth = matrix.shape
    block = min(256, columns)
    whole = pl.BlockSpec(memory_space=pltpu.VMEM)
    inputs = len(hints) + 1

    def kernel(*refs):
        outs = refs[inputs + len(totals) : -2]
        previous = refs[inputs : inputs + len(totals)]
        second_kernel(block, places, refs[: inputs - 1], refs[inputs - 1], previous, outs, *refs[-2:])

    shape = jax.ShapeDtypeStruct((len(places) // count, half, columns), jnp.int32)
    return pl.pallas_call(
        kernel,
        out_shape=[shape] * count,
        in_specs=[whole] * (inputs + len(totals)),
        out_specs=[whole] * count,
        scratch_shapes=[pltpu.VMEM((len(places) * half, depth), jnp.bfloat16)] * 2,
        input_output_aliases={inputs + i: i for i in range(len(totals))},
        compiler_params=pltpu.CompilerParams(vmem_limit_bytes=VMEM_LIMIT),
        cost_estimate=pl.CostEstimate(
            flops=8 * len(places) * half * depth * columns,
            bytes_accessed=8 * depth * columns + 8 * len(places) * half * columns,
            transcendentals=0,
        ),
        name="second_hint",
    )(*hints, matrix, *totals)


def halves_kernel(first, flip, value_ref, *refs):
    out_ref, low, high, sems = refs[-4:]
    digits, half, _ = value_ref.shape
    core = lax.axis_index("row") % 2
    start = pl.multiple_of((1 - core if flip else core) * half, half)
    rows = low.shape[2]
    scale = np.float32(1 / 65536)
    copies = []
    for i in range(digits):
        for j in range(half // rows):
            value = value_ref[i, j * rows : (j + 1) * rows]
            low[i, j] = (value & 65535).astype(jnp.float32) * scale
            high[i, j] = lax.shift_right_logical(value, jnp.int32(16)).astype(jnp.float32) * scale
            for k, source in enumerate((low, high)):
                target = out_ref.at[first + i, k, pl.ds(start + j * rows, rows)]
                copies.append(pltpu.make_async_copy(source.at[i, j], target, sems.at[i, j, k]))
                copies[-1].start()
    for copy in copies:
        copy.wait()


def write_halves(value, flip, first, out=None):
    digits, half, columns = value.shape
    rows = max(half // 2, 8)
    cuts = half // rows
    anywhere = pl.BlockSpec(memory_space=pl.ANY)
    return pl.pallas_call(
        functools.partial(halves_kernel, first, flip),
        in_specs=[pl.BlockSpec(memory_space=pltpu.VMEM)] + [anywhere] * (out is not None),
        out_specs=anywhere,
        out_shape=jax.ShapeDtypeStruct((4, 2, 2 * half, columns), jnp.float32),
        scratch_shapes=[pltpu.VMEM((digits, cuts, rows, columns), jnp.float32)] * 2
        + [pltpu.SemaphoreType.DMA((digits, cuts, 2))],
        input_output_aliases={} if out is None else {1: 0},
        compiler_params=pltpu.CompilerParams(vmem_limit_bytes=VMEM_LIMIT),
        name="write_halves",
    )(value, *([] if out is None else [out]))


def shift_by(value, axis, offset):
    return lax.ppermute(value, axis, [(i, i ^ offset) for i in range(lax.axis_size(axis))])


def on_device(ingest, row_order, matrix_seeds):
    row_size, col_size = lax.axis_size("row"), lax.axis_size("col")
    rows, depth = ingest.shape
    half = N // col_size // 2
    chips = row_size // 2
    pair_rows = 2 * col_size * rows

    peer = shift_by(ingest, "row", 1)
    peer_order = shift_by(row_order, "row", 1)
    by_column, by_n, by_row = tables(
        matrix_seeds, depth, col_size, half, chips, row_order.shape[1]
    )

    hints = [None] * col_size
    count = 2
    for s in reversed(range(0, col_size, count)):
        parts = first_hint(ingest, peer, by_column, by_n, s, count, half, 1024, 512)
        for i, part in enumerate(parts):
            hints[s + i] = shift_by(part, "col", s + i) if s + i else part
    hint = sort_rows(hints, row_order, peer_order)
    sources = [hint]
    for t in range(1, chips):
        sources.append(shift_by(hint, "row", 2 * t))

    count = max(1, min(chips, 1024 // pair_rows))
    totals = ()
    for group in range(chips // count):
        after = [] if group < 2 else [totals[0]]
        matrix = second_matrix(by_row, group, count, N, after)
        some = sources[group * count : (group + 1) * count]
        if group < chips // count - 1:
            totals = second_hint(some, matrix, (0, 1, 2, 3), 2, totals)
        else:
            totals = [
                second_hint(some, matrix, (2 * i, 2 * i + 1), 1, totals[i : i + 1])[0]
                for i in range(2)
            ]

    others = [shift_by(total, "row", 1) for total in totals]
    out = None
    for flip, values in enumerate((totals, others)):
        for i, value in enumerate(values):
            out = write_halves(value, flip, 2 * i, out)
    return out


def solution(mesh):
    in_specs = (P(("row", "col"), None), P("row", None), P())
    out_specs = P(None, None, "col", None)
    return jax.shard_map(
        on_device, mesh=mesh, in_specs=in_specs, out_specs=out_specs, check_vma=False
    )
```

time: 70.3 us -> 64.1 us (0.912)
  Pallas kernels: 44 us -> 40.9 us
  starting transfers between devices: 12.9 us -> 10.4 us
  waiting for transfers between devices: 8.81 us -> 10.5 us
  local copies, waits for them, and re-layouts: 3.13 us -> 1.88 us
  other arithmetic: 0.98 us -> 0 us
    pallas_call x8 -> x9, Pallas kernels: 21.2 us -> 18.2 us  [the longest x3 10.4 us: second_hint(): pl.pallas_call(kernel, out_shape=[shape] * count, in_specs=[whole] * (inp...]
    ppermute x12 -> x10, starting transfers between devices: 12.9 us -> 10.4 us  [shift_by(): lax.ppermute(value, axis, [(i, i ^ offset) for i in range(lax.axis_size(a...]
    ppermute x12 -> x10, waiting for transfers between devices: 8.81 us -> 10.5 us  [shift_by(): lax.ppermute(value, axis, [(i, i ^ offset) for i in range(lax.axis_size(a...]
    reduce_sum x1 -> x0, other arithmetic: 0.79 us -> none  [on_device(): jnp.sum(jnp.where(order[None, :] == r_index, k_index, 0), axis=1)]
    pallas_call x4 -> x2, Pallas kernels: 7.84 us -> 8.04 us  [second_matrix(): pl.pallas_call(functools.partial(matrix_kernel, block), grid=(1,), out_sh...]
  transfers between devices with their start and end apart: 12 -> 10, of which waited for: 8 -> 5; matrix products, arithmetic and copies ran while one was open for 2% -> 0% of each run, Pallas kernels for 27% -> 45%
where the time goes in v3:
time: 64.1 us; the launch traced here: 63.9 us
  Pallas kernels  40.9 us (64%)
  waiting for transfers between devices  10.5 us (16%)
  starting transfers between devices  10.4 us (16%)
  local copies, waits for them, and re-layouts  1.88 us (3%)
    pallas_call x2, Pallas kernels, first_hint(): pl.pallas_call(functools.partial(first_kernel, width, lane), grid=(1,), o...  14.7 us
    ppermute x10, waiting for transfers between devices, shift_by(): lax.ppermute(value, axis, [(i, i ^ offset) for i in range(lax.axis_size(a...  10.5 us
    ppermute x10, starting transfers between devices, shift_by(): lax.ppermute(value, axis, [(i, i ^ offset) for i in range(lax.axis_size(a...  10.4 us
    pallas_call x3, Pallas kernels, second_hint(): pl.pallas_call(kernel, out_shape=[shape] * count, in_specs=[whole] * (inp...  10.4 us
    pallas_call x2, Pallas kernels, second_matrix(): pl.pallas_call(functools.partial(matrix_kernel, block), grid=(1,), out_sh...  8.04 us
    pallas_call x4, Pallas kernels, write_halves(): pl.pallas_call(functools.partial(halves_kernel, first, flip), in_specs=[p...  5.62 us
    unnamed x6, local copies, waits for them, and re-layouts  1.88 us
    pallas_call x1, Pallas kernels, tables(): pl.pallas_call(functools.partial(tables_kernel, half, block_rows), out_sh...  1.63 us
  transfers between devices with their start and end apart: 10, of which 5 were waited for; matrix products, arithmetic and copies ran while one was open for 0% of the time, Pallas kernels for 45%

profile of v3, /device:TPU:0, one launch (start us, length us, event | category | flops | bytes accessed | tf_op | source)
XLA Modules:
  0.0 63.9 jit_solution(14152370177177718910)
XLA Ops:
  0.0 0.5 collective-permute-start
  0.5 0.7 %copy-done.2 = s32[2]{0:T(128)S(1)} copy-done((s32[2]{0:T(128)S(1)}, s32[2]{0:T(128)}, u32[]{:S(2)}) %copy-start.2) | copy-done | bytes 32
  1.1 1.6 %tables.1 = (s32[8,8192]{1,0:T(8,128)S(1)}, s32[4,3,16,128]{3,2,1,0:T(8,128)S(1)}, s32[4,8,512]{2,1,0:T(8,128)S(1)}) custom-call(s32[2]{0:T(128)S(1)} %copy-done.2), custom_call_target="tpu_custom_call" | custom-call | tf_op jit(solution)/shard_map/tables/pallas_call | solution.py:92
  2.8 0.2 collective-permute-done.peer_ref
  3.0 1.2 %copy-done.1 = bf16[64,8192]{1,0:T(8,128)(2,1)S(1)} copy-done((bf16[64,8192]{1,0:T(8,128)(2,1)S(1)}, bf16[64,8192]{1,0:T(8,128)(2,1)}, u32[]{:S(2)}) %copy-start.1) | copy-done | bytes 1048600
  4.2 7.4 %first_hint.3 = (s32[128,128]{1,0:T(8,128)S(1)}, s32[128,128]{1,0:T(8,128)S(1)}) custom-call(bf16[64,8192]{1,0:T(8,128)(2,1)S(1)} %copy-done.1, bf16[64,8192]{1,0:T(8,128)(2,1)S(1)} %collective-permute-done.peer_ref, s32[8,8192]{1,0:T(8,128)S(1)} %get-tuple-element.14.first_ref, s32[4,3,16,128]{3,2,1,0:T(8,128)S(1)} %get-tuple-element.15.second_ref), custom_call_target="tpu_custom_call" | custom-call | flops 8589934592 | bytes 2097152 | tf_op jit(solution)/shard_map/first_hint/pallas_call | solution.py:182
  11.6 4.0 %collective-permute-start.2 = (s32[128,128]{1,0:T(8,128)S(1)}, s32[128,128]{1,0:T(8,128)S(1)}, u32[]{:S(2)}, u32[]{:S(2)}) collective-permute-start(s32[128,128]{1,0:T(8,128)S(1)} %get-tuple-element.18), channel_id=1, source_target_pairs={{0,2},{1,3},{2,0},{3,1},{4,6},{5,7},{6,4},{7,5},{8,10},{9,11},{10,... | collective-permute-start | bytes 196616 | tf_op jit(solution)/shard_map/ppermute | solution.py:408
  15.6 1.3 %collective-permute-start.3 = (s32[128,128]{1,0:T(8,128)S(1)}, s32[128,128]{1,0:T(8,128)S(1)}, u32[]{:S(2)}, u32[]{:S(2)}) collective-permute-start(s32[128,128]{1,0:T(8,128)S(1)} %get-tuple-element.19), channel_id=1, source_target_pairs={{0,3},{1,2},{2,1},{3,0},{4,7},{5,6},{6,5},{7,4},{8,11},{9,10},{10,... | collective-permute-start | bytes 196616 | tf_op jit(solution)/shard_map/ppermute | solution.py:408
  16.9 7.4 %first_hint.2 = (s32[128,128]{1,0:T(8,128)S(1)}, s32[128,128]{1,0:T(8,128)S(1)}) custom-call(bf16[64,8192]{1,0:T(8,128)(2,1)S(1)} %copy-done.1, bf16[64,8192]{1,0:T(8,128)(2,1)S(1)} %collective-permute-done.peer_ref, s32[8,8192]{1,0:T(8,128)S(1)} %get-tuple-element.14.first_ref, s32[4,3,16,128]{3,2,1,0:T(8,128)S(1)} %get-tuple-element.15.second_ref), custom_call_target="tpu_custom_call" | custom-call | flops 8589934592 | bytes 2097152 | tf_op jit(solution)/shard_map/first_hint/pallas_call | solution.py:182
  24.3 0.3 collective-permute-start.1
  24.6 1.2 %collective-permute-done.4.refs_5_ = s32[1,256]{1,0:T(1,128)S(1)} collective-permute-done((s32[1,256]{1,0:T(1,128)S(1)}, s32[1,256]{1,0:T(1,128)S(1)}, u32[]{:S(2)}, u32[]{:S(2)}) %collective-permute-start.4) | collective-permute-done | bytes 1056 | tf_op jit(solution)/shard_map/ppermute | solution.py:408
  25.8 0.0 collective-permute-done.2.refs_2_
  25.8 0.0 collective-permute-done.3.refs_3_
  25.8 2.9 %collective-permute-done.1.refs_1_ = s32[128,128]{1,0:T(8,128)S(1)} collective-permute-done((s32[128,128]{1,0:T(8,128)S(1)}, s32[128,128]{1,0:T(8,128)S(1)}, u32[]{:S(2)}, u32[]{:S(2)}) %collective-permute-start.1) | collective-permute-done | bytes 65568 | tf_op jit(solution)/shard_map/ppermute | solution.py:408
  28.6 0.5 sort_rows.1.refs_0_
  29.2 1.6 %collective-permute-start.7 = (s32[128,512]{1,0:T(8,128)S(1)}, s32[128,512]{1,0:T(8,128)S(1)}, u32[]{:S(2)}, u32[]{:S(2)}) collective-permute-start(s32[128,512]{1,0:T(8,128)S(1)} %sort_rows.1.refs_0_), channel_id=1, source_target_pairs={{0,8},{4,12},{8,0},{12,4},{16,24},{20,28},{24,16},{28,20},{1,9},{5... | collective-permute-start | bytes 786440 | tf_op jit(solution)/shard_map/ppermute | solution.py:408
  30.7 3.9 %second_matrix.2.refs_2_ = bf16[4,1024,1024]{2,1,0:T(8,128)(2,1)S(1)} custom-call(s32[4,8,512]{2,1,0:T(8,128)S(1)} %get-tuple-element.20.first_ref), custom_call_target="tpu_custom_call" | custom-call | flops 2097152000 | bytes 8388608 | tf_op jit(solution)/shard_map/second_matrix/pallas_call | solution.py:291
  34.6 4.1 %second_matrix.3.refs_2_ = bf16[4,1024,1024]{2,1,0:T(8,128)(2,1)S(1)} custom-call(s32[4,8,512]{2,1,0:T(8,128)S(1)} %get-tuple-element.20.first_ref), custom_call_target="tpu_custom_call" | custom-call | flops 2097152000 | bytes 8388608 | tf_op jit(solution)/shard_map/second_matrix/pallas_call | solution.py:291
  38.8 1.6 %collective-permute-start.6 = (s32[128,512]{1,0:T(8,128)S(1)}, s32[128,512]{1,0:T(8,128)S(1)}, u32[]{:S(2)}, u32[]{:S(2)}) collective-permute-start(s32[128,512]{1,0:T(8,128)S(1)} %sort_rows.1.refs_0_), channel_id=1, source_target_pairs={{0,24},{4,28},{8,16},{12,20},{16,8},{20,12},{24,0},{28,4},{1,25},{... | collective-permute-start | bytes 786440 | tf_op jit(solution)/shard_map/ppermute | solution.py:408
  40.3 0.5 collective-permute-start.5
  40.8 0.0 collective-permute-done.7.refs_1_
  40.8 4.7 %second_hint.3 = (s32[2,128,1024]{2,1,0:T(8,128)S(1)}, s32[2,128,1024]{2,1,0:T(8,128)S(1)}) custom-call(s32[128,512]{1,0:T(8,128)S(1)} %sort_rows.1.refs_0_, s32[128,512]{1,0:T(8,128)S(1)} %collective-permute-done.7.refs_1_, bf16[4,1024,1024]{2,1,0:T(8,128)(2,1)S(1)} %second_matrix.3.refs_2_), custom_call_target="tpu_custom_call" | custom-call | flops 4294967296 | bytes 12582912 | tf_op jit(solution)/shard_map/second_hint/pallas_call | solution.py:351
  45.5 0.7 %collective-permute-done.6.refs_1_ = s32[128,512]{1,0:T(8,128)S(1)} collective-permute-done((s32[128,512]{1,0:T(8,128)S(1)}, s32[128,512]{1,0:T(8,128)S(1)}, u32[]{:S(2)}, u32[]{:S(2)}) %collective-permute-start.6) | collective-permute-done | bytes 262176 | tf_op jit(solution)/shard_map/ppermute | solution.py:408
  46.2 5.5 %collective-permute-done.5.refs_0_ = s32[128,512]{1,0:T(8,128)S(1)} collective-permute-done((s32[128,512]{1,0:T(8,128)S(1)}, s32[128,512]{1,0:T(8,128)S(1)}, u32[]{:S(2)}, u32[]{:S(2)}) %collective-permute-start.5) | collective-permute-done | bytes 262176 | tf_op jit(solution)/shard_map/ppermute | solution.py:408
  51.7 2.8 %second_hint.5.value_ref = s32[2,128,1024]{2,1,0:T(8,128)S(1)} custom-call(s32[128,512]{1,0:T(8,128)S(1)} %collective-permute-done.5.refs_0_, s32[128,512]{1,0:T(8,128)S(1)} %collective-permute-done.6.refs_1_, bf16[4,1024,1024]{2,1,0:T(8,128)(2,1)S(1)} %second_matrix.2.refs_2_, ...), custom_call_target="tpu_custom_call", output_to_operand_aliasing={{}: (3, {})} | custom-call | flops 2147483648 | bytes 10485760 | tf_op jit(solution)/shard_map/second_hint/pallas_call | solution.py:351
  54.6 0.1 collective-permute-start.9
  54.7 2.9 %second_hint.4.value_ref = s32[2,128,1024]{2,1,0:T(8,128)S(1)} custom-call(s32[128,512]{1,0:T(8,128)S(1)} %collective-permute-done.5.refs_0_, s32[128,512]{1,0:T(8,128)S(1)} %collective-permute-done.6.refs_1_, bf16[4,1024,1024]{2,1,0:T(8,128)(2,1)S(1)} %second_matrix.2.refs_2_, ...), custom_call_target="tpu_custom_call", output_to_operand_aliasing={{}: (3, {})} | custom-call | flops 2147483648 | bytes 10485760 | tf_op jit(solution)/shard_map/second_hint/pallas_call | solution.py:351
  57.6 0.5 collective-permute-start.8
  58.1 1.4 %write_halves.4.refs_0_ = f32[4,2,256,1024]{3,2,1,0:T(8,128)} custom-call(s32[2,128,1024]{2,1,0:T(8,128)S(1)} %second_hint.5.value_ref), custom_call_target="tpu_custom_call" | custom-call | tf_op jit(solution)/shard_map/write_halves/pallas_call | solution.py:394
  59.5 1.4 %write_halves.5.refs_0_ = f32[4,2,256,1024]{3,2,1,0:T(8,128)} custom-call(s32[2,128,1024]{2,1,0:T(8,128)S(1)} %second_hint.4.value_ref, f32[4,2,256,1024]{3,2,1,0:T(8,128)} %write_halves.4.refs_0_), custom_call_target="tpu_custom_call", output_to_operand_aliasing={{}: (1, {})} | custom-call | tf_op jit(solution)/shard_map/write_halves/pallas_call | solution.py:394
  60.9 1.4 %write_halves.6.refs_0_ = f32[4,2,256,1024]{3,2,1,0:T(8,128)} custom-call(s32[2,128,1024]{2,1,0:T(8,128)S(1)} %collective-permute-done.9.value_ref, f32[4,2,256,1024]{3,2,1,0:T(8,128)} %write_halves.5.refs_0_), custom_call_target="tpu_custom_call", output_to_operand_aliasing={{}: (1, {})} | custom-call | tf_op jit(solution)/shard_map/write_halves/pallas_call | solution.py:394
  62.4 1.4 %write_halves.7 = f32[4,2,256,1024]{3,2,1,0:T(8,128)} custom-call(s32[2,128,1024]{2,1,0:T(8,128)S(1)} %collective-permute-done.8.value_ref, f32[4,2,256,1024]{3,2,1,0:T(8,128)} %write_halves.6.refs_0_), custom_call_target="tpu_custom_call", output_to_operand_aliasing={{}: (1, {})} | custom-call | tf_op jit(solution)/shard_map/write_halves/pallas_call | solution.py:394
  (7 shorter events, 0.0 us)
Async XLA Ops:
  0.0 3.0 %collective-permute-start = (bf16[64,8192]{1,0:T(8,128)(2,1)}, bf16[64,8192]{1,0:T(8,128)(2,1)S(1)}, u32[]{:S(2)}, u32[]{:S(2)}) collective-permute-start(bf16[64,8192]{1,0:T(8,128)(2,1)} %own_ref.3), channel_id=1, source_target_pairs={{0,4},{4,0},{8,12},{12,8},{16,20},{20,16},{24,28},{28,24},{1,5},{5... | collective-permute-start | bytes 3145736 | tf_op jit(solution)/shard_map/ppermute | solution.py:408
  0.5 0.7 %copy-start.2 = (s32[2]{0:T(128)S(1)}, s32[2]{0:T(128)}, u32[]{:S(2)}) copy-start(s32[2]{0:T(128)} %seeds_ref.1) | copy-start | bytes 28
  3.0 1.2 %copy-start.1 = (bf16[64,8192]{1,0:T(8,128)(2,1)S(1)}, bf16[64,8192]{1,0:T(8,128)(2,1)}, u32[]{:S(2)}) copy-start(bf16[64,8192]{1,0:T(8,128)(2,1)} %own_ref.3) | copy-start | bytes 3145732
  11.6 14.2 %collective-permute-start.2 = (s32[128,128]{1,0:T(8,128)S(1)}, s32[128,128]{1,0:T(8,128)S(1)}, u32[]{:S(2)}, u32[]{:S(2)}) collective-permute-start(s32[128,128]{1,0:T(8,128)S(1)} %get-tuple-element.18), channel_id=1, source_target_pairs={{0,2},{1,3},{2,0},{3,1},{4,6},{5,7},{6,4},{7,5},{8,10},{9,11},{10,... | collective-permute-start | bytes 196616 | tf_op jit(solution)/shard_map/ppermute | solution.py:408
  15.6 9.0 %copy-start = (s32[1,256]{1,0:T(1,128)S(1)}, s32[1,256]{1,0:T(1,128)}, u32[]{:S(2)}) copy-start(s32[1,256]{1,0:T(1,128)} %refs_4_.1) | copy-start | bytes 3076
  15.6 10.2 %collective-permute-start.3 = (s32[128,128]{1,0:T(8,128)S(1)}, s32[128,128]{1,0:T(8,128)S(1)}, u32[]{:S(2)}, u32[]{:S(2)}) collective-permute-start(s32[128,128]{1,0:T(8,128)S(1)} %get-tuple-element.19), channel_id=1, source_target_pairs={{0,3},{1,2},{2,1},{3,0},{4,7},{5,6},{6,5},{7,4},{8,11},{9,10},{10,... | collective-permute-start | bytes 196616 | tf_op jit(solution)/shard_map/ppermute | solution.py:408
  24.3 4.3 %collective-permute-start.1 = (s32[128,128]{1,0:T(8,128)S(1)}, s32[128,128]{1,0:T(8,128)S(1)}, u32[]{:S(2)}, u32[]{:S(2)}) collective-permute-start(s32[128,128]{1,0:T(8,128)S(1)} %get-tuple-element.17), channel_id=1, source_target_pairs={{0,1},{1,0},{2,3},{3,2},{4,5},{5,4},{6,7},{7,6},{8,9},{9,8},{10,11... | collective-permute-start | bytes 196616 | tf_op jit(solution)/shard_map/ppermute | solution.py:408
  24.6 1.2 %collective-permute-start.4 = (s32[1,256]{1,0:T(1,128)S(1)}, s32[1,256]{1,0:T(1,128)S(1)}, u32[]{:S(2)}, u32[]{:S(2)}) collective-permute-start(s32[1,256]{1,0:T(1,128)S(1)} %copy-done), channel_id=1, source_target_pairs={{0,4},{4,0},{8,12},{12,8},{16,20},{20,16},{24,28},{28,24},{1,5},{5... | collective-permute-start | bytes 3080 | tf_op jit(solution)/shard_map/ppermute | solution.py:408
  29.2 11.7 %collective-permute-start.7 = (s32[128,512]{1,0:T(8,128)S(1)}, s32[128,512]{1,0:T(8,128)S(1)}, u32[]{:S(2)}, u32[]{:S(2)}) collective-permute-start(s32[128,512]{1,0:T(8,128)S(1)} %sort_rows.1.refs_0_), channel_id=1, source_target_pairs={{0,8},{4,12},{8,0},{12,4},{16,24},{20,28},{24,16},{28,20},{1,9},{5... | collective-permute-start | bytes 786440 | tf_op jit(solution)/shard_map/ppermute | solution.py:408
  38.8 7.5 %collective-permute-start.6 = (s32[128,512]{1,0:T(8,128)S(1)}, s32[128,512]{1,0:T(8,128)S(1)}, u32[]{:S(2)}, u32[]{:S(2)}) collective-permute-start(s32[128,512]{1,0:T(8,128)S(1)} %sort_rows.1.refs_0_), channel_id=1, source_target_pairs={{0,24},{4,28},{8,16},{12,20},{16,8},{20,12},{24,0},{28,4},{1,25},{... | collective-permute-start | bytes 786440 | tf_op jit(solution)/shard_map/ppermute | solution.py:408
  40.3 11.4 %collective-permute-start.5 = (s32[128,512]{1,0:T(8,128)S(1)}, s32[128,512]{1,0:T(8,128)S(1)}, u32[]{:S(2)}, u32[]{:S(2)}) collective-permute-start(s32[128,512]{1,0:T(8,128)S(1)} %sort_rows.1.refs_0_), channel_id=1, source_target_pairs={{0,16},{4,20},{8,24},{12,28},{16,0},{20,4},{24,8},{28,12},{1,17},{... | collective-permute-start | bytes 786440 | tf_op jit(solution)/shard_map/ppermute | solution.py:408
  54.6 6.3 %collective-permute-start.9 = (s32[2,128,1024]{2,1,0:T(8,128)S(1)}, s32[2,128,1024]{2,1,0:T(8,128)S(1)}, u32[]{:S(2)}, u32[]{:S(2)}) collective-permute-start(s32[2,128,1024]{2,1,0:T(8,128)S(1)} %second_hint.5.value_ref), channel_id=1, source_target_pairs={{0,4},{4,0},{8,12},{12,8},{16,20},{20,16},{24,28},{28,24},{1,5},{5... | collective-permute-start | bytes 3145736 | tf_op jit(solution)/shard_map/ppermute | solution.py:408
  57.6 4.8 %collective-permute-start.8 = (s32[2,128,1024]{2,1,0:T(8,128)S(1)}, s32[2,128,1024]{2,1,0:T(8,128)S(1)}, u32[]{:S(2)}, u32[]{:S(2)}) collective-permute-start(s32[2,128,1024]{2,1,0:T(8,128)S(1)} %second_hint.4.value_ref), channel_id=1, source_target_pairs={{0,4},{4,0},{8,12},{12,8},{16,20},{20,16},{24,28},{28,24},{1,5},{5... | collective-permute-start | bytes 3145736 | tf_op jit(solution)/shard_map/ppermute | solution.py:408

commit v4 on v3

--- a/solution.py
+++ b/solution.py
@@ -130,7 +130,7 @@
                 slope = slope + bend(SUBLANES)
 
 
-def first_kernel(width, lane, own_ref, peer_ref, first_ref, second_ref, *refs):
+def first_kernel(offset, width, lane, own_ref, peer_ref, first_ref, second_ref, *refs):
     outs, even, odd = refs[:-2], refs[-2], refs[-1]
     half = outs[0].shape[0]
     total = own_ref.shape[1] // width
@@ -143,7 +143,7 @@
                 top = ((i % 2 * len(outs) + s) * 2 + i // 2) * half + row
                 limbs[top : top + SUBLANES, column : column + lane] = value
 
-            second = [second_ref[s, i] for i in range(3)]
+            second = [second_ref[offset + s, i] for i in range(3)]
             make_limbs(first_ref, second, step * width, width, lane, half // SUBLANES, store)
 
     def use(step, limbs):
@@ -180,11 +180,9 @@
     lane = min(lane, width)
     whole = pl.BlockSpec(memory_space=pltpu.VMEM)
     return pl.pallas_call(
-        functools.partial(first_kernel, width, lane),
-        grid=(1,),
+        functools.partial(first_kernel, s, width, lane),
         out_shape=[jax.ShapeDtypeStruct((half, 2 * rows), jnp.int32)] * count,
-        in_specs=[whole] * 3
-        + [pl.BlockSpec((count,) + by_n.shape[1:], lambda i: (s // count, 0, 0, 0))],
+        in_specs=[whole] * 4,
         out_specs=[whole] * count,
         scratch_shapes=[pltpu.VMEM((4 * count * half, width), jnp.bfloat16)] * 2,
         compiler_params=pltpu.CompilerParams(vmem_limit_bytes=VMEM_LIMIT),
@@ -305,19 +303,24 @@
     )(by_row, *after)
 
 
-def second_kernel(block, places, hints, matrix_ref, totals, outs, digits, small_digits):
-    half, rows = hints[0].shape
-    for t, hint_ref in enumerate(hints):
-        hint = hint_ref[...]
-        for i, place in enumerate(places):
-            byte = byte_digits(hint, place)
-            at = (slice(i * half, (i + 1) * half), slice(t * rows, (t + 1) * rows))
-            digits[at] = byte
-            small_digits[at] = byte * jnp.bfloat16(1 / 256)
-
-    per_out = len(places) // len(outs)
-    for start in range(0, matrix_ref.shape[1], block):
-        at = slice(start, start + block)
+def second_kernel(block, first, count, has_total, has_next, *refs):
+    refs = list(refs)
+    hint_ref, matrix_ref = refs[:2]
+    total_ref = refs[2] if has_total else None
+    next_ref, next_matrix_ref = (refs[2 + has_total], refs[-3]) if has_next else (None, None)
+    out_ref, digits, small_digits = refs[-4 if has_next else -3], refs[-2], refs[-1]
+    half = hint_ref.shape[0]
+    depth = matrix_ref.shape[2]
+    hint = hint_ref[...]
+    for place in range(4):
+        byte = byte_digits(hint, place)
+        digits[place * half : (place + 1) * half] = byte
+        small_digits[place * half : (place + 1) * half] = byte * jnp.bfloat16(1 / 256)
+    sub = lax.broadcasted_iota(jnp.int32, (SUBLANES, LANES), 0)
+    lane = min(512, depth)
+
+    for start in range(0, count, block):
+        at = slice(first + start, first + start + block)
         total = join(
             [
                 lax.dot_general(
@@ -329,75 +332,73 @@
                 for limb in range(4)
             ]
         )
-        for i in range(len(places)):
-            term = total[i * half : (i + 1) * half]
-            k, j = i // per_out, i % per_out
-            outs[k][j, :, at] = totals[k][j, :, at] + term if totals else term
-
-
-def second_hint(hints, matrix, places, count, totals=()):
-    half = hints[0].shape[0]
-    _, columns, depth = matrix.shape
-    block = min(256, columns)
+        for place in range(4):
+            term = total[place * half : (place + 1) * half]
+            out = slice(start, start + block)
+            out_ref[place, :, out] = term if total_ref is None else total_ref[place, :, at] + term
+        if has_next:
+
+            def store(i, row, column, value, start=start):
+                top = start + row
+                next_matrix_ref[i, top : top + SUBLANES, column : column + lane] = value
+
+            second = by_second(start + sub, SUBLANES)
+            make_limbs(next_ref, second, 0, depth, lane, block // SUBLANES, store)
+
+
+def second_hint(hint, matrix, first, count, total=None, by_row=None, t=0):
+    half = hint.shape[0]
+    depth = matrix.shape[2]
+    has_total, has_next = total is not None, by_row is not None
     whole = pl.BlockSpec(memory_space=pltpu.VMEM)
-    inputs = len(hints) + 1
-
-    def kernel(*refs):
-        outs = refs[inputs + len(totals) : -2]
-        previous = refs[inputs : inputs + len(totals)]
-        second_kernel(block, places, refs[: inputs - 1], refs[inputs - 1], previous, outs, *refs[-2:])
-
-    shape = jax.ShapeDtypeStruct((len(places) // count, half, columns), jnp.int32)
-    return pl.pallas_call(
-        kernel,
-        out_shape=[shape] * count,
-        in_specs=[whole] * (inputs + len(totals)),
-        out_specs=[whole] * count,
-        scratch_shapes=[pltpu.VMEM((len(places) * half, depth), jnp.bfloat16)] * 2,
-        input_output_aliases={inputs + i: i for i in range(len(totals))},
+    row_spec = pl.BlockSpec((None,) + by_row.shape[1:], lambda i: (t, 0, 0)) if has_next else None
+    return pl.pallas_call(
+        functools.partial(second_kernel, min(256, count), first, count, has_total, has_next),
+        grid=(1,),
+        out_shape=[jax.ShapeDtypeStruct((4, half, count), jnp.int32)]
+        + [jax.ShapeDtypeStruct(matrix.shape, matrix.dtype)] * has_next,
+        in_specs=[whole] * (2 + has_total) + [row_spec] * has_next,
+        out_specs=[whole] * (1 + has_next),
+        scratch_shapes=[pltpu.VMEM((4 * half, depth), jnp.bfloat16)] * 2,
         compiler_params=pltpu.CompilerParams(vmem_limit_bytes=VMEM_LIMIT),
         cost_estimate=pl.CostEstimate(
-            flops=8 * len(places) * half * depth * columns,
-            bytes_accessed=8 * depth * columns + 8 * len(places) * half * columns,
+            flops=32 * half * depth * count,
+            bytes_accessed=8 * depth * count + 32 * half * count,
             transcendentals=0,
         ),
         name="second_hint",
-    )(*hints, matrix, *totals)
+    )(hint, matrix, *([total] if has_total else []), *([by_row] if has_next else []))
 
 
 def halves_kernel(first, flip, value_ref, *refs):
     out_ref, low, high, sems = refs[-4:]
-    digits, half, _ = value_ref.shape
+    digits, half, columns = value_ref.shape
     core = lax.axis_index("row") % 2
     start = pl.multiple_of((1 - core if flip else core) * half, half)
-    rows = low.shape[2]
     scale = np.float32(1 / 65536)
     copies = []
     for i in range(digits):
-        for j in range(half // rows):
-            value = value_ref[i, j * rows : (j + 1) * rows]
-            low[i, j] = (value & 65535).astype(jnp.float32) * scale
-            high[i, j] = lax.shift_right_logical(value, jnp.int32(16)).astype(jnp.float32) * scale
-            for k, source in enumerate((low, high)):
-                target = out_ref.at[first + i, k, pl.ds(start + j * rows, rows)]
-                copies.append(pltpu.make_async_copy(source.at[i, j], target, sems.at[i, j, k]))
-                copies[-1].start()
+        value = value_ref[i]
+        low[i] = (value & 65535).astype(jnp.float32) * scale
+        high[i] = lax.shift_right_logical(value, jnp.int32(16)).astype(jnp.float32) * scale
+        for k, source in enumerate((low, high)):
+            target = out_ref.at[i, k, pl.ds(start, half), pl.ds(first, columns)]
+            copies.append(pltpu.make_async_copy(source.at[i], target, sems.at[i, k]))
+            copies[-1].start()
     for copy in copies:
         copy.wait()
 
 
-def write_halves(value, flip, first, out=None):
-    digits, half, columns = value.shape
-    rows = max(half // 2, 8)
-    cuts = half // rows
+def write_halves(value, flip, first, columns, out=None):
+    digits, half, some = value.shape
     anywhere = pl.BlockSpec(memory_space=pl.ANY)
     return pl.pallas_call(
         functools.partial(halves_kernel, first, flip),
         in_specs=[pl.BlockSpec(memory_space=pltpu.VMEM)] + [anywhere] * (out is not None),
         out_specs=anywhere,
-        out_shape=jax.ShapeDtypeStruct((4, 2, 2 * half, columns), jnp.float32),
-        scratch_shapes=[pltpu.VMEM((digits, cuts, rows, columns), jnp.float32)] * 2
-        + [pltpu.SemaphoreType.DMA((digits, cuts, 2))],
+        out_shape=jax.ShapeDtypeStruct((digits, 2, 2 * half, columns), jnp.float32),
+        scratch_shapes=[pltpu.VMEM((digits, half, some), jnp.float32)] * 2
+        + [pltpu.SemaphoreType.DMA((digits, 2))],
         input_output_aliases={} if out is None else {1: 0},
         compiler_params=pltpu.CompilerParams(vmem_limit_bytes=VMEM_LIMIT),
         name="write_halves",
@@ -410,10 +411,9 @@
 
 def on_device(ingest, row_order, matrix_seeds):
     row_size, col_size = lax.axis_size("row"), lax.axis_size("col")
-    rows, depth = ingest.shape
+    _, depth = ingest.shape
     half = N // col_size // 2
     chips = row_size // 2
-    pair_rows = 2 * col_size * rows
 
     peer = shift_by(ingest, "row", 1)
     peer_order = shift_by(row_order, "row", 1)
@@ -422,8 +422,7 @@
     )
 
     hints = [None] * col_size
-    count = 2
-    for s in reversed(range(0, col_size, count)):
+    for s, count in ((1, col_size - 1), (0, 1)):
         parts = first_hint(ingest, peer, by_column, by_n, s, count, half, 1024, 512)
         for i, part in enumerate(parts):
             hints[s + i] = shift_by(part, "col", s + i) if s + i else part
@@ -432,25 +431,18 @@
     for t in range(1, chips):
         sources.append(shift_by(hint, "row", 2 * t))
 
-    count = max(1, min(chips, 1024 // pair_rows))
-    totals = ()
-    for group in range(chips // count):
-        after = [] if group < 2 else [totals[0]]
-        matrix = second_matrix(by_row, group, count, N, after)
-        some = sources[group * count : (group + 1) * count]
-        if group < chips // count - 1:
-            totals = second_hint(some, matrix, (0, 1, 2, 3), 2, totals)
-        else:
-            totals = [
-                second_hint(some, matrix, (2 * i, 2 * i + 1), 1, totals[i : i + 1])[0]
-                for i in range(2)
-            ]
-
-    others = [shift_by(total, "row", 1) for total in totals]
+    matrix = second_matrix(by_row, 0, 1, N)
+    total = None
+    for t in range(chips - 1):
+        total, matrix = second_hint(sources[t], matrix, 0, N, total, by_row, t + 1)
+    cut = N // 2
+    totals = [second_hint(sources[-1], matrix, i * cut, cut, total)[0] for i in range(2)]
+
+    others = [shift_by(value, "row", 1) for value in totals]
     out = None
     for flip, values in enumerate((totals, others)):
         for i, value in enumerate(values):
-            out = write_halves(value, flip, 2 * i, out)
+            out = write_halves(value, flip, i * cut, N, out)
     return out
 
 

time: 64.1 us -> 56.3 us (0.88)
  waiting for transfers between devices: 10.5 us -> 5.2 us
  Pallas kernels: 40.9 us -> 38.4 us
    pallas_call x2 -> x1, Pallas kernels: 8.04 us -> 2.34 us  [second_matrix(): pl.pallas_call(functools.partial(matrix_kernel, block), grid=(1,), out_sh...]
    ppermute x10, waiting for transfers between devices: 10.5 us -> 5.2 us  [shift_by(): lax.ppermute(value, axis, [(i, i ^ offset) for i in range(lax.axis_size(a...]
    pallas_call x5 -> x7, Pallas kernels: 25.1 us -> 28.3 us  [the longest x2 14.9 us: first_hint(): pl.pallas_call(functools.partial(first_kernel, s, width, lane), out_shape...]
  transfers between devices with their start and end apart: 10 -> 10, of which waited for: 5 -> 4; matrix products, arithmetic and copies ran while one was open for 0% -> 0% of each run, Pallas kernels for 45% -> 63%
where the time goes in v4:
time: 56.3 us; the launch traced here: 56.1 us
  Pallas kernels  38.4 us (68%)
  starting transfers between devices  10.4 us (18%)
  waiting for transfers between devices  5.2 us (9%)
  local copies, waits for them, and re-layouts  1.88 us (3%)
    pallas_call x2, Pallas kernels, first_hint(): pl.pallas_call(functools.partial(first_kernel, s, width, lane), out_shape...  14.9 us
    pallas_call x5, Pallas kernels, second_hint(): pl.pallas_call(functools.partial(second_kernel, min(256, count), first, c...  13.4 us
    ppermute x10, starting transfers between devices, shift_by(): lax.ppermute(value, axis, [(i, i ^ offset) for i in range(lax.axis_size(a...  10.4 us
    pallas_call x4, Pallas kernels, write_halves(): pl.pallas_call(functools.partial(halves_kernel, first, flip), in_specs=[p...  5.62 us
    ppermute x10, waiting for transfers between devices, shift_by(): lax.ppermute(value, axis, [(i, i ^ offset) for i in range(lax.axis_size(a...  5.2 us
    pallas_call x1, Pallas kernels, second_matrix(): pl.pallas_call(functools.partial(matrix_kernel, block), grid=(1,), out_sh...  2.34 us
    unnamed x6, local copies, waits for them, and re-layouts  1.88 us
    pallas_call x1, Pallas kernels, tables(): pl.pallas_call(functools.partial(tables_kernel, half, block_rows), out_sh...  1.63 us
  transfers between devices with their start and end apart: 10, of which 4 were waited for; matrix products, arithmetic and copies ran while one was open for 0% of the time, Pallas kernels for 63%

profile of v4, /device:TPU:0, one launch (start us, length us, event | category | flops | bytes accessed | tf_op | source)
XLA Modules:
  0.0 56.1 jit_solution(10338647011751180775)
XLA Ops:
  0.0 0.5 collective-permute-start
  0.5 0.0 collective-permute-start.4
  0.5 0.7 %copy-done.2 = s32[2]{0:T(128)S(1)} copy-done((s32[2]{0:T(128)S(1)}, s32[2]{0:T(128)}, u32[]{:S(2)}) %copy-start.2) | copy-done | bytes 32
  1.2 1.6 %tables.1 = (s32[8,8192]{1,0:T(8,128)S(1)}, s32[4,3,16,128]{3,2,1,0:T(8,128)S(1)}, s32[4,8,512]{2,1,0:T(8,128)S(1)}) custom-call(s32[2]{0:T(128)S(1)} %copy-done.2), custom_call_target="tpu_custom_call" | custom-call | tf_op jit(solution)/shard_map/tables/pallas_call | solution.py:92
  2.8 0.2 collective-permute-done.peer_ref
  3.0 1.2 %copy-done.1 = bf16[64,8192]{1,0:T(8,128)(2,1)S(1)} copy-done((bf16[64,8192]{1,0:T(8,128)(2,1)S(1)}, bf16[64,8192]{1,0:T(8,128)(2,1)}, u32[]{:S(2)}) %copy-start.1) | copy-done | bytes 1048600
  4.2 10.9 %first_hint.3 = (s32[128,128]{1,0:T(8,128)S(1)}, s32[128,128]{1,0:T(8,128)S(1)}, s32[128,128]{1,0:T(8,128)S(1)}) custom-call(bf16[64,8192]{1,0:T(8,128)(2,1)S(1)} %copy-done.1, bf16[64,8192]{1,0:T(8,128)(2,1)S(1)} %collective-permute-done.peer_ref, s32[8,8192]{1,0:T(8,128)S(1)} %get-tuple-element.17.first_ref, s32[4,3,16,128]{3,2,1,0:T(8,128)S(1)} %get-tuple-element.18.second_ref), custom_call_target="tpu_custom_call" | custom-call | flops 12884901888 | bytes 2097152 | tf_op jit(solution)/shard_map/first_hint/pallas_call | solution.py:182
  15.1 3.0 %collective-permute-start.1 = (s32[128,128]{1,0:T(8,128)S(1)}, s32[128,128]{1,0:T(8,128)S(1)}, u32[]{:S(2)}, u32[]{:S(2)}) collective-permute-start(s32[128,128]{1,0:T(8,128)S(1)} %get-tuple-element.19), channel_id=1, source_target_pairs={{0,1},{1,0},{2,3},{3,2},{4,5},{5,4},{6,7},{7,6},{8,9},{9,8},{10,11... | collective-permute-start | bytes 196616 | tf_op jit(solution)/shard_map/ppermute | solution.py:409
  18.1 2.6 %collective-permute-start.2 = (s32[128,128]{1,0:T(8,128)S(1)}, s32[128,128]{1,0:T(8,128)S(1)}, u32[]{:S(2)}, u32[]{:S(2)}) collective-permute-start(s32[128,128]{1,0:T(8,128)S(1)} %get-tuple-element.20), channel_id=1, source_target_pairs={{0,2},{1,3},{2,0},{3,1},{4,6},{5,7},{6,4},{7,5},{8,10},{9,11},{10,... | collective-permute-start | bytes 196616 | tf_op jit(solution)/shard_map/ppermute | solution.py:409
  20.7 0.0 collective-permute-start.3
  20.7 4.0 %first_hint.2.refs_0_ = s32[128,128]{1,0:T(8,128)S(1)} custom-call(bf16[64,8192]{1,0:T(8,128)(2,1)S(1)} %copy-done.1, bf16[64,8192]{1,0:T(8,128)(2,1)S(1)} %collective-permute-done.peer_ref, s32[8,8192]{1,0:T(8,128)S(1)} %get-tuple-element.17.first_ref, s32[4,3,16,128]{3,2,1,0:T(8,128)S(1)} %get-tuple-element.18.second_ref), custom_call_target="tpu_custom_call" | custom-call | flops 4294967296 | bytes 2097152 | tf_op jit(solution)/shard_map/first_hint/pallas_call | solution.py:182
  24.7 0.0 collective-permute-done.4.refs_5_
  24.7 0.9 %collective-permute-done.2.refs_2_ = s32[128,128]{1,0:T(8,128)S(1)} collective-permute-done((s32[128,128]{1,0:T(8,128)S(1)}, s32[128,128]{1,0:T(8,128)S(1)}, u32[]{:S(2)}, u32[]{:S(2)}) %collective-permute-start.2) | collective-permute-done | bytes 65568 | tf_op jit(solution)/shard_map/ppermute | solution.py:409
  25.6 1.2 %collective-permute-done.3.refs_3_ = s32[128,128]{1,0:T(8,128)S(1)} collective-permute-done((s32[128,128]{1,0:T(8,128)S(1)}, s32[128,128]{1,0:T(8,128)S(1)}, u32[]{:S(2)}, u32[]{:S(2)}) %collective-permute-start.3) | collective-permute-done | bytes 65568 | tf_op jit(solution)/shard_map/ppermute | solution.py:409
  26.8 0.5 sort_rows.1.refs_0_
  27.4 1.6 %collective-permute-start.7 = (s32[128,512]{1,0:T(8,128)S(1)}, s32[128,512]{1,0:T(8,128)S(1)}, u32[]{:S(2)}, u32[]{:S(2)}) collective-permute-start(s32[128,512]{1,0:T(8,128)S(1)} %sort_rows.1.refs_0_), channel_id=1, source_target_pairs={{0,8},{4,12},{8,0},{12,4},{16,24},{20,28},{24,16},{28,20},{1,9},{5... | collective-permute-start | bytes 786440 | tf_op jit(solution)/shard_map/ppermute | solution.py:409
  28.9 2.3 %second_matrix.1.refs_1_ = bf16[4,1024,512]{2,1,0:T(8,128)(2,1)S(1)} custom-call(s32[4,8,512]{2,1,0:T(8,128)S(1)} %get-tuple-element.22.first_ref.refs_2_.refs_3_), custom_call_target="tpu_custom_call" | custom-call | flops 1048576000 | bytes 4194304 | tf_op jit(solution)/shard_map/second_matrix/pallas_call | solution.py:289
  31.3 1.6 %collective-permute-start.6 = (s32[128,512]{1,0:T(8,128)S(1)}, s32[128,512]{1,0:T(8,128)S(1)}, u32[]{:S(2)}, u32[]{:S(2)}) collective-permute-start(s32[128,512]{1,0:T(8,128)S(1)} %sort_rows.1.refs_0_), channel_id=1, source_target_pairs={{0,16},{4,20},{8,24},{12,28},{16,0},{20,4},{24,8},{28,12},{1,17},{... | collective-permute-start | bytes 786440 | tf_op jit(solution)/shard_map/ppermute | solution.py:409
  32.8 0.5 collective-permute-start.5
  33.3 3.5 %second_hint.5 = (s32[4,128,1024]{2,1,0:T(8,128)S(1)}, bf16[4,1024,512]{2,1,0:T(8,128)(2,1)S(1)}) custom-call(s32[128,512]{1,0:T(8,128)S(1)} %sort_rows.1.refs_0_, bf16[4,1024,512]{2,1,0:T(8,128)(2,1)S(1)} %second_matrix.1.refs_1_, s32[4,8,512]{2,1,0:T(8,128)S(1)} %get-tuple-element.22.first_ref.refs_2_.refs_3_), custom_call_target="tpu_custom_call" | custom-call | flops 2147483648 | bytes 8388608 | tf_op jit(solution)/shard_map/second_hint/pallas_call | solution.py:355
  36.8 0.0 collective-permute-done.7.refs_0_
  36.8 3.6 %second_hint.6 = (s32[4,128,1024]{2,1,0:T(8,128)S(1)}, bf16[4,1024,512]{2,1,0:T(8,128)(2,1)S(1)}) custom-call(s32[128,512]{1,0:T(8,128)S(1)} %collective-permute-done.7.refs_0_, bf16[4,1024,512]{2,1,0:T(8,128)(2,1)S(1)} %get-tuple-element.23.refs_1_, s32[4,128,1024]{2,1,0:T(8,128)S(1)} %get-tuple-element.24.refs_2_, ...), custom_call_target="tpu_custom_call" | custom-call | flops 2147483648 | bytes 8388608 | tf_op jit(solution)/shard_map/second_hint/pallas_call | solution.py:355
  40.4 2.9 %collective-permute-done.6.refs_0_ = s32[128,512]{1,0:T(8,128)S(1)} collective-permute-done((s32[128,512]{1,0:T(8,128)S(1)}, s32[128,512]{1,0:T(8,128)S(1)}, u32[]{:S(2)}, u32[]{:S(2)}) %collective-permute-start.6) | collective-permute-done | bytes 262176 | tf_op jit(solution)/shard_map/ppermute | solution.py:409
  43.3 3.6 %second_hint.7 = (s32[4,128,1024]{2,1,0:T(8,128)S(1)}, bf16[4,1024,512]{2,1,0:T(8,128)(2,1)S(1)}) custom-call(s32[128,512]{1,0:T(8,128)S(1)} %collective-permute-done.6.refs_0_, bf16[4,1024,512]{2,1,0:T(8,128)(2,1)S(1)} %get-tuple-element.25.refs_1_, s32[4,128,1024]{2,1,0:T(8,128)S(1)} %get-tuple-element.26.refs_2_, ...), custom_call_target="tpu_custom_call" | custom-call | flops 2147483648 | bytes 8388608 | tf_op jit(solution)/shard_map/second_hint/pallas_call | solution.py:355
  46.9 1.4 %second_hint.9.value_ref = s32[4,128,512]{2,1,0:T(8,128)S(1)} custom-call(s32[128,512]{1,0:T(8,128)S(1)} %collective-permute-done.5.refs_0_, bf16[4,1024,512]{2,1,0:T(8,128)(2,1)S(1)} %get-tuple-element.27.refs_1_, s32[4,128,1024]{2,1,0:T(8,128)S(1)} %get-tuple-element.28.refs_2_), custom_call_target="tpu_custom_call" | custom-call | flops 1073741824 | bytes 4194304 | tf_op jit(solution)/shard_map/second_hint/pallas_call | solution.py:355
  48.3 0.1 collective-permute-start.9
  48.4 1.4 %second_hint.8.value_ref = s32[4,128,512]{2,1,0:T(8,128)S(1)} custom-call(s32[128,512]{1,0:T(8,128)S(1)} %collective-permute-done.5.refs_0_, bf16[4,1024,512]{2,1,0:T(8,128)(2,1)S(1)} %get-tuple-element.27.refs_1_, s32[4,128,1024]{2,1,0:T(8,128)S(1)} %get-tuple-element.28.refs_2_), custom_call_target="tpu_custom_call" | custom-call | flops 1073741824 | bytes 4194304 | tf_op jit(solution)/shard_map/second_hint/pallas_call | solution.py:355
  49.8 0.6 collective-permute-start.8
  50.3 1.4 %write_halves.4.refs_0_ = f32[4,2,256,1024]{3,2,1,0:T(8,128)} custom-call(s32[4,128,512]{2,1,0:T(8,128)S(1)} %second_hint.9.value_ref), custom_call_target="tpu_custom_call" | custom-call | tf_op jit(solution)/shard_map/write_halves/pallas_call | solution.py:395
  51.7 1.4 %write_halves.5.refs_0_ = f32[4,2,256,1024]{3,2,1,0:T(8,128)} custom-call(s32[4,128,512]{2,1,0:T(8,128)S(1)} %second_hint.8.value_ref, f32[4,2,256,1024]{3,2,1,0:T(8,128)} %write_halves.4.refs_0_), custom_call_target="tpu_custom_call", output_to_operand_aliasing={{}: (1, {})} | custom-call | tf_op jit(solution)/shard_map/write_halves/pallas_call | solution.py:395
  53.2 1.4 %write_halves.6.refs_0_ = f32[4,2,256,1024]{3,2,1,0:T(8,128)} custom-call(s32[4,128,512]{2,1,0:T(8,128)S(1)} %collective-permute-done.9.value_ref, f32[4,2,256,1024]{3,2,1,0:T(8,128)} %write_halves.5.refs_0_), custom_call_target="tpu_custom_call", output_to_operand_aliasing={{}: (1, {})} | custom-call | tf_op jit(solution)/shard_map/write_halves/pallas_call | solution.py:395
  54.6 1.4 %write_halves.7 = f32[4,2,256,1024]{3,2,1,0:T(8,128)} custom-call(s32[4,128,512]{2,1,0:T(8,128)S(1)} %collective-permute-done.8.value_ref, f32[4,2,256,1024]{3,2,1,0:T(8,128)} %write_halves.6.refs_0_), custom_call_target="tpu_custom_call", output_to_operand_aliasing={{}: (1, {})} | custom-call | tf_op jit(solution)/shard_map/write_halves/pallas_call | solution.py:395
  (8 shorter events, 0.0 us)
Async XLA Ops:
  0.0 3.0 %collective-permute-start = (bf16[64,8192]{1,0:T(8,128)(2,1)}, bf16[64,8192]{1,0:T(8,128)(2,1)S(1)}, u32[]{:S(2)}, u32[]{:S(2)}) collective-permute-start(bf16[64,8192]{1,0:T(8,128)(2,1)} %own_ref.3), channel_id=1, source_target_pairs={{0,4},{4,0},{8,12},{12,8},{16,20},{20,16},{24,28},{28,24},{1,5},{5... | collective-permute-start | bytes 3145736 | tf_op jit(solution)/shard_map/ppermute | solution.py:409
  0.5 24.2 %collective-permute-start.4 = (s32[1,256]{1,0:T(1,128)}, s32[1,256]{1,0:T(1,128)S(1)}, u32[]{:S(2)}, u32[]{:S(2)}) collective-permute-start(s32[1,256]{1,0:T(1,128)} %refs_4_.1), channel_id=1, source_target_pairs={{0,4},{4,0},{8,12},{12,8},{16,20},{20,16},{24,28},{28,24},{1,5},{5... | collective-permute-start | bytes 3080 | tf_op jit(solution)/shard_map/ppermute | solution.py:409
  0.5 0.7 %copy-start.2 = (s32[2]{0:T(128)S(1)}, s32[2]{0:T(128)}, u32[]{:S(2)}) copy-start(s32[2]{0:T(128)} %seeds_ref.1) | copy-start | bytes 28
  3.0 1.2 %copy-start.1 = (bf16[64,8192]{1,0:T(8,128)(2,1)S(1)}, bf16[64,8192]{1,0:T(8,128)(2,1)}, u32[]{:S(2)}) copy-start(bf16[64,8192]{1,0:T(8,128)(2,1)} %own_ref.3) | copy-start | bytes 3145732
  15.1 9.7 %collective-permute-start.1 = (s32[128,128]{1,0:T(8,128)S(1)}, s32[128,128]{1,0:T(8,128)S(1)}, u32[]{:S(2)}, u32[]{:S(2)}) collective-permute-start(s32[128,128]{1,0:T(8,128)S(1)} %get-tuple-element.19), channel_id=1, source_target_pairs={{0,1},{1,0},{2,3},{3,2},{4,5},{5,4},{6,7},{7,6},{8,9},{9,8},{10,11... | collective-permute-start | bytes 196616 | tf_op jit(solution)/shard_map/ppermute | solution.py:409
  18.1 7.5 %collective-permute-start.2 = (s32[128,128]{1,0:T(8,128)S(1)}, s32[128,128]{1,0:T(8,128)S(1)}, u32[]{:S(2)}, u32[]{:S(2)}) collective-permute-start(s32[128,128]{1,0:T(8,128)S(1)} %get-tuple-element.20), channel_id=1, source_target_pairs={{0,2},{1,3},{2,0},{3,1},{4,6},{5,7},{6,4},{7,5},{8,10},{9,11},{10,... | collective-permute-start | bytes 196616 | tf_op jit(solution)/shard_map/ppermute | solution.py:409
  20.7 6.2 %copy-start = (s32[1,256]{1,0:T(1,128)S(1)}, s32[1,256]{1,0:T(1,128)}, u32[]{:S(2)}) copy-start(s32[1,256]{1,0:T(1,128)} %refs_4_.1) | copy-start | bytes 3076
  20.7 6.2 %collective-permute-start.3 = (s32[128,128]{1,0:T(8,128)S(1)}, s32[128,128]{1,0:T(8,128)S(1)}, u32[]{:S(2)}, u32[]{:S(2)}) collective-permute-start(s32[128,128]{1,0:T(8,128)S(1)} %get-tuple-element.21), channel_id=1, source_target_pairs={{0,3},{1,2},{2,1},{3,0},{4,7},{5,6},{6,5},{7,4},{8,11},{9,10},{10,... | collective-permute-start | bytes 196616 | tf_op jit(solution)/shard_map/ppermute | solution.py:409
  27.4 9.5 %collective-permute-start.7 = (s32[128,512]{1,0:T(8,128)S(1)}, s32[128,512]{1,0:T(8,128)S(1)}, u32[]{:S(2)}, u32[]{:S(2)}) collective-permute-start(s32[128,512]{1,0:T(8,128)S(1)} %sort_rows.1.refs_0_), channel_id=1, source_target_pairs={{0,8},{4,12},{8,0},{12,4},{16,24},{20,28},{24,16},{28,20},{1,9},{5... | collective-permute-start | bytes 786440 | tf_op jit(solution)/shard_map/ppermute | solution.py:409
  31.3 12.0 %collective-permute-start.6 = (s32[128,512]{1,0:T(8,128)S(1)}, s32[128,512]{1,0:T(8,128)S(1)}, u32[]{:S(2)}, u32[]{:S(2)}) collective-permute-start(s32[128,512]{1,0:T(8,128)S(1)} %sort_rows.1.refs_0_), channel_id=1, source_target_pairs={{0,16},{4,20},{8,24},{12,28},{16,0},{20,4},{24,8},{28,12},{1,17},{... | collective-permute-start | bytes 786440 | tf_op jit(solution)/shard_map/ppermute | solution.py:409
  32.8 14.0 %collective-permute-start.5 = (s32[128,512]{1,0:T(8,128)S(1)}, s32[128,512]{1,0:T(8,128)S(1)}, u32[]{:S(2)}, u32[]{:S(2)}) collective-permute-start(s32[128,512]{1,0:T(8,128)S(1)} %sort_rows.1.refs_0_), channel_id=1, source_target_pairs={{0,24},{4,28},{8,16},{12,20},{16,8},{20,12},{24,0},{28,4},{1,25},{... | collective-permute-start | bytes 786440 | tf_op jit(solution)/shard_map/ppermute | solution.py:409
  48.3 4.9 %collective-permute-start.9 = (s32[4,128,512]{2,1,0:T(8,128)S(1)}, s32[4,128,512]{2,1,0:T(8,128)S(1)}, u32[]{:S(2)}, u32[]{:S(2)}) collective-permute-start(s32[4,128,512]{2,1,0:T(8,128)S(1)} %second_hint.9.value_ref), channel_id=1, source_target_pairs={{0,4},{4,0},{8,12},{12,8},{16,20},{20,16},{24,28},{28,24},{1,5},{5... | collective-permute-start | bytes 3145736 | tf_op jit(solution)/shard_map/ppermute | solution.py:409
  49.8 4.8 %collective-permute-start.8 = (s32[4,128,512]{2,1,0:T(8,128)S(1)}, s32[4,128,512]{2,1,0:T(8,128)S(1)}, u32[]{:S(2)}, u32[]{:S(2)}) collective-permute-start(s32[4,128,512]{2,1,0:T(8,128)S(1)} %second_hint.8.value_ref), channel_id=1, source_target_pairs={{0,4},{4,0},{8,12},{12,8},{16,20},{20,16},{24,28},{28,24},{1,5},{5... | collective-permute-start | bytes 3145736 | tf_op jit(solution)/shard_map/ppermute | solution.py:409

commit v5 on v4

--- a/solution.py
+++ b/solution.py
@@ -114,11 +114,11 @@
     return low_p + (((low_q + (high_q << 8)) << 8) + high_p << 8)
 
 
-def make_limbs(first_ref, second, start, width, lane, count, store):
+def make_limbs(first_ref, second, start, width, lane, count, store, mixes=(0, 1)):
     second = [jnp.concatenate([value] * (lane // LANES), axis=1) for value in second]
     for t in range(width // lane):
         at = pl.ds(pl.multiple_of(start + t * lane, lane), lane)
-        for mix in range(2):
+        for mix in mixes:
             a, square, slope = (first_ref[4 * mix + i : 4 * mix + i + 1, at] for i in range(3))
             value = a * second[0] + square + second[1]
             slope = slope + second[2]
@@ -303,106 +303,183 @@
     )(by_row, *after)
 
 
-def second_kernel(block, first, count, has_total, has_next, *refs):
-    refs = list(refs)
-    hint_ref, matrix_ref = refs[:2]
-    total_ref = refs[2] if has_total else None
-    next_ref, next_matrix_ref = (refs[2 + has_total], refs[-3]) if has_next else (None, None)
-    out_ref, digits, small_digits = refs[-4 if has_next else -3], refs[-2], refs[-1]
-    half = hint_ref.shape[0]
+def spread(hint_refs, digits, small_digits):
+    half = sum(ref.shape[0] for ref in hint_refs)
+    for i, ref in enumerate(hint_refs):
+        hint = ref[...]
+        rows = ref.shape[0]
+        for place in range(4):
+            at = slice(place * half + i * rows, place * half + (i + 1) * rows)
+            byte = byte_digits(hint, place)
+            digits[at] = byte
+            small_digits[at] = byte * jnp.bfloat16(1 / 256)
+
+
+def product(digits, small_digits, matrix_ref, at):
+    return join(
+        [
+            lax.dot_general(
+                [digits, small_digits][limb % 2][...],
+                matrix_ref[limb, at],
+                NT,
+                preferred_element_type=jnp.float32,
+            )
+            for limb in range(4)
+        ]
+    )
+
+
+def second_kernel(block, count, has_total, *refs):
+    hint_refs, (matrix_ref, next_ref) = refs[:count], refs[count : count + 2]
+    total_ref = refs[count + 2] if has_total else None
+    out_ref, next_matrix_ref, digits, small_digits = refs[-4:]
+    _, half, columns = out_ref.shape
     depth = matrix_ref.shape[2]
-    hint = hint_ref[...]
-    for place in range(4):
-        byte = byte_digits(hint, place)
-        digits[place * half : (place + 1) * half] = byte
-        small_digits[place * half : (place + 1) * half] = byte * jnp.bfloat16(1 / 256)
+    spread(hint_refs, digits, small_digits)
     sub = lax.broadcasted_iota(jnp.int32, (SUBLANES, LANES), 0)
     lane = min(512, depth)
 
-    for start in range(0, count, block):
-        at = slice(first + start, first + start + block)
-        total = join(
-            [
+    for start in range(0, columns, block):
+        at = slice(start, start + block)
+
+        def store(i, row, column, value, start=start):
+            top = start + row
+            next_matrix_ref[i, top : top + SUBLANES, column : column + lane] = value
+
+        limbs = []
+        second = by_second(start + sub, SUBLANES)
+        for limb in range(4):
+            limbs.append(
                 lax.dot_general(
                     [digits, small_digits][limb % 2][...],
                     matrix_ref[limb, at],
                     NT,
                     preferred_element_type=jnp.float32,
                 )
-                for limb in range(4)
-            ]
-        )
+            )
+            if limb % 2:
+                make_limbs(next_ref, second, 0, depth, lane, block // SUBLANES, store, (limb // 2,))
+        total = join(limbs)
         for place in range(4):
             term = total[place * half : (place + 1) * half]
-            out = slice(start, start + block)
-            out_ref[place, :, out] = term if total_ref is None else total_ref[place, :, at] + term
-        if has_next:
-
-            def store(i, row, column, value, start=start):
-                top = start + row
-                next_matrix_ref[i, top : top + SUBLANES, column : column + lane] = value
-
-            second = by_second(start + sub, SUBLANES)
-            make_limbs(next_ref, second, 0, depth, lane, block // SUBLANES, store)
-
-
-def second_hint(hint, matrix, first, count, total=None, by_row=None, t=0):
-    half = hint.shape[0]
+            out_ref[place, :, at] = total_ref[place, :, at] + term if has_total else term
+
+
+def product_cost(rows, depth, columns):
+    return pl.CostEstimate(
+        flops=8 * rows * depth * columns,
+        bytes_accessed=8 * depth * columns + 8 * rows * columns,
+        transcendentals=0,
+    )
+
+
+def second_hint(hints, matrix, by_row, t, total=None):
+    half = sum(hint.shape[0] for hint in hints)
+    _, columns, depth = matrix.shape
+    has_total = total is not None
+    whole = pl.BlockSpec(memory_space=pltpu.VMEM)
+    row_spec = pl.BlockSpec((None,) + by_row.shape[1:], lambda i: (t, 0, 0))
+    return pl.pallas_call(
+        functools.partial(second_kernel, min(256, columns), len(hints), has_total),
+        grid=(1,),
+        out_shape=[
+            jax.ShapeDtypeStruct((4, half, columns), jnp.int32),
+            jax.ShapeDtypeStruct(matrix.shape, matrix.dtype),
+        ],
+        in_specs=[whole] * (len(hints) + 1) + [row_spec] + [whole] * has_total,
+        out_specs=[whole] * 2,
+        scratch_shapes=[pltpu.VMEM((4 * half, depth), jnp.bfloat16)] * 2,
+        compiler_params=pltpu.CompilerParams(vmem_limit_bytes=VMEM_LIMIT),
+        cost_estimate=product_cost(4 * half, depth, columns),
+        name="second_hint",
+    )(*hints, matrix, by_row, *([total] if has_total else []))
+
+
+def own_rows(half, flip):
+    core = lax.axis_index("row") % 2
+    return pl.ds(pl.multiple_of((1 - core if flip else core) * half, half), half)
+
+
+def put_halves(value, out_ref, place, rows, columns, low, high, sems):
+    scale = np.float32(1 / 65536)
+    low[...] = (value & 65535).astype(jnp.float32) * scale
+    high[...] = lax.shift_right_logical(value, jnp.int32(16)).astype(jnp.float32) * scale
+    copies = []
+    for k, source in enumerate((low, high)):
+        target = out_ref.at[place, k, rows, columns]
+        copies.append(pltpu.make_async_copy(source, target, sems.at[k]))
+        copies[-1].start()
+    return copies
+
+
+def last_kernel(block, first, count, *refs):
+    hint_refs, (matrix_ref, total_ref, sum_ref, digits, small_digits) = refs[:count], refs[count:]
+    _, half, columns = sum_ref.shape
+    spread(hint_refs, digits, small_digits)
+    for i in range(columns // block):
+        inner = slice(i * block, (i + 1) * block)
+        at = slice(first + i * block, first + (i + 1) * block)
+        total = product(digits, small_digits, matrix_ref, at)
+        for place in range(4):
+            term = total[place * half : (place + 1) * half]
+            sum_ref[place, :, inner] = total_ref[place, :, at] + term
+
+
+def last_hint(hints, matrix, total, first, count):
+    half = sum(hint.shape[0] for hint in hints)
     depth = matrix.shape[2]
-    has_total, has_next = total is not None, by_row is not None
     whole = pl.BlockSpec(memory_space=pltpu.VMEM)
-    row_spec = pl.BlockSpec((None,) + by_row.shape[1:], lambda i: (t, 0, 0)) if has_next else None
-    return pl.pallas_call(
-        functools.partial(second_kernel, min(256, count), first, count, has_total, has_next),
-        grid=(1,),
-        out_shape=[jax.ShapeDtypeStruct((4, half, count), jnp.int32)]
-        + [jax.ShapeDtypeStruct(matrix.shape, matrix.dtype)] * has_next,
-        in_specs=[whole] * (2 + has_total) + [row_spec] * has_next,
-        out_specs=[whole] * (1 + has_next),
+    return pl.pallas_call(
+        functools.partial(last_kernel, min(256, count), first, len(hints)),
+        in_specs=[whole] * (len(hints) + 2),
+        out_specs=whole,
+        out_shape=jax.ShapeDtypeStruct((4, half, count), jnp.int32),
         scratch_shapes=[pltpu.VMEM((4 * half, depth), jnp.bfloat16)] * 2,
         compiler_params=pltpu.CompilerParams(vmem_limit_bytes=VMEM_LIMIT),
-        cost_estimate=pl.CostEstimate(
-            flops=32 * half * depth * count,
-            bytes_accessed=8 * depth * count + 32 * half * count,
-            transcendentals=0,
-        ),
-        name="second_hint",
-    )(hint, matrix, *([total] if has_total else []), *([by_row] if has_next else []))
-
-
-def halves_kernel(first, flip, value_ref, *refs):
-    out_ref, low, high, sems = refs[-4:]
+        cost_estimate=product_cost(4 * half, depth, count),
+        name="last_hint",
+    )(*hints, matrix, total)
+
+
+def halves_scratch(shape):
+    return [pltpu.VMEM(shape, jnp.float32)] * 2 + [pltpu.SemaphoreType.DMA((shape[0], 2))]
+
+
+def write_part(value_ref, out_ref, flip, first, low, high, sems):
     digits, half, columns = value_ref.shape
-    core = lax.axis_index("row") % 2
-    start = pl.multiple_of((1 - core if flip else core) * half, half)
-    scale = np.float32(1 / 65536)
+    rows, at = own_rows(half, flip), pl.ds(first, columns)
     copies = []
     for i in range(digits):
-        value = value_ref[i]
-        low[i] = (value & 65535).astype(jnp.float32) * scale
-        high[i] = lax.shift_right_logical(value, jnp.int32(16)).astype(jnp.float32) * scale
-        for k, source in enumerate((low, high)):
-            target = out_ref.at[i, k, pl.ds(start, half), pl.ds(first, columns)]
-            copies.append(pltpu.make_async_copy(source.at[i], target, sems.at[i, k]))
-            copies[-1].start()
+        copies += put_halves(
+            value_ref[i], out_ref, i, rows, at, low.at[i], high.at[i], sems.at[i]
+        )
+    return copies
+
+
+def write_kernel(parts, *refs):
+    scratch = refs[len(refs) - 3 * len(parts) :]
+    out_ref = refs[len(refs) - 3 * len(parts) - 1]
+    copies = []
+    for i, (flip, first) in enumerate(parts):
+        copies += write_part(refs[i], out_ref, flip, first, *scratch[3 * i : 3 * i + 3])
     for copy in copies:
         copy.wait()
 
 
-def write_halves(value, flip, first, columns, out=None):
-    digits, half, some = value.shape
+def write_parts(values, parts, columns, out=None):
+    digits, half, _ = values[0].shape
     anywhere = pl.BlockSpec(memory_space=pl.ANY)
-    return pl.pallas_call(
-        functools.partial(halves_kernel, first, flip),
-        in_specs=[pl.BlockSpec(memory_space=pltpu.VMEM)] + [anywhere] * (out is not None),
+    has_out = out is not None
+    return pl.pallas_call(
+        functools.partial(write_kernel, parts),
+        in_specs=[pl.BlockSpec(memory_space=pltpu.VMEM)] * len(values) + [anywhere] * has_out,
         out_specs=anywhere,
         out_shape=jax.ShapeDtypeStruct((digits, 2, 2 * half, columns), jnp.float32),
-        scratch_shapes=[pltpu.VMEM((digits, half, some), jnp.float32)] * 2
-        + [pltpu.SemaphoreType.DMA((digits, 2))],
-        input_output_aliases={} if out is None else {1: 0},
-        compiler_params=pltpu.CompilerParams(vmem_limit_bytes=VMEM_LIMIT),
-        name="write_halves",
-    )(value, *([] if out is None else [out]))
+        scratch_shapes=[scratch for value in values for scratch in halves_scratch(value.shape)],
+        input_output_aliases={len(values): 0} if has_out else {},
+        compiler_params=pltpu.CompilerParams(vmem_limit_bytes=VMEM_LIMIT),
+        name="write_parts",
+    )(*values, *([out] if has_out else []))
 
 
 def shift_by(value, axis, offset):
@@ -427,23 +504,28 @@
         for i, part in enumerate(parts):
             hints[s + i] = shift_by(part, "col", s + i) if s + i else part
     hint = sort_rows(hints, row_order, peer_order)
-    sources = [hint]
+    sources = [[hint]]
     for t in range(1, chips):
-        sources.append(shift_by(hint, "row", 2 * t))
+        low = t & -t
+        if low == t:
+            sources.append([shift_by(hint, "row", 2 * t)])
+            continue
+        halves = []
+        for i, (via, rest) in enumerate(((low, t ^ low), (t ^ low, low))):
+            piece = jnp.concatenate(sources[rest]) if len(sources[rest]) > 1 else sources[rest][0]
+            piece = piece[i * (half // 2) : (i + 1) * (half // 2)]
+            halves.append(shift_by(piece, "row", 2 * via))
+        sources.append(halves)
 
     matrix = second_matrix(by_row, 0, 1, N)
     total = None
     for t in range(chips - 1):
-        total, matrix = second_hint(sources[t], matrix, 0, N, total, by_row, t + 1)
+        total, matrix = second_hint(sources[t], matrix, by_row, t + 1, total)
     cut = N // 2
-    totals = [second_hint(sources[-1], matrix, i * cut, cut, total)[0] for i in range(2)]
-
-    others = [shift_by(value, "row", 1) for value in totals]
-    out = None
-    for flip, values in enumerate((totals, others)):
-        for i, value in enumerate(values):
-            out = write_halves(value, flip, i * cut, N, out)
-    return out
+    sums = [last_hint(sources[-1], matrix, total, i * cut, cut) for i in range(2)]
+    others = [shift_by(value, "row", 1) for value in sums]
+    out = write_parts(sums, [(False, 0), (False, cut)], N)
+    return write_parts(others, [(True, 0), (True, cut)], N, out)
 
 
 def solution(mesh):

time: 56.3 us -> 51.6 us (0.917)
  Pallas kernels: 38.4 us -> 35.5 us
  waiting for transfers between devices: 5.2 us -> 2.41 us
  starting transfers between devices: 10.4 us -> 11.3 us
    pallas_call x9 -> x7, Pallas kernels: 19 us -> 16.1 us  [the longest x3 9.03 us: second_hint(): pl.pallas_call(functools.partial(second_kernel, min(256, columns), len(hi...]
    ppermute x10 -> x11, waiting for transfers between devices: 5.2 us -> 2.41 us  [shift_by(): lax.ppermute(value, axis, [(i, i ^ offset) for i in range(lax.axis_size(a...]
    ppermute x10 -> x11, starting transfers between devices: 10.4 us -> 11.3 us  [shift_by(): lax.ppermute(value, axis, [(i, i ^ offset) for i in range(lax.axis_size(a...]
  transfers between devices with their start and end apart: 10 -> 11, of which waited for: 4 -> 4; matrix products, arithmetic and copies ran while one was open for 0% -> 0% of each run, Pallas kernels for 63% -> 61%
where the time goes in v5:
time: 51.6 us; the launch traced here: 51.4 us
  Pallas kernels  35.5 us (69%)
  starting transfers between devices  11.3 us (22%)
  waiting for transfers between devices  2.41 us (5%)
  local copies, waits for them, and re-layouts  1.9 us (4%)
    pallas_call x2, Pallas kernels, first_hint(): pl.pallas_call(functools.partial(first_kernel, s, width, lane), out_shape...  14.9 us
    ppermute x11, starting transfers between devices, shift_by(): lax.ppermute(value, axis, [(i, i ^ offset) for i in range(lax.axis_size(a...  11.3 us
    pallas_call x3, Pallas kernels, second_hint(): pl.pallas_call(functools.partial(second_kernel, min(256, columns), len(hi...  9.03 us
    pallas_call x2, Pallas kernels, write_parts(): pl.pallas_call(functools.partial(write_kernel, parts), in_specs=[pl.Block...  4.32 us
    pallas_call x2, Pallas kernels, last_hint(): pl.pallas_call(functools.partial(last_kernel, min(256, count), first, len...  2.77 us
    ppermute x11, waiting for transfers between devices, shift_by(): lax.ppermute(value, axis, [(i, i ^ offset) for i in range(lax.axis_size(a...  2.41 us
    pallas_call x1, Pallas kernels, second_matrix(): pl.pallas_call(functools.partial(matrix_kernel, block), grid=(1,), out_sh...  2.34 us
    unnamed x6, local copies, waits for them, and re-layouts  1.88 us
  transfers between devices with their start and end apart: 11, of which 4 were waited for; matrix products, arithmetic and copies ran while one was open for 0% of the time, Pallas kernels for 61%

profile of v5, /device:TPU:0, one launch (start us, length us, event | category | flops | bytes accessed | tf_op | source)
XLA Modules:
  0.0 51.4 jit_solution(5641660699272165594)
XLA Ops:
  0.0 0.5 collective-permute-start
  0.5 0.0 collective-permute-start.4
  0.5 0.7 %copy-done.2 = s32[2]{0:T(128)S(1)} copy-done((s32[2]{0:T(128)S(1)}, s32[2]{0:T(128)}, u32[]{:S(2)}) %copy-start.2) | copy-done | bytes 32
  1.2 1.6 %tables.1 = (s32[8,8192]{1,0:T(8,128)S(1)}, s32[4,3,16,128]{3,2,1,0:T(8,128)S(1)}, s32[4,8,512]{2,1,0:T(8,128)S(1)}) custom-call(s32[2]{0:T(128)S(1)} %copy-done.2), custom_call_target="tpu_custom_call" | custom-call | tf_op jit(solution)/shard_map/tables/pallas_call | solution.py:92
  2.8 0.2 collective-permute-done.peer_ref
  3.0 1.2 %copy-done.1 = bf16[64,8192]{1,0:T(8,128)(2,1)S(1)} copy-done((bf16[64,8192]{1,0:T(8,128)(2,1)S(1)}, bf16[64,8192]{1,0:T(8,128)(2,1)}, u32[]{:S(2)}) %copy-start.1) | copy-done | bytes 1048600
  4.2 10.9 %first_hint.3 = (s32[128,128]{1,0:T(8,128)S(1)}, s32[128,128]{1,0:T(8,128)S(1)}, s32[128,128]{1,0:T(8,128)S(1)}) custom-call(bf16[64,8192]{1,0:T(8,128)(2,1)S(1)} %copy-done.1, bf16[64,8192]{1,0:T(8,128)(2,1)S(1)} %collective-permute-done.peer_ref, s32[8,8192]{1,0:T(8,128)S(1)} %get-tuple-element.17.first_ref, s32[4,3,16,128]{3,2,1,0:T(8,128)S(1)} %get-tuple-element.18.second_ref), custom_call_target="tpu_custom_call" | custom-call | flops 12884901888 | bytes 2097152 | tf_op jit(solution)/shard_map/first_hint/pallas_call | solution.py:182
  15.1 3.0 %collective-permute-start.1 = (s32[128,128]{1,0:T(8,128)S(1)}, s32[128,128]{1,0:T(8,128)S(1)}, u32[]{:S(2)}, u32[]{:S(2)}) collective-permute-start(s32[128,128]{1,0:T(8,128)S(1)} %get-tuple-element.19), channel_id=1, source_target_pairs={{0,1},{1,0},{2,3},{3,2},{4,5},{5,4},{6,7},{7,6},{8,9},{9,8},{10,11... | collective-permute-start | bytes 196616 | tf_op jit(solution)/shard_map/ppermute | solution.py:486
  18.1 2.6 %collective-permute-start.2 = (s32[128,128]{1,0:T(8,128)S(1)}, s32[128,128]{1,0:T(8,128)S(1)}, u32[]{:S(2)}, u32[]{:S(2)}) collective-permute-start(s32[128,128]{1,0:T(8,128)S(1)} %get-tuple-element.20), channel_id=1, source_target_pairs={{0,2},{1,3},{2,0},{3,1},{4,6},{5,7},{6,4},{7,5},{8,10},{9,11},{10,... | collective-permute-start | bytes 196616 | tf_op jit(solution)/shard_map/ppermute | solution.py:486
  20.7 4.0 %first_hint.2.refs_0_ = s32[128,128]{1,0:T(8,128)S(1)} custom-call(bf16[64,8192]{1,0:T(8,128)(2,1)S(1)} %copy-done.1, bf16[64,8192]{1,0:T(8,128)(2,1)S(1)} %collective-permute-done.peer_ref, s32[8,8192]{1,0:T(8,128)S(1)} %get-tuple-element.17.first_ref, s32[4,3,16,128]{3,2,1,0:T(8,128)S(1)} %get-tuple-element.18.second_ref), custom_call_target="tpu_custom_call" | custom-call | flops 4294967296 | bytes 2097152 | tf_op jit(solution)/shard_map/first_hint/pallas_call | solution.py:182
  24.7 0.0 collective-permute-done.4.refs_5_
  24.8 0.0 collective-permute-done.1.refs_1_
  24.8 0.9 %collective-permute-done.2.refs_2_ = s32[128,128]{1,0:T(8,128)S(1)} collective-permute-done((s32[128,128]{1,0:T(8,128)S(1)}, s32[128,128]{1,0:T(8,128)S(1)}, u32[]{:S(2)}, u32[]{:S(2)}) %collective-permute-start.2) | collective-permute-done | bytes 65568 | tf_op jit(solution)/shard_map/ppermute | solution.py:486
  25.6 1.2 %collective-permute-done.3.refs_3_ = s32[128,128]{1,0:T(8,128)S(1)} collective-permute-done((s32[128,128]{1,0:T(8,128)S(1)}, s32[128,128]{1,0:T(8,128)S(1)}, u32[]{:S(2)}, u32[]{:S(2)}) %collective-permute-start.3) | collective-permute-done | bytes 65568 | tf_op jit(solution)/shard_map/ppermute | solution.py:486
  26.9 0.5 %sort_rows.1.refs_0_ = s32[128,512]{1,0:T(8,128)S(1)} custom-call(s32[128,128]{1,0:T(8,128)S(1)} %first_hint.2.refs_0_, s32[128,128]{1,0:T(8,128)S(1)} %collective-permute-done.1.refs_1_, s32[128,128]{1,0:T(8,128)S(1)} %collective-permute-done.2.refs_2_, s32[128,128]{1,0:T(8,128)S(1)} %collective-permute-done.3.refs_3_, s32[1,256]{1,0:T(1,128)S(1)} %copy-done, ...), custom_call_target="tpu_custom_call" | custom-call | tf_op jit(solution)/shard_map/sort_rows/pallas_call | solution.py:251
  27.4 1.6 %collective-permute-start.7 = (s32[128,512]{1,0:T(8,128)S(1)}, s32[128,512]{1,0:T(8,128)S(1)}, u32[]{:S(2)}, u32[]{:S(2)}) collective-permute-start(s32[128,512]{1,0:T(8,128)S(1)} %sort_rows.1.refs_0_), channel_id=1, source_target_pairs={{0,8},{4,12},{8,0},{12,4},{16,24},{20,28},{24,16},{28,20},{1,9},{5... | collective-permute-start | bytes 786440 | tf_op jit(solution)/shard_map/ppermute | solution.py:486
  28.9 1.5 %collective-permute-start.5 = (s32[128,512]{1,0:T(8,128)S(1)}, s32[128,512]{1,0:T(8,128)S(1)}, u32[]{:S(2)}, u32[]{:S(2)}) collective-permute-start(s32[128,512]{1,0:T(8,128)S(1)} %sort_rows.1.refs_0_), channel_id=1, source_target_pairs={{0,16},{4,20},{8,24},{12,28},{16,0},{20,4},{24,8},{28,12},{1,17},{... | collective-permute-start | bytes 786440 | tf_op jit(solution)/shard_map/ppermute | solution.py:486
  30.5 2.3 %second_matrix.1.refs_1_ = bf16[4,1024,512]{2,1,0:T(8,128)(2,1)S(1)} custom-call(s32[4,8,512]{2,1,0:T(8,128)S(1)} %get-tuple-element.22.first_ref.refs_2_), custom_call_target="tpu_custom_call" | custom-call | flops 1048576000 | bytes 4194304 | tf_op jit(solution)/shard_map/second_matrix/pallas_call | solution.py:289
  32.8 2.9 %second_hint.3 = (s32[4,128,1024]{2,1,0:T(8,128)S(1)}, bf16[4,1024,512]{2,1,0:T(8,128)(2,1)S(1)}) custom-call(s32[128,512]{1,0:T(8,128)S(1)} %sort_rows.1.refs_0_, bf16[4,1024,512]{2,1,0:T(8,128)(2,1)S(1)} %second_matrix.1.refs_1_, s32[4,8,512]{2,1,0:T(8,128)S(1)} %get-tuple-element.22.first_ref.refs_2_), custom_call_target="tpu_custom_call" | custom-call | flops 2147483648 | bytes 8388608 | tf_op jit(solution)/shard_map/second_hint/pallas_call | solution.py:382
  35.8 0.0 collective-permute-done.7.refs_0_
  35.8 0.6 %collective-permute-start.8 = (s32[64,512]{1,0:T(8,128)S(1)}, s32[64,512]{1,0:T(8,128)S(1)}, u32[]{:S(2)}, u32[]{:S(2)}) collective-permute-start(s32[64,512]{1,0:T(8,128)S(1)} %slice.9), channel_id=1, source_target_pairs={{0,16},{4,20},{8,24},{12,28},{16,0},{20,4},{24,8},{28,12},{1,17},{... | collective-permute-start | bytes 393224 | tf_op jit(solution)/shard_map/ppermute | solution.py:486
  36.4 0.0 collective-permute-done.5.refs_0_
  36.4 0.9 %collective-permute-start.6 = (s32[64,512]{1,0:T(8,128)S(1)}, s32[64,512]{1,0:T(8,128)S(1)}, u32[]{:S(2)}, u32[]{:S(2)}) collective-permute-start(s32[64,512]{1,0:T(8,128)S(1)} %slice.8), channel_id=1, source_target_pairs={{0,8},{4,12},{8,0},{12,4},{16,24},{20,28},{24,16},{28,20},{1,9},{5... | collective-permute-start | bytes 393224 | tf_op jit(solution)/shard_map/ppermute | solution.py:486
  37.3 3.0 %second_hint.4 = (s32[4,128,1024]{2,1,0:T(8,128)S(1)}, bf16[4,1024,512]{2,1,0:T(8,128)(2,1)S(1)}) custom-call(s32[128,512]{1,0:T(8,128)S(1)} %collective-permute-done.7.refs_0_, bf16[4,1024,512]{2,1,0:T(8,128)(2,1)S(1)} %get-tuple-element.23.refs_1_, s32[4,8,512]{2,1,0:T(8,128)S(1)} %get-tuple-element.22.first_ref.refs_2_, ...), custom_call_target="tpu_custom_call" | custom-call | flops 2147483648 | bytes 8388608 | tf_op jit(solution)/shard_map/second_hint/pallas_call | solution.py:382
  40.3 3.0 %second_hint.5 = (s32[4,128,1024]{2,1,0:T(8,128)S(1)}, bf16[4,1024,512]{2,1,0:T(8,128)(2,1)S(1)}) custom-call(s32[128,512]{1,0:T(8,128)S(1)} %collective-permute-done.5.refs_0_, bf16[4,1024,512]{2,1,0:T(8,128)(2,1)S(1)} %get-tuple-element.25.refs_1_, s32[4,8,512]{2,1,0:T(8,128)S(1)} %get-tuple-element.22.first_ref.refs_2_, ...), custom_call_target="tpu_custom_call" | custom-call | flops 2147483648 | bytes 8388608 | tf_op jit(solution)/shard_map/second_hint/pallas_call | solution.py:382
  43.4 1.4 %last_hint.2.refs_0_ = s32[4,128,512]{2,1,0:T(8,128)S(1)} custom-call(s32[64,512]{1,0:T(8,128)S(1)} %collective-permute-done.6.refs_0_, s32[64,512]{1,0:T(8,128)S(1)} %collective-permute-done.8.refs_1_, bf16[4,1024,512]{2,1,0:T(8,128)(2,1)S(1)} %get-tuple-element.27.refs_2_, s32[4,128,1024]{2,1,0:T(8,128)S(1)} %get-tuple-element.28.refs_3_), custom_call_target="tpu_custom_call" | custom-call | flops 1073741824 | bytes 4194304 | tf_op jit(solution)/shard_map/last_hint/pallas_call | solution.py:432
  44.8 0.1 collective-permute-start.9
  44.9 1.4 %last_hint.3.refs_1_ = s32[4,128,512]{2,1,0:T(8,128)S(1)} custom-call(s32[64,512]{1,0:T(8,128)S(1)} %collective-permute-done.6.refs_0_, s32[64,512]{1,0:T(8,128)S(1)} %collective-permute-done.8.refs_1_, bf16[4,1024,512]{2,1,0:T(8,128)(2,1)S(1)} %get-tuple-element.27.refs_2_, s32[4,128,1024]{2,1,0:T(8,128)S(1)} %get-tuple-element.28.refs_3_), custom_call_target="tpu_custom_call" | custom-call | flops 1073741824 | bytes 4194304 | tf_op jit(solution)/shard_map/last_hint/pallas_call | solution.py:432
  46.3 0.6 %collective-permute-start.10 = (s32[4,128,512]{2,1,0:T(8,128)S(1)}, s32[4,128,512]{2,1,0:T(8,128)S(1)}, u32[]{:S(2)}, u32[]{:S(2)}) collective-permute-start(s32[4,128,512]{2,1,0:T(8,128)S(1)} %last_hint.3.refs_1_), channel_id=1, source_target_pairs={{0,4},{4,0},{8,12},{12,8},{16,20},{20,16},{24,28},{28,24},{1,5},{5... | collective-permute-start | bytes 3145736 | tf_op jit(solution)/shard_map/ppermute | solution.py:486
  46.8 2.2 %write_parts.2.refs_2_ = f32[4,2,256,1024]{3,2,1,0:T(8,128)} custom-call(s32[4,128,512]{2,1,0:T(8,128)S(1)} %last_hint.2.refs_0_, s32[4,128,512]{2,1,0:T(8,128)S(1)} %last_hint.3.refs_1_), custom_call_target="tpu_custom_call" | custom-call | tf_op jit(solution)/shard_map/write_parts/pallas_call | solution.py:473
  49.0 0.1 collective-permute-done.10.refs_1_
  49.1 2.2 %write_parts.3 = f32[4,2,256,1024]{3,2,1,0:T(8,128)} custom-call(s32[4,128,512]{2,1,0:T(8,128)S(1)} %collective-permute-done.9.refs_0_, s32[4,128,512]{2,1,0:T(8,128)S(1)} %collective-permute-done.10.refs_1_, f32[4,2,256,1024]{3,2,1,0:T(8,128)} %write_parts.2.refs_2_), custom_call_target="tpu_custom_call", output_to_operand_aliasing={{}: (2, {})} | custom-call | tf_op jit(solution)/shard_map/write_parts/pallas_call | solution.py:473
  (10 shorter events, 0.0 us)
Async XLA Ops:
  0.0 3.0 %collective-permute-start = (bf16[64,8192]{1,0:T(8,128)(2,1)}, bf16[64,8192]{1,0:T(8,128)(2,1)S(1)}, u32[]{:S(2)}, u32[]{:S(2)}) collective-permute-start(bf16[64,8192]{1,0:T(8,128)(2,1)} %own_ref.3), channel_id=1, source_target_pairs={{0,4},{4,0},{8,12},{12,8},{16,20},{20,16},{24,28},{28,24},{1,5},{5... | collective-permute-start | bytes 3145736 | tf_op jit(solution)/shard_map/ppermute | solution.py:486
  0.5 24.3 %collective-permute-start.4 = (s32[1,256]{1,0:T(1,128)}, s32[1,256]{1,0:T(1,128)S(1)}, u32[]{:S(2)}, u32[]{:S(2)}) collective-permute-start(s32[1,256]{1,0:T(1,128)} %refs_4_.1), channel_id=1, source_target_pairs={{0,4},{4,0},{8,12},{12,8},{16,20},{20,16},{24,28},{28,24},{1,5},{5... | collective-permute-start | bytes 3080 | tf_op jit(solution)/shard_map/ppermute | solution.py:486
  0.5 0.7 %copy-start.2 = (s32[2]{0:T(128)S(1)}, s32[2]{0:T(128)}, u32[]{:S(2)}) copy-start(s32[2]{0:T(128)} %seeds_ref.1) | copy-start | bytes 28
  3.0 1.2 %copy-start.1 = (bf16[64,8192]{1,0:T(8,128)(2,1)S(1)}, bf16[64,8192]{1,0:T(8,128)(2,1)}, u32[]{:S(2)}) copy-start(bf16[64,8192]{1,0:T(8,128)(2,1)} %own_ref.3) | copy-start | bytes 3145732
  15.1 9.7 %collective-permute-start.1 = (s32[128,128]{1,0:T(8,128)S(1)}, s32[128,128]{1,0:T(8,128)S(1)}, u32[]{:S(2)}, u32[]{:S(2)}) collective-permute-start(s32[128,128]{1,0:T(8,128)S(1)} %get-tuple-element.19), channel_id=1, source_target_pairs={{0,1},{1,0},{2,3},{3,2},{4,5},{5,4},{6,7},{7,6},{8,9},{9,8},{10,11... | collective-permute-start | bytes 196616 | tf_op jit(solution)/shard_map/ppermute | solution.py:486
  18.1 7.5 %collective-permute-start.2 = (s32[128,128]{1,0:T(8,128)S(1)}, s32[128,128]{1,0:T(8,128)S(1)}, u32[]{:S(2)}, u32[]{:S(2)}) collective-permute-start(s32[128,128]{1,0:T(8,128)S(1)} %get-tuple-element.20), channel_id=1, source_target_pairs={{0,2},{1,3},{2,0},{3,1},{4,6},{5,7},{6,4},{7,5},{8,10},{9,11},{10,... | collective-permute-start | bytes 196616 | tf_op jit(solution)/shard_map/ppermute | solution.py:486
  20.7 6.2 %copy-start = (s32[1,256]{1,0:T(1,128)S(1)}, s32[1,256]{1,0:T(1,128)}, u32[]{:S(2)}) copy-start(s32[1,256]{1,0:T(1,128)} %refs_4_.1) | copy-start | bytes 3076
  20.7 6.2 %collective-permute-start.3 = (s32[128,128]{1,0:T(8,128)S(1)}, s32[128,128]{1,0:T(8,128)S(1)}, u32[]{:S(2)}, u32[]{:S(2)}) collective-permute-start(s32[128,128]{1,0:T(8,128)S(1)} %get-tuple-element.21), channel_id=1, source_target_pairs={{0,3},{1,2},{2,1},{3,0},{4,7},{5,6},{6,5},{7,4},{8,11},{9,10},{10,... | collective-permute-start | bytes 196616 | tf_op jit(solution)/shard_map/ppermute | solution.py:486
  27.4 8.4 %collective-permute-start.7 = (s32[128,512]{1,0:T(8,128)S(1)}, s32[128,512]{1,0:T(8,128)S(1)}, u32[]{:S(2)}, u32[]{:S(2)}) collective-permute-start(s32[128,512]{1,0:T(8,128)S(1)} %sort_rows.1.refs_0_), channel_id=1, source_target_pairs={{0,8},{4,12},{8,0},{12,4},{16,24},{20,28},{24,16},{28,20},{1,9},{5... | collective-permute-start | bytes 786440 | tf_op jit(solution)/shard_map/ppermute | solution.py:486
  28.9 7.4 %collective-permute-start.5 = (s32[128,512]{1,0:T(8,128)S(1)}, s32[128,512]{1,0:T(8,128)S(1)}, u32[]{:S(2)}, u32[]{:S(2)}) collective-permute-start(s32[128,512]{1,0:T(8,128)S(1)} %sort_rows.1.refs_0_), channel_id=1, source_target_pairs={{0,16},{4,20},{8,24},{12,28},{16,0},{20,4},{24,8},{28,12},{1,17},{... | collective-permute-start | bytes 786440 | tf_op jit(solution)/shard_map/ppermute | solution.py:486
  35.8 7.6 %collective-permute-start.8 = (s32[64,512]{1,0:T(8,128)S(1)}, s32[64,512]{1,0:T(8,128)S(1)}, u32[]{:S(2)}, u32[]{:S(2)}) collective-permute-start(s32[64,512]{1,0:T(8,128)S(1)} %slice.9), channel_id=1, source_target_pairs={{0,16},{4,20},{8,24},{12,28},{16,0},{20,4},{24,8},{28,12},{1,17},{... | collective-permute-start | bytes 393224 | tf_op jit(solution)/shard_map/ppermute | solution.py:486
  36.4 7.0 %collective-permute-start.6 = (s32[64,512]{1,0:T(8,128)S(1)}, s32[64,512]{1,0:T(8,128)S(1)}, u32[]{:S(2)}, u32[]{:S(2)}) collective-permute-start(s32[64,512]{1,0:T(8,128)S(1)} %slice.8), channel_id=1, source_target_pairs={{0,8},{4,12},{8,0},{12,4},{16,24},{20,28},{24,16},{28,20},{1,9},{5... | collective-permute-start | bytes 393224 | tf_op jit(solution)/shard_map/ppermute | solution.py:486
  44.8 4.2 %collective-permute-start.9 = (s32[4,128,512]{2,1,0:T(8,128)S(1)}, s32[4,128,512]{2,1,0:T(8,128)S(1)}, u32[]{:S(2)}, u32[]{:S(2)}) collective-permute-start(s32[4,128,512]{2,1,0:T(8,128)S(1)} %last_hint.2.refs_0_), channel_id=1, source_target_pairs={{0,4},{4,0},{8,12},{12,8},{16,20},{20,16},{24,28},{28,24},{1,5},{5... | collective-permute-start | bytes 3145736 | tf_op jit(solution)/shard_map/ppermute | solution.py:486
  46.3 2.8 %collective-permute-start.10 = (s32[4,128,512]{2,1,0:T(8,128)S(1)}, s32[4,128,512]{2,1,0:T(8,128)S(1)}, u32[]{:S(2)}, u32[]{:S(2)}) collective-permute-start(s32[4,128,512]{2,1,0:T(8,128)S(1)} %last_hint.3.refs_1_), channel_id=1, source_target_pairs={{0,4},{4,0},{8,12},{12,8},{16,20},{20,16},{24,28},{28,24},{1,5},{5... | collective-permute-start | bytes 3145736 | tf_op jit(solution)/shard_map/ppermute | solution.py:486

commit v6 on v5

--- a/solution.py
+++ b/solution.py
@@ -413,9 +413,13 @@
 
 
 def last_kernel(block, first, count, *refs):
-    hint_refs, (matrix_ref, total_ref, sum_ref, digits, small_digits) = refs[:count], refs[count:]
+    hint_refs, refs = refs[:count], refs[count:]
+    if count:
+        matrix_ref, total_ref, sum_ref, digits, small_digits = refs
+        spread(hint_refs, digits, small_digits)
+    else:
+        digits, small_digits, matrix_ref, total_ref, sum_ref = refs
     _, half, columns = sum_ref.shape
-    spread(hint_refs, digits, small_digits)
     for i in range(columns // block):
         inner = slice(i * block, (i + 1) * block)
         at = slice(first + i * block, first + (i + 1) * block)
@@ -425,20 +429,22 @@
             sum_ref[place, :, inner] = total_ref[place, :, at] + term
 
 
-def last_hint(hints, matrix, total, first, count):
-    half = sum(hint.shape[0] for hint in hints)
+def last_hint(hints, matrix, total, first, count, digits=()):
+    half = total.shape[1]
     depth = matrix.shape[2]
     whole = pl.BlockSpec(memory_space=pltpu.VMEM)
-    return pl.pallas_call(
-        functools.partial(last_kernel, min(256, count), first, len(hints)),
-        in_specs=[whole] * (len(hints) + 2),
-        out_specs=whole,
-        out_shape=jax.ShapeDtypeStruct((4, half, count), jnp.int32),
-        scratch_shapes=[pltpu.VMEM((4 * half, depth), jnp.bfloat16)] * 2,
+    sources = list(digits) or list(hints)
+    extra = 0 if digits else 2
+    return pl.pallas_call(
+        functools.partial(last_kernel, min(256, count), first, 0 if digits else len(hints)),
+        in_specs=[whole] * (len(sources) + 2),
+        out_specs=[whole] * (1 + extra),
+        out_shape=[jax.ShapeDtypeStruct((4, half, count), jnp.int32)]
+        + [jax.ShapeDtypeStruct((4 * half, depth), jnp.bfloat16)] * extra,
         compiler_params=pltpu.CompilerParams(vmem_limit_bytes=VMEM_LIMIT),
         cost_estimate=product_cost(4 * half, depth, count),
         name="last_hint",
-    )(*hints, matrix, total)
+    )(*sources, matrix, total)
 
 
 def halves_scratch(shape):
@@ -522,7 +528,9 @@
     for t in range(chips - 1):
         total, matrix = second_hint(sources[t], matrix, by_row, t + 1, total)
     cut = N // 2
-    sums = [last_hint(sources[-1], matrix, total, i * cut, cut) for i in range(2)]
+    early, *digits = last_hint(sources[-1], matrix, total, 0, cut)
+    (late,) = last_hint(sources[-1], matrix, total, cut, cut, digits)
+    sums = [early, late]
     others = [shift_by(value, "row", 1) for value in sums]
     out = write_parts(sums, [(False, 0), (False, cut)], N)
     return write_parts(others, [(True, 0), (True, cut)], N, out)

time: 51.6 us -> 52.9 us (1.025)
  waiting for transfers between devices: 2.41 us -> 3.77 us
    ppermute x11, waiting for transfers between devices: 2.41 us -> 3.77 us  [shift_by(): lax.ppermute(value, axis, [(i, i ^ offset) for i in range(lax.axis_size(a...]
  transfers between devices with their start and end apart: 11 -> 11, of which waited for: 4 -> 4; matrix products, arithmetic and copies ran while one was open for 0% -> 0% of each run, Pallas kernels for 61% -> 57%
where the time goes in v6:
time: 52.9 us; the launch traced here: 52.7 us
  Pallas kernels  35.5 us (67%)
  starting transfers between devices  11.2 us (21%)
  waiting for transfers between devices  3.77 us (7%)
  local copies, waits for them, and re-layouts  1.9 us (4%)
    pallas_call x2, Pallas kernels, first_hint(): pl.pallas_call(functools.partial(first_kernel, s, width, lane), out_shape...  14.9 us
    ppermute x11, starting transfers between devices, shift_by(): lax.ppermute(value, axis, [(i, i ^ offset) for i in range(lax.axis_size(a...  11.2 us
    pallas_call x3, Pallas kernels, second_hint(): pl.pallas_call(functools.partial(second_kernel, min(256, columns), len(hi...  9.03 us
    pallas_call x2, Pallas kernels, write_parts(): pl.pallas_call(functools.partial(write_kernel, parts), in_specs=[pl.Block...  4.32 us
    ppermute x11, waiting for transfers between devices, shift_by(): lax.ppermute(value, axis, [(i, i ^ offset) for i in range(lax.axis_size(a...  3.77 us
    pallas_call x2, Pallas kernels, last_hint(): pl.pallas_call(functools.partial(last_kernel, min(256, count), first, 0 i...  2.75 us
    pallas_call x1, Pallas kernels, second_matrix(): pl.pallas_call(functools.partial(matrix_kernel, block), grid=(1,), out_sh...  2.34 us
    unnamed x6, local copies, waits for them, and re-layouts  1.88 us
  transfers between devices with their start and end apart: 11, of which 4 were waited for; matrix products, arithmetic and copies ran while one was open for 0% of the time, Pallas kernels for 57%

profile of v6, /device:TPU:0, one launch (start us, length us, event | category | flops | bytes accessed | tf_op | source)
XLA Modules:
  0.0 52.7 jit_solution(2474779276036376613)
XLA Ops:
  0.0 0.5 collective-permute-start
  0.5 0.0 collective-permute-start.4
  0.5 0.7 %copy-done.2 = s32[2]{0:T(128)S(1)} copy-done((s32[2]{0:T(128)S(1)}, s32[2]{0:T(128)}, u32[]{:S(2)}) %copy-start.2) | copy-done | bytes 32
  1.2 1.6 %tables.1 = (s32[8,8192]{1,0:T(8,128)S(1)}, s32[4,3,16,128]{3,2,1,0:T(8,128)S(1)}, s32[4,8,512]{2,1,0:T(8,128)S(1)}) custom-call(s32[2]{0:T(128)S(1)} %copy-done.2), custom_call_target="tpu_custom_call" | custom-call | tf_op jit(solution)/shard_map/tables/pallas_call | solution.py:92
  2.8 0.2 collective-permute-done.peer_ref
  3.0 1.2 %copy-done.1 = bf16[64,8192]{1,0:T(8,128)(2,1)S(1)} copy-done((bf16[64,8192]{1,0:T(8,128)(2,1)S(1)}, bf16[64,8192]{1,0:T(8,128)(2,1)}, u32[]{:S(2)}) %copy-start.1) | copy-done | bytes 1048600
  4.2 10.9 %first_hint.3 = (s32[128,128]{1,0:T(8,128)S(1)}, s32[128,128]{1,0:T(8,128)S(1)}, s32[128,128]{1,0:T(8,128)S(1)}) custom-call(bf16[64,8192]{1,0:T(8,128)(2,1)S(1)} %copy-done.1, bf16[64,8192]{1,0:T(8,128)(2,1)S(1)} %collective-permute-done.peer_ref, s32[8,8192]{1,0:T(8,128)S(1)} %get-tuple-element.20.first_ref, s32[4,3,16,128]{3,2,1,0:T(8,128)S(1)} %get-tuple-element.21.second_ref), custom_call_target="tpu_custom_call" | custom-call | flops 12884901888 | bytes 2097152 | tf_op jit(solution)/shard_map/first_hint/pallas_call | solution.py:182
  15.1 3.0 %collective-permute-start.1 = (s32[128,128]{1,0:T(8,128)S(1)}, s32[128,128]{1,0:T(8,128)S(1)}, u32[]{:S(2)}, u32[]{:S(2)}) collective-permute-start(s32[128,128]{1,0:T(8,128)S(1)} %get-tuple-element.22), channel_id=1, source_target_pairs={{0,1},{1,0},{2,3},{3,2},{4,5},{5,4},{6,7},{7,6},{8,9},{9,8},{10,11... | collective-permute-start | bytes 196616 | tf_op jit(solution)/shard_map/ppermute | solution.py:492
  18.1 2.6 %collective-permute-start.2 = (s32[128,128]{1,0:T(8,128)S(1)}, s32[128,128]{1,0:T(8,128)S(1)}, u32[]{:S(2)}, u32[]{:S(2)}) collective-permute-start(s32[128,128]{1,0:T(8,128)S(1)} %get-tuple-element.23), channel_id=1, source_target_pairs={{0,2},{1,3},{2,0},{3,1},{4,6},{5,7},{6,4},{7,5},{8,10},{9,11},{10,... | collective-permute-start | bytes 196616 | tf_op jit(solution)/shard_map/ppermute | solution.py:492
  20.7 4.0 %first_hint.2.refs_0_ = s32[128,128]{1,0:T(8,128)S(1)} custom-call(bf16[64,8192]{1,0:T(8,128)(2,1)S(1)} %copy-done.1, bf16[64,8192]{1,0:T(8,128)(2,1)S(1)} %collective-permute-done.peer_ref, s32[8,8192]{1,0:T(8,128)S(1)} %get-tuple-element.20.first_ref, s32[4,3,16,128]{3,2,1,0:T(8,128)S(1)} %get-tuple-element.21.second_ref), custom_call_target="tpu_custom_call" | custom-call | flops 4294967296 | bytes 2097152 | tf_op jit(solution)/shard_map/first_hint/pallas_call | solution.py:182
  24.7 0.0 collective-permute-done.4.refs_5_
  24.8 0.0 collective-permute-done.1.refs_1_
  24.8 0.9 %collective-permute-done.2.refs_2_ = s32[128,128]{1,0:T(8,128)S(1)} collective-permute-done((s32[128,128]{1,0:T(8,128)S(1)}, s32[128,128]{1,0:T(8,128)S(1)}, u32[]{:S(2)}, u32[]{:S(2)}) %collective-permute-start.2) | collective-permute-done | bytes 65568 | tf_op jit(solution)/shard_map/ppermute | solution.py:492
  25.6 1.2 %collective-permute-done.3.refs_3_ = s32[128,128]{1,0:T(8,128)S(1)} collective-permute-done((s32[128,128]{1,0:T(8,128)S(1)}, s32[128,128]{1,0:T(8,128)S(1)}, u32[]{:S(2)}, u32[]{:S(2)}) %collective-permute-start.3) | collective-permute-done | bytes 65568 | tf_op jit(solution)/shard_map/ppermute | solution.py:492
  26.9 0.5 sort_rows.1.refs_0_
  27.4 1.6 %collective-permute-start.7 = (s32[128,512]{1,0:T(8,128)S(1)}, s32[128,512]{1,0:T(8,128)S(1)}, u32[]{:S(2)}, u32[]{:S(2)}) collective-permute-start(s32[128,512]{1,0:T(8,128)S(1)} %sort_rows.1.refs_0_), channel_id=1, source_target_pairs={{0,8},{4,12},{8,0},{12,4},{16,24},{20,28},{24,16},{28,20},{1,9},{5... | collective-permute-start | bytes 786440 | tf_op jit(solution)/shard_map/ppermute | solution.py:492
  28.9 1.5 %collective-permute-start.5 = (s32[128,512]{1,0:T(8,128)S(1)}, s32[128,512]{1,0:T(8,128)S(1)}, u32[]{:S(2)}, u32[]{:S(2)}) collective-permute-start(s32[128,512]{1,0:T(8,128)S(1)} %sort_rows.1.refs_0_), channel_id=1, source_target_pairs={{0,16},{4,20},{8,24},{12,28},{16,0},{20,4},{24,8},{28,12},{1,17},{... | collective-permute-start | bytes 786440 | tf_op jit(solution)/shard_map/ppermute | solution.py:492
  30.5 2.3 %second_matrix.1.refs_1_ = bf16[4,1024,512]{2,1,0:T(8,128)(2,1)S(1)} custom-call(s32[4,8,512]{2,1,0:T(8,128)S(1)} %get-tuple-element.25.first_ref.refs_2_), custom_call_target="tpu_custom_call" | custom-call | flops 1048576000 | bytes 4194304 | tf_op jit(solution)/shard_map/second_matrix/pallas_call | solution.py:289
  32.8 2.9 %second_hint.3 = (s32[4,128,1024]{2,1,0:T(8,128)S(1)}, bf16[4,1024,512]{2,1,0:T(8,128)(2,1)S(1)}) custom-call(s32[128,512]{1,0:T(8,128)S(1)} %sort_rows.1.refs_0_, bf16[4,1024,512]{2,1,0:T(8,128)(2,1)S(1)} %second_matrix.1.refs_1_, s32[4,8,512]{2,1,0:T(8,128)S(1)} %get-tuple-element.25.first_ref.refs_2_), custom_call_target="tpu_custom_call" | custom-call | flops 2147483648 | bytes 8388608 | tf_op jit(solution)/shard_map/second_hint/pallas_call | solution.py:382
  35.8 0.0 collective-permute-done.7.refs_0_
  35.8 0.6 %collective-permute-start.8 = (s32[64,512]{1,0:T(8,128)S(1)}, s32[64,512]{1,0:T(8,128)S(1)}, u32[]{:S(2)}, u32[]{:S(2)}) collective-permute-start(s32[64,512]{1,0:T(8,128)S(1)} %slice.9), channel_id=1, source_target_pairs={{0,16},{4,20},{8,24},{12,28},{16,0},{20,4},{24,8},{28,12},{1,17},{... | collective-permute-start | bytes 393224 | tf_op jit(solution)/shard_map/ppermute | solution.py:492
  36.4 0.0 collective-permute-done.5.refs_0_
  36.4 0.9 %collective-permute-start.6 = (s32[64,512]{1,0:T(8,128)S(1)}, s32[64,512]{1,0:T(8,128)S(1)}, u32[]{:S(2)}, u32[]{:S(2)}) collective-permute-start(s32[64,512]{1,0:T(8,128)S(1)} %slice.8), channel_id=1, source_target_pairs={{0,8},{4,12},{8,0},{12,4},{16,24},{20,28},{24,16},{28,20},{1,9},{5... | collective-permute-start | bytes 393224 | tf_op jit(solution)/shard_map/ppermute | solution.py:492
  37.3 3.0 %second_hint.4 = (s32[4,128,1024]{2,1,0:T(8,128)S(1)}, bf16[4,1024,512]{2,1,0:T(8,128)(2,1)S(1)}) custom-call(s32[128,512]{1,0:T(8,128)S(1)} %collective-permute-done.7.refs_0_, bf16[4,1024,512]{2,1,0:T(8,128)(2,1)S(1)} %get-tuple-element.26.refs_1_, s32[4,8,512]{2,1,0:T(8,128)S(1)} %get-tuple-element.25.first_ref.refs_2_, ...), custom_call_target="tpu_custom_call" | custom-call | flops 2147483648 | bytes 8388608 | tf_op jit(solution)/shard_map/second_hint/pallas_call | solution.py:382
  40.3 3.0 %second_hint.5 = (s32[4,128,1024]{2,1,0:T(8,128)S(1)}, bf16[4,1024,512]{2,1,0:T(8,128)(2,1)S(1)}) custom-call(s32[128,512]{1,0:T(8,128)S(1)} %collective-permute-done.5.refs_0_, bf16[4,1024,512]{2,1,0:T(8,128)(2,1)S(1)} %get-tuple-element.28.refs_1_, s32[4,8,512]{2,1,0:T(8,128)S(1)} %get-tuple-element.25.first_ref.refs_2_, ...), custom_call_target="tpu_custom_call" | custom-call | flops 2147483648 | bytes 8388608 | tf_op jit(solution)/shard_map/second_hint/pallas_call | solution.py:382
  43.4 1.4 %last_hint.2 = (s32[4,128,512]{2,1,0:T(8,128)S(1)}, bf16[512,512]{1,0:T(8,128)(2,1)S(1)}, bf16[512,512]{1,0:T(8,128)(2,1)S(1)}) custom-call(s32[64,512]{1,0:T(8,128)S(1)} %collective-permute-done.6.refs_0_, s32[64,512]{1,0:T(8,128)S(1)} %collective-permute-done.8.refs_1_, bf16[4,1024,512]{2,1,0:T(8,128)(2,1)S(1)} %get-tuple-element.30.refs_2_, ...), custom_call_target="tpu_custom_call" | custom-call | flops 1073741824 | bytes 4194304 | tf_op jit(solution)/shard_map/last_hint/pallas_call | solution.py:438
  44.8 1.4 %last_hint.3.refs_1_ = s32[4,128,512]{2,1,0:T(8,128)S(1)} custom-call(bf16[512,512]{1,0:T(8,128)(2,1)S(1)} %get-tuple-element.33.refs_0_, bf16[512,512]{1,0:T(8,128)(2,1)S(1)} %get-tuple-element.34.refs_1_, bf16[4,1024,512]{2,1,0:T(8,128)(2,1)S(1)} %get-tuple-element.30.refs_2_, s32[4,128,1024]{2,1,0:T(8,128)S(1)} %get-tuple-element.31.refs_3_), custom_call_target="tpu_custom_call" | custom-call | flops 1073741824 | bytes 4194304 | tf_op jit(solution)/shard_map/last_hint/pallas_call | solution.py:438
  46.1 0.1 collective-permute-start.10
  46.2 0.5 collective-permute-start.9
  46.7 2.2 %write_parts.2.refs_2_ = f32[4,2,256,1024]{3,2,1,0:T(8,128)} custom-call(s32[4,128,512]{2,1,0:T(8,128)S(1)} %get-tuple-element.32.refs_0_, s32[4,128,512]{2,1,0:T(8,128)S(1)} %last_hint.3.refs_1_), custom_call_target="tpu_custom_call" | custom-call | tf_op jit(solution)/shard_map/write_parts/pallas_call | solution.py:479
  48.9 1.5 %collective-permute-done.9.refs_0_ = s32[4,128,512]{2,1,0:T(8,128)S(1)} collective-permute-done((s32[4,128,512]{2,1,0:T(8,128)S(1)}, s32[4,128,512]{2,1,0:T(8,128)S(1)}, u32[]{:S(2)}, u32[]{:S(2)}) %collective-permute-start.9) | collective-permute-done | bytes 1048608 | tf_op jit(solution)/shard_map/ppermute | solution.py:492
  50.4 2.2 %write_parts.3 = f32[4,2,256,1024]{3,2,1,0:T(8,128)} custom-call(s32[4,128,512]{2,1,0:T(8,128)S(1)} %collective-permute-done.9.refs_0_, s32[4,128,512]{2,1,0:T(8,128)S(1)} %collective-permute-done.10.refs_1_, f32[4,2,256,1024]{3,2,1,0:T(8,128)} %write_parts.2.refs_2_), custom_call_target="tpu_custom_call", output_to_operand_aliasing={{}: (2, {})} | custom-call | tf_op jit(solution)/shard_map/write_parts/pallas_call | solution.py:479
  (10 shorter events, 0.0 us)
Async XLA Ops:
  0.0 3.0 %collective-permute-start = (bf16[64,8192]{1,0:T(8,128)(2,1)}, bf16[64,8192]{1,0:T(8,128)(2,1)S(1)}, u32[]{:S(2)}, u32[]{:S(2)}) collective-permute-start(bf16[64,8192]{1,0:T(8,128)(2,1)} %own_ref.3), channel_id=1, source_target_pairs={{0,4},{4,0},{8,12},{12,8},{16,20},{20,16},{24,28},{28,24},{1,5},{5... | collective-permute-start | bytes 3145736 | tf_op jit(solution)/shard_map/ppermute | solution.py:492
  0.5 24.3 %collective-permute-start.4 = (s32[1,256]{1,0:T(1,128)}, s32[1,256]{1,0:T(1,128)S(1)}, u32[]{:S(2)}, u32[]{:S(2)}) collective-permute-start(s32[1,256]{1,0:T(1,128)} %refs_4_.1), channel_id=1, source_target_pairs={{0,4},{4,0},{8,12},{12,8},{16,20},{20,16},{24,28},{28,24},{1,5},{5... | collective-permute-start | bytes 3080 | tf_op jit(solution)/shard_map/ppermute | solution.py:492
  0.5 0.7 %copy-start.2 = (s32[2]{0:T(128)S(1)}, s32[2]{0:T(128)}, u32[]{:S(2)}) copy-start(s32[2]{0:T(128)} %seeds_ref.1) | copy-start | bytes 28
  3.0 1.2 %copy-start.1 = (bf16[64,8192]{1,0:T(8,128)(2,1)S(1)}, bf16[64,8192]{1,0:T(8,128)(2,1)}, u32[]{:S(2)}) copy-start(bf16[64,8192]{1,0:T(8,128)(2,1)} %own_ref.3) | copy-start | bytes 3145732
  15.1 9.7 %collective-permute-start.1 = (s32[128,128]{1,0:T(8,128)S(1)}, s32[128,128]{1,0:T(8,128)S(1)}, u32[]{:S(2)}, u32[]{:S(2)}) collective-permute-start(s32[128,128]{1,0:T(8,128)S(1)} %get-tuple-element.22), channel_id=1, source_target_pairs={{0,1},{1,0},{2,3},{3,2},{4,5},{5,4},{6,7},{7,6},{8,9},{9,8},{10,11... | collective-permute-start | bytes 196616 | tf_op jit(solution)/shard_map/ppermute | solution.py:492
  18.1 7.5 %collective-permute-start.2 = (s32[128,128]{1,0:T(8,128)S(1)}, s32[128,128]{1,0:T(8,128)S(1)}, u32[]{:S(2)}, u32[]{:S(2)}) collective-permute-start(s32[128,128]{1,0:T(8,128)S(1)} %get-tuple-element.23), channel_id=1, source_target_pairs={{0,2},{1,3},{2,0},{3,1},{4,6},{5,7},{6,4},{7,5},{8,10},{9,11},{10,... | collective-permute-start | bytes 196616 | tf_op jit(solution)/shard_map/ppermute | solution.py:492
  20.7 6.2 %copy-start = (s32[1,256]{1,0:T(1,128)S(1)}, s32[1,256]{1,0:T(1,128)}, u32[]{:S(2)}) copy-start(s32[1,256]{1,0:T(1,128)} %refs_4_.1) | copy-start | bytes 3076
  20.7 6.2 %collective-permute-start.3 = (s32[128,128]{1,0:T(8,128)S(1)}, s32[128,128]{1,0:T(8,128)S(1)}, u32[]{:S(2)}, u32[]{:S(2)}) collective-permute-start(s32[128,128]{1,0:T(8,128)S(1)} %get-tuple-element.24), channel_id=1, source_target_pairs={{0,3},{1,2},{2,1},{3,0},{4,7},{5,6},{6,5},{7,4},{8,11},{9,10},{10,... | collective-permute-start | bytes 196616 | tf_op jit(solution)/shard_map/ppermute | solution.py:492
  27.4 8.4 %collective-permute-start.7 = (s32[128,512]{1,0:T(8,128)S(1)}, s32[128,512]{1,0:T(8,128)S(1)}, u32[]{:S(2)}, u32[]{:S(2)}) collective-permute-start(s32[128,512]{1,0:T(8,128)S(1)} %sort_rows.1.refs_0_), channel_id=1, source_target_pairs={{0,8},{4,12},{8,0},{12,4},{16,24},{20,28},{24,16},{28,20},{1,9},{5... | collective-permute-start | bytes 786440 | tf_op jit(solution)/shard_map/ppermute | solution.py:492
  28.9 7.4 %collective-permute-start.5 = (s32[128,512]{1,0:T(8,128)S(1)}, s32[128,512]{1,0:T(8,128)S(1)}, u32[]{:S(2)}, u32[]{:S(2)}) collective-permute-start(s32[128,512]{1,0:T(8,128)S(1)} %sort_rows.1.refs_0_), channel_id=1, source_target_pairs={{0,16},{4,20},{8,24},{12,28},{16,0},{20,4},{24,8},{28,12},{1,17},{... | collective-permute-start | bytes 786440 | tf_op jit(solution)/shard_map/ppermute | solution.py:492
  35.8 7.6 %collective-permute-start.8 = (s32[64,512]{1,0:T(8,128)S(1)}, s32[64,512]{1,0:T(8,128)S(1)}, u32[]{:S(2)}, u32[]{:S(2)}) collective-permute-start(s32[64,512]{1,0:T(8,128)S(1)} %slice.9), channel_id=1, source_target_pairs={{0,16},{4,20},{8,24},{12,28},{16,0},{20,4},{24,8},{28,12},{1,17},{... | collective-permute-start | bytes 393224 | tf_op jit(solution)/shard_map/ppermute | solution.py:492
  36.4 7.0 %collective-permute-start.6 = (s32[64,512]{1,0:T(8,128)S(1)}, s32[64,512]{1,0:T(8,128)S(1)}, u32[]{:S(2)}, u32[]{:S(2)}) collective-permute-start(s32[64,512]{1,0:T(8,128)S(1)} %slice.8), channel_id=1, source_target_pairs={{0,8},{4,12},{8,0},{12,4},{16,24},{20,28},{24,16},{28,20},{1,9},{5... | collective-permute-start | bytes 393224 | tf_op jit(solution)/shard_map/ppermute | solution.py:492
  46.1 2.7 %collective-permute-start.10 = (s32[4,128,512]{2,1,0:T(8,128)S(1)}, s32[4,128,512]{2,1,0:T(8,128)S(1)}, u32[]{:S(2)}, u32[]{:S(2)}) collective-permute-start(s32[4,128,512]{2,1,0:T(8,128)S(1)} %last_hint.3.refs_1_), channel_id=1, source_target_pairs={{0,4},{4,0},{8,12},{12,8},{16,20},{20,16},{24,28},{28,24},{1,5},{5... | collective-permute-start | bytes 3145736 | tf_op jit(solution)/shard_map/ppermute | solution.py:492
  46.2 4.1 %collective-permute-start.9 = (s32[4,128,512]{2,1,0:T(8,128)S(1)}, s32[4,128,512]{2,1,0:T(8,128)S(1)}, u32[]{:S(2)}, u32[]{:S(2)}) collective-permute-start(s32[4,128,512]{2,1,0:T(8,128)S(1)} %get-tuple-element.32.refs_0_), channel_id=1, source_target_pairs={{0,4},{4,0},{8,12},{12,8},{16,20},{20,16},{24,28},{28,24},{1,5},{5... | collective-permute-start | bytes 3145736 | tf_op jit(solution)/shard_map/ppermute | solution.py:492
